TPU v7x, 512 devices: a whole 4x8x8 slice. The times are simulated.
512 devices in a mesh: seq: 64 (over z_lo, x, y), tp: 8 (over z_hi, core).
Axes of the slice: x: 4, y: 8, z: 8 (z_hi: 4, z_lo: 2; z = z_hi * 2 + z_lo), core: 2. Of those that a mesh axis runs over, the one named last changes fastest.
Arguments:
- patches: bfloat16 [1664, 65536], P('tp', 'seq'), may hold values from -400 to 400
- ln_gain: bfloat16 [1664], P('tp'), may hold values from 0.099609375 to 1.8984375
- ln_bias: bfloat16 [1664], P('tp'), may hold values from -3 to 3
- merge_weight: bfloat16 [4, 1664, 1664], P(None, 'tp', 'seq'), may hold values from -0.078125 to 0.078125
- merge_bias: bfloat16 [1664], P('tp'), may hold values from -3 to 3
- targets: int32 [16384], P('seq'), may hold values from 0 to 24575, as said below
- text_embed: bfloat16 [1664, 24576], P('tp', 'seq'), may hold values from -6 to 6
Outputs:
- prompt_embeds: bfloat16 [1664, 24576], P('tp', 'seq')
Inputs may be any that keep to these rules, and one draw needn't show every extreme that they name: `targets`: Distinct. The merged rows of one index of seq go to the positions of 32 indices of seq (position p belongs to index p // 384); at most 10 of them to one index, and exactly 10 to some index, from every index.
All inputs are finite; a program needn't handle non-finite values.
Results may differ from a plain program's by a relative error of at most 0.015.
Values may be sent and summed in bfloat16 or wider, within the bound.
No kernel may reach another device: no remote copies, remote signals or barrier semaphores. Data moves between devices by JAX's collectives and lax.ppermute only.
A program may use at most 64 MiB of HBM per device.

v0:
```python
import jax
import jax.numpy as jnp
from jax import lax
from jax.sharding import PartitionSpec as P

D = 1664
GROUP = 4


def shards(patches, ln_gain, ln_bias, merge_weight, merge_bias, targets, text_embed):
    values = patches.astype(jnp.float32)
    feature_total = lax.psum(jnp.sum(values, axis=0), "tp")
    row_mean = feature_total / D
    centered = values - row_mean[None, :]
    square_total = lax.psum(jnp.sum(centered * centered, axis=0), "tp")
    row_var = square_total / D
    scaled = (
        centered * lax.rsqrt(row_var + 1e-06)[None, :] * ln_gain.astype(jnp.float32)[:, None]
        + ln_bias.astype(jnp.float32)[:, None]
    )
    normed = scaled.astype(jnp.bfloat16)
    feat_width = normed.shape[0]
    merged_rows = normed.shape[1] // GROUP
    grouped = normed.reshape(feat_width, merged_rows, GROUP)
    partial_terms = jnp.einsum(
        "fmk,kfc->cm",
        grouped,
        lax.all_gather(merge_weight, "seq", axis=2, tiled=True),
        preferred_element_type=jnp.float32,
    )
    summed = lax.psum_scatter(
        partial_terms.astype(jnp.bfloat16), "tp", scatter_dimension=0, tiled=True
    ).astype(jnp.float32)
    merged = (summed + merge_bias.astype(jnp.float32)[:, None]).astype(jnp.bfloat16)
    seq_count = lax.axis_size("seq")
    prompt_rows = text_embed.shape[1]
    capacity = 5 * merged_rows // (2 * seq_count)
    target_dev = targets // prompt_rows
    local_pos = targets % prompt_rows
    one_hot = (target_dev[:, None] == jnp.arange(seq_count, dtype=jnp.int32)[None, :]).astype(
        jnp.int32
    )
    order_in = jnp.sum((jnp.cumsum(one_hot, axis=0) - 1) * one_hot, axis=1)
    slot_index = target_dev * capacity + order_in
    send_rows = (
        jnp.zeros((feat_width, seq_count * capacity), jnp.bfloat16).at[:, slot_index].set(merged)
    )
    send_pos = (
        jnp.full((seq_count * capacity,), prompt_rows, jnp.int32).at[slot_index].set(local_pos)
    )
    got_rows, got_pos = (
        lax.all_to_all(
            send_rows.reshape(feat_width, seq_count, capacity),
            "seq",
            split_axis=1,
            concat_axis=1,
            tiled=True,
        ),
        lax.all_to_all(
            send_pos.reshape(1, seq_count, capacity), "seq", split_axis=1, concat_axis=1, tiled=True
        ),
    )
    return text_embed.at[:, got_pos.reshape(-1)].set(got_rows.reshape(feat_width, -1), mode="drop")


def solution(mesh):
    in_specs = (
        P("tp", "seq"),
        P("tp"),
        P("tp"),
        P(None, "tp", "seq"),
        P("tp"),
        P("seq"),
        P("tp", "seq"),
    )
    out_specs = P("tp", "seq")
    return jax.shard_map(shards, mesh=mesh, in_specs=in_specs, out_specs=out_specs, check_vma=False)
```

profile of v0, /device:TPU:1, one launch (start us, length us, event | category | flops | bytes accessed | tf_op | source)
XLA Modules:
  0.0 404.6 jit_solution(16491951005488885185)
XLA Ops:
  6.5 0.0 all-gather.2.cloned.1.call-start
  6.5 0.7 all-gather.2.cloned.1.call-update
  7.3 0.0 reduce-scatter.4.cloned.1.call-start
  7.3 0.7 convert_element_type.34
  8.0 0.7 convert_element_type.35
  8.6 1.1 convert_reduce_fusion
  9.7 20.5 %psum.14 = f32[1024]{0:T(1024)S(1)} all-reduce(f32[1024]{0:T(1024)S(1)} %convert_reduce_fusion), channel_id=1, replica_groups=mesh['seq'=64,'tp'=8] {'tp'}, use_global_device_ids=true, to_apply=%region_5.6 | all-reduce | flops 1024 | bytes 8192 | tf_op jit(solution)/shard_map/psum | solution.py:12
  30.2 1.1 fusion.13
  31.3 17.4 %psum.15 = f32[1024]{0:T(1024)S(1)} all-reduce(f32[1024]{0:T(1024)S(1)} %fusion.13), channel_id=1, replica_groups=mesh['seq'=64,'tp'=8] {'tp'}, use_global_device_ids=true, to_apply=%region_7.8 | all-reduce | flops 1024 | bytes 8192 | tf_op jit(solution)/shard_map/psum | solution.py:15
  48.8 1.2 fusion.16
  50.0 0.2 copy.20
  50.2 0.2 reshape.69
  50.4 0.0 copy-start.1
  50.4 0.0 copy-start.2
  50.4 227.1 %all-gather.2.cloned.1.call-done = bf16[4,208,1664]{1,0,2:T(4,128)(2,1)} async-done(((bf16[4,208,26]{1,0,2:T(4,128)(2,1)}), bf16[4,208,1664]{1,0,2:T(4,128)(2,1)}) %all-gather.2.cloned.1.call-update) | async-done | bytes 2768912 | tf_op jit(solution)/shard_map/all_gather | solution.py:28
  277.5 3.1 fusion.8
  280.6 0.0 copy-start
  280.6 1.3 copy.25
  281.9 0.0 reduce-scatter.4.cloned.1.call-update
  281.9 0.0 copy-done.1
  282.0 0.6 reduce-window.6
  282.6 0.2 slice_reduce_fusion
  282.8 0.1 fusion.26
  283.0 1.4 scatter_custom_fusion
  284.4 0.7 reshape.67
  285.1 6.6 %all-to-all-start = ((s32[1,64,10]{2,0,1:T(1,128)}), s32[1,64,10]{2,0,1:T(1,128)S(1)}, u32[]{:S(2)}, u32[]{:S(2)}) async-start(s32[1,64,10]{2,0,1:T(1,128)} %bitcast.2), calls=%async_computation | async-start | bytes 65536 | tf_op jit(solution)/shard_map/all_to_all | solution.py:59
  291.7 0.0 copy-done.2
  291.8 70.7 %reduce-scatter.4.cloned.1.call-done = bf16[208,256]{1,0:T(8,128)(2,1)} async-done(((bf16[1664,256]{1,0:T(8,128)(2,1)}), bf16[208,256]{1,0:T(8,128)(2,1)}) %reduce-scatter.4.cloned.1.call-update) | async-done | bytes 106512
  362.4 1.0 copy.26
  363.4 1.6 scatter_custom_fusion.1
  365.0 0.9 reshape.70
  366.0 0.0 all-to-all-done
  366.0 9.8 %all-to-all-start.1 = ((bf16[208,64,10]{0,2,1:T(8,128)(2,1)}), bf16[208,64,10]{0,2,1:T(8,128)(2,1)S(1)}, u32[]{:S(2)}, u32[]{:S(2)}) async-start(bf16[208,64,10]{0,2,1:T(8,128)(2,1)} %reshape.70), calls=%async_computation.1 | async-start | bytes 1048576 | tf_op jit(solution)/shard_map/all_to_all | solution.py:52
  375.7 0.0 copy-done
  375.7 0.1 copy.23
  375.9 0.5 broadcast.83
  376.4 0.7 reduce.7
  377.1 0.1 reshape.68
  377.3 13.6 %all-to-all-done.1 = bf16[208,64,10]{0,2,1:T(8,128)(2,1)S(1)} async-done(((bf16[208,64,10]{0,2,1:T(8,128)(2,1)}), bf16[208,64,10]{0,2,1:T(8,128)(2,1)S(1)}, u32[]{:S(2)}, u32[]{:S(2)}) %all-to-all-start.1) | async-done | bytes 266272 | tf_op jit(solution)/shard_map/all_to_all | solution.py:52
  390.9 0.2 reshape.89
  391.2 5.8 %scatter_custom_fusion.2 = bf16[208,384]{0,1:T(8,128)(2,1)S(1)} fusion(bf16[208,384]{0,1:T(8,128)(2,1)S(1)} %copy.23, s32[640]{0:T(1024)S(1)} %fusion.28, bf16[208,640]{0,1:T(8,128)(2,1)S(1)} %reshape.89), kind=kCustom, calls=%fused_computation.17 | custom fusion | bytes 487424 | tf_op jit(solution)/shard_map/scatter | solution.py:63
  396.9 0.8 copy.24
  (9 shorter events, 0.1 us)
Async XLA Ops:
  6.5 271.0 %all-gather.2.cloned.1.call-start = ((), (), s32[]{:S(2)}) async-start(), calls=%async_computation.3 | async-start | bytes 3461120 | tf_op jit(solution)/shard_map/all_gather | solution.py:28
  7.3 355.2 %reduce-scatter.4.cloned.1.call-start = ((), (), s32[]{:S(2)}) async-start(), calls=%async_computation.4 | async-start | bytes 958464
  50.4 231.6 %copy-start.1 = (s32[256]{0:T(256)S(1)}, s32[256]{0:T(256)}, u32[]{:S(2)}) copy-start(s32[256]{0:T(256)} %param.12) | copy-start | bytes 3076
  50.4 241.4 %copy-start.2 = (bf16[208]{0:T(256)(128)(2,1)S(1)}, bf16[208]{0:T(256)(128)(2,1)}, u32[]{:S(2)}) copy-start(bf16[208]{0:T(256)(128)(2,1)} %param.11) | copy-start | bytes 1252
  280.6 95.1 %copy-start = (bf16[208,384]{1,0:T(8,128)(2,1)S(1)}, bf16[208,384]{1,0:T(8,128)(2,1)}, u32[]{:S(2)}) copy-start(bf16[208,384]{1,0:T(8,128)(2,1)} %param.13) | copy-start | bytes 479236
  285.1 80.8 %all-to-all-start = ((s32[1,64,10]{2,0,1:T(1,128)}), s32[1,64,10]{2,0,1:T(1,128)S(1)}, u32[]{:S(2)}, u32[]{:S(2)}) async-start(s32[1,64,10]{2,0,1:T(1,128)} %bitcast.2), calls=%async_computation | async-start | bytes 65536 | tf_op jit(solution)/shard_map/all_to_all | solution.py:59
  366.0 25.0 %all-to-all-start.1 = ((bf16[208,64,10]{0,2,1:T(8,128)(2,1)}), bf16[208,64,10]{0,2,1:T(8,128)(2,1)S(1)}, u32[]{:S(2)}, u32[]{:S(2)}) async-start(bf16[208,64,10]{0,2,1:T(8,128)(2,1)} %reshape.70), calls=%async_computation.1 | async-start | bytes 1048576 | tf_op jit(solution)/shard_map/all_to_all | solution.py:52
Sparse Core Ops, SparseCore 0:
  9.4 268.0 all-gather.1
  282.1 80.3 reduce-scatter.3
where the time goes:
time: 408 us; the launch traced here: 405 us
  waiting for transfers between devices  312 us (76%)
  blocking collectives  37.9 us (9%)
  starting transfers between devices  16.4 us (4%)
  between operations  13.6 us (3%)
  local copies, waits for them, and re-layouts  13.5 us (3%)
  other arithmetic  7.87 us (2%)
    all_gather x1, waiting for transfers between devices, shards(): lax.all_gather(merge_weight, 'seq', axis=2, tiled=True)  227 us
    unnamed x3, waiting for transfers between devices  71.4 us
    psum x1, blocking collectives, shards(): feature_total = lax.psum(jnp.sum(values, axis=0), 'tp')  20.5 us
    psum x1, blocking collectives, shards(): square_total = lax.psum(jnp.sum(centered * centered, axis=0), 'tp')  17.4 us
    all_to_all x1, waiting for transfers between devices, shards(): lax.all_to_all(send_rows.reshape(feat_width, seq_count, capacity), 'seq',...  13.6 us
    all_to_all x1, starting transfers between devices, shards(): lax.all_to_all(send_rows.reshape(feat_width, seq_count, capacity), 'seq',...  9.76 us
  transfers between devices with their start and end apart: 4, of which 3 were waited for; matrix products, arithmetic and copies ran while one was open for 3% of the time, Pallas kernels for 0%

commit v1 on v0

v1 whole, which is shorter than its diff:
```python
import functools

import jax
import jax.numpy as jnp
import numpy as np
from jax import lax
from jax.experimental import pallas as pl
from jax.experimental.pallas import tpu as pltpu
from jax.sharding import Mesh
from jax.sharding import PartitionSpec as P

D = 1664
GROUP = 4
N_SEQ = 64
N_TP = 8
FEAT = D // N_TP
TOK = 1024
ROWS = TOK // GROUP
CHUNK = D // N_SEQ
CHUNK_PAD = 32
POS = 384
CAP = 10
SLOTS = 24
HALF = FEAT // 2
LANES = 128
SHARE = ("zl", "xl")
GATHER = ("xh", "y")
SEQ = ("zl", "xh", "xl", "y")
TP = ("zh", "c")
BF16 = jnp.bfloat16
F32 = jnp.float32


def _vmem(n):
    return [pl.BlockSpec(memory_space=pltpu.VMEM)] * n


def _call(body, outs, n_in, n_smem=0):
    return pl.pallas_call(
        body,
        out_shape=outs,
        in_specs=[pl.BlockSpec(memory_space=pltpu.SMEM)] * n_smem + _vmem(n_in),
        out_specs=jax.tree.map(lambda _: pl.BlockSpec(memory_space=pltpu.VMEM), outs),
        compiler_params=pltpu.CompilerParams(vmem_limit_bytes=48 << 20),
    )


def split_body(x_ref, xd_ref, st_ref):
    row = lax.broadcasted_iota(jnp.int32, (512, 512), 0)
    col = lax.broadcasted_iota(jnp.int32, (512, 512), 1)
    pick = jnp.where(row == 4 * (col & 127) + (col >> 7), 1.0, 0.0).astype(BF16)
    for half in range(2):
        lanes = pl.ds(half * 128, 128)
        moved = jnp.dot(x_ref[:, pl.ds(half * 512, 512)], pick, preferred_element_type=F32)
        for k in range(GROUP):
            block = moved[:, k * 128 : (k + 1) * 128]
            xd_ref[pl.ds(k * FEAT, FEAT), lanes] = block.astype(BF16)
            mean = jnp.sum(block, axis=0, keepdims=True) * (1.0 / FEAT)
            off = block - mean
            st_ref[pl.ds(k, 1), lanes] = mean
            st_ref[pl.ds(GROUP + k, 1), lanes] = jnp.sum(off * off, axis=0, keepdims=True)


def project_body(
    ids, own, rx, rk, rs, st, gain, bias, wg, pack, keep_ref, send_ref, normed, weight
):
    c, q = ids[0], ids[1]
    for g in range(2):
        rows = jnp.concatenate([wg[g * 8 + y] for y in range(8)], axis=0)
        weight[g] = jnp.dot(pack[...], rows, preferred_element_type=F32).astype(BF16)
    gain_col = jnp.broadcast_to(gain[...], (FEAT, ROWS))
    bias_col = jnp.broadcast_to(bias[...], (FEAT, ROWS))
    for job in range(4):
        kept, i = job // 2 == 1, job % 2
        e = 2 * (c if kept else 1 - c) + i
        parts = st[q ^ e]
        mean = jnp.sum(parts[:, :GROUP], axis=0) * (1.0 / N_TP)
        off = parts[:, :GROUP] - mean[None]
        var = (jnp.sum(parts[:, GROUP:], axis=0) + FEAT * jnp.sum(off * off, axis=0)) * (1.0 / D)
        scale = lax.rsqrt(var + 1e-06)
        for k in range(GROUP):
            at = pl.ds(k * FEAT, FEAT)
            if i == 1:
                x = (rk if kept else rs)[at, :]
            else:
                x = jnp.where((c == 1) == kept, rx[at, :], own[at, :])
            centered = x.astype(F32) - mean[k : k + 1]
            normed[at, :] = (centered * scale[k : k + 1] * gain_col + bias_col).astype(BF16)
        for g in range(2):
            out = jnp.dot(weight[g], normed[...], preferred_element_type=F32).astype(BF16)
            (keep_ref if kept else send_ref)[2 * i + g] = out


def pair_body(ids, keep, got, *outs):
    zh = ids[0]
    for k in range(4):
        p = zh ^ k
        outs[k][...] = (keep[p].astype(F32) + got[p].astype(F32)).astype(BF16)


def place_body(z0, z1, z2, z3, bias, slot, extra, send_ref):
    total = (z0[...].astype(F32) + z1[...].astype(F32)) + (z2[...].astype(F32) + z3[...].astype(F32))
    merged = total + bias[...]
    fill = jnp.zeros((LANES - HALF - 8, ROWS), F32)
    row = lax.broadcasted_iota(jnp.int32, (N_SEQ * SLOTS, ROWS), 0)
    tag_row = lax.broadcasted_iota(jnp.int32, (8, ROWS), 0)
    out = None
    for h in range(2):
        tag = jnp.where(tag_row == 3, float(h), extra[...])
        data = jnp.concatenate([merged[h * HALF : (h + 1) * HALF], tag, fill], axis=0)
        pick = jnp.where(row == slot[...] + h * CAP, 1.0, 0.0).astype(BF16)
        part = lax.dot_general(
            pick, data.astype(BF16), (((1,), (1,)), ((), ())), preferred_element_type=F32
        )
        out = part if out is None else out + part
    send_ref[...] = out.astype(BF16).reshape(N_SEQ, SLOTS, LANES)


def final_body(got, text, out_ref):
    rows = got[...].reshape(N_SEQ * SLOTS, LANES)
    tags = rows.astype(F32)
    at = tags[:, HALF : HALF + 1] * 16.0 + tags[:, HALF + 1 : HALF + 2] - 16.0
    side = tags[:, HALF + 3 : HALF + 4]
    want = lax.broadcasted_iota(jnp.int32, (N_SEQ * SLOTS, POS), 1).astype(F32)
    halves = []
    for h in range(2):
        mine = jnp.where(side == float(h), at, -1.0)
        pick = jnp.where(want == mine, 1.0, 0.0).astype(BF16)
        halves.append(
            lax.dot_general(rows, pick, (((0,), (0,)), ((), ())), preferred_element_type=F32)
        )
    hit = halves[0][HALF + 2 : HALF + 3] > 0.5
    full = jnp.concatenate([halves[0][:HALF], halves[1][:HALF]], axis=0)
    out_ref[...] = jnp.where(hit, full, text[...].astype(F32)).astype(BF16)


def _pairs(sizes, dest):
    return [
        (int(np.ravel_multi_index(at, sizes)), int(np.ravel_multi_index(dest(*at), sizes)))
        for at in np.ndindex(*sizes)
    ]


def shards(patches, ln_gain, ln_bias, merge_weight, merge_bias, targets, text_embed):
    sds = jax.ShapeDtypeStruct
    zl, xl, zh, c = (lax.axis_index(a) for a in ("zl", "xl", "zh", "c"))

    chunk = jnp.transpose(merge_weight, (2, 0, 1)).reshape(CHUNK, GROUP * FEAT)
    chunk = jnp.pad(chunk, ((0, CHUNK_PAD - CHUNK), (0, 0)))
    columns = lax.all_to_all(
        jnp.broadcast_to(chunk[None], (16, CHUNK_PAD, GROUP * FEAT)), GATHER, 0, 0, tiled=True
    )

    own, stats = _call(split_body, (sds((GROUP * FEAT, ROWS), BF16), sds((8, ROWS), F32)), 1)(patches)
    axes, sizes = ("zl", "xl", "c"), (2, 2, 2)
    rx = lax.ppermute(own, axes, _pairs(sizes, lambda z, x, k: (z ^ 1, x, k)))
    rk = lax.ppermute(own, axes, _pairs(sizes, lambda z, x, k: (z ^ k, x ^ 1, k)))
    rs = lax.ppermute(own, axes, _pairs(sizes, lambda z, x, k: (z ^ k ^ 1, x ^ 1, k)))
    all_stats = lax.all_to_all(
        jnp.broadcast_to(stats[None], (32, 8, ROWS)), SHARE + TP, 0, 0, tiled=True
    ).reshape(4, N_TP, 8, ROWS)

    packed = np.arange(FEAT)
    pack = np.zeros((FEAT, 8 * CHUNK_PAD), np.float32)
    pack[packed, packed // CHUNK * CHUNK_PAD + packed % CHUNK] = 1.0
    ids = jnp.stack([c, 2 * zl + xl]).astype(jnp.int32)
    piece = sds((4, FEAT, ROWS), BF16)
    keep, send = pl.pallas_call(
        project_body,
        out_shape=(piece, piece),
        in_specs=[pl.BlockSpec(memory_space=pltpu.SMEM)] + _vmem(9),
        out_specs=tuple(_vmem(2)),
        scratch_shapes=[
            pltpu.VMEM((GROUP * FEAT, ROWS), BF16),
            pltpu.VMEM((2, FEAT, GROUP * FEAT), BF16),
        ],
        compiler_params=pltpu.CompilerParams(vmem_limit_bytes=48 << 20),
    )(
        ids, own, rx, rk, rs, all_stats,
        ln_gain.astype(F32)[:, None], ln_bias.astype(F32)[:, None], columns, jnp.asarray(pack, BF16),
    )

    got = lax.ppermute(send, "c", [(0, 1), (1, 0)])
    part = sds((FEAT, ROWS), BF16)
    parts = _call(pair_body, (part,) * 4, 2, 1)(zh[None].astype(jnp.int32), keep, got)
    axes, sizes = ("zl", "xl", "zh", "c"), (2, 2, 4, 2)
    moved = [
        lax.ppermute(
            parts[k],
            axes,
            _pairs(sizes, lambda z, x, h, k2, k=k: (z ^ k2, x ^ ((h ^ k) >> 1), 2 * z + ((h ^ k) & 1), x)),
        )
        for k in range(4)
    ]

    target_dev = targets // POS
    local_pos = targets % POS
    before = jnp.arange(ROWS)[:, None] < jnp.arange(ROWS)[None, :]
    rank = jnp.sum(((target_dev[:, None] == target_dev[None, :]) & before).astype(jnp.int32), axis=0)
    slot = (target_dev * SLOTS + rank)[None, :]
    zero = jnp.zeros((ROWS,), F32)
    one = jnp.ones((ROWS,), F32)
    tags = [(local_pos // 16 + 1).astype(F32), (local_pos % 16).astype(F32), one, zero, zero, zero, zero, zero]
    extra = jnp.stack(tags)

    sent = _call(place_body, sds((N_SEQ, SLOTS, LANES), BF16), 7)(
        *moved, merge_bias.astype(F32)[:, None], slot, extra
    )
    rows = lax.all_to_all(sent, SEQ, 0, 0, tiled=True)
    return _call(final_body, sds((FEAT, POS), BF16), 2)(rows, text_embed)


def solution(mesh):
    wide = Mesh(mesh.devices.reshape(2, 2, 2, 8, 4, 2), ("zl", "xh", "xl", "y", "zh", "c"))
    in_specs = (
        P(TP, SEQ),
        P(TP),
        P(TP),
        P(None, TP, SEQ),
        P(TP),
        P(SEQ),
        P(TP, SEQ),
    )
    return jax.shard_map(shards, mesh=wide, in_specs=in_specs, out_specs=P(TP, SEQ), check_vma=False)
```

time: 408 us -> 127 us (0.31)
  waiting for transfers between devices: 312 us -> 37 us
  starting transfers between devices: 16.4 us -> 51.1 us
  between operations: 13.6 us -> 0.27 us
  blocking collectives: 37.9 us -> 26.9 us
  other arithmetic: 7.87 us -> 0.23 us
  local copies, waits for them, and re-layouts: 13.5 us -> 6.01 us
  Pallas kernels: 0 us -> 5.19 us
    all_gather x1 -> x0, waiting for transfers between devices: 227 us -> none  [shards(): lax.all_gather(merge_weight, 'seq', axis=2, tiled=True)]
    unnamed x3 -> x0, waiting for transfers between devices: 71.4 us -> none
    psum x2 -> x0, blocking collectives: 37.9 us -> none  [the longest x1 20.5 us: shards(): feature_total = lax.psum(jnp.sum(values, axis=0), 'tp')]
    ppermute x0 -> x8, starting transfers between devices: none -> 29 us  [the longest x4 18.6 us: shards(): lax.ppermute(parts[k], axes, _pairs(sizes, lambda z, x, h, k2, k=k: (z ^...]
    all_to_all x0 -> x1, blocking collectives: none -> 26.9 us  [shards(): rows = lax.all_to_all(sent, SEQ, 0, 0, tiled=True)]
    ppermute x0 -> x8, waiting for transfers between devices: none -> 24.9 us  [the longest x1 10.8 us: shards(): lax.ppermute(own, axes, _pairs(sizes, lambda z, x, k: (z ^ k, x ^ 1, k)))]
    scatter x3 -> x0, local copies, waits for them, and re-layouts: 7.96 us -> none  [the longest x2 6.55 us: shards(): text_embed.at[:, got_pos.reshape(-1)]]
    all_to_all x2, starting transfers between devices: 16.4 us -> 22.1 us  [the longest x1 13 us: shards(): lax.all_to_all(jnp.broadcast_to(stats[None], (32, 8, ROWS)), SHARE + TP,...]
  transfers between devices with their start and end apart: 4 -> 10, of which waited for: 3 -> 6; matrix products, arithmetic and copies ran while one was open for 3% -> 1% of each run, Pallas kernels for 0% -> 0%
where the time goes in v1:
time: 127 us
  starting transfers between devices  51.1 us (40%)
  waiting for transfers between devices  37 us (29%)
  blocking collectives  26.9 us (21%)
  local copies, waits for them, and re-layouts  6.01 us (5%)
  Pallas kernels  5.19 us (4%)
    all_to_all x1, blocking collectives, shards(): rows = lax.all_to_all(sent, SEQ, 0, 0, tiled=True)  26.9 us
    ppermute x4, starting transfers between devices, shards(): lax.ppermute(parts[k], axes, _pairs(sizes, lambda z, x, h, k2, k=k: (z ^...  18.6 us
    all_to_all x1, starting transfers between devices, shards(): lax.all_to_all(jnp.broadcast_to(stats[None], (32, 8, ROWS)), SHARE + TP,...  13 us
    all_to_all x1, waiting for transfers between devices, shards(): lax.all_to_all(jnp.broadcast_to(stats[None], (32, 8, ROWS)), SHARE + TP,...  12.1 us
    ppermute x1, waiting for transfers between devices, shards(): lax.ppermute(own, axes, _pairs(sizes, lambda z, x, k: (z ^ k, x ^ 1, k)))  10.8 us
    all_to_all x1, starting transfers between devices, shards(): lax.all_to_all(jnp.broadcast_to(chunk[None], (16, CHUNK_PAD, GROUP * FEAT...  9.09 us
    ppermute x1, waiting for transfers between devices, shards(): lax.ppermute(own, axes, _pairs(sizes, lambda z, x, k: (z ^ k ^ 1, x ^ 1,...  8.15 us
    unnamed x16, local copies, waits for them, and re-layouts  3.77 us
  transfers between devices with their start and end apart: 10, of which 6 were waited for; matrix products, arithmetic and copies ran while one was open for 1% of the time, Pallas kernels for 0%

profile of v1, /device:TPU:1, one launch (start us, length us, event | category | flops | bytes accessed | tf_op | source)
XLA Modules:
  0.0 126.7 jit_solution(4539491527632255722)
XLA Ops:
  0.0 0.0 copy-start
  0.0 1.0 copy-done
  1.0 0.5 shard_map.82
  1.5 0.7 broadcast_in_dim.38
  2.2 0.0 copy-start.3
  2.2 13.0 %all-to-all-start = ((f32[32,8,256]{2,1,0:T(8,128)}), f32[32,8,256]{2,1,0:T(8,128)S(1)}, u32[]{:S(2)}, u32[]{:S(2)}) async-start(f32[32,8,256]{2,1,0:T(8,128)} %broadcast_in_dim.38), calls=%async_computation | async-start | bytes 524288 | tf_op jit(solution)/shard_map/all_to_all | solution.py:159
  15.3 0.0 copy-done.3
  15.3 0.1 reshape.11
  15.4 12.1 %all-to-all-done = f32[32,8,256]{2,1,0:T(8,128)S(1)} async-done(((f32[32,8,256]{2,1,0:T(8,128)}), f32[32,8,256]{2,1,0:T(8,128)S(1)}, u32[]{:S(2)}, u32[]{:S(2)}) %all-to-all-start) | async-done | bytes 262176 | tf_op jit(solution)/shard_map/all_to_all | solution.py:159
  27.5 1.0 broadcast_in_dim.43
  28.5 9.1 %all-to-all-start.1 = ((bf16[16,32,832]{2,1,0:T(8,128)(2,1)}), bf16[16,32,832]{2,1,0:T(8,128)(2,1)S(1)}, u32[]{:S(2)}, u32[]{:S(2)}) async-start(bf16[16,32,832]{2,1,0:T(8,128)(2,1)} %broadcast_in_dim.43), calls=%async_computation.1 | async-start | bytes 1835008 | tf_op jit(solution)/shard_map/all_to_all | solution.py:150
  37.6 2.8 %collective-permute-start = (bf16[832,256]{1,0:T(8,128)(2,1)S(1)}, bf16[832,256]{1,0:T(8,128)(2,1)S(1)}, u32[]{:S(2)}, u32[]{:S(2)}) collective-permute-start(bf16[832,256]{1,0:T(8,128)(2,1)S(1)} %get-tuple-element.13.own), channel_id=1, source_target_pairs={{0,256},{1,257},{64,320},{65,321},{256,0},{257,1},{320,64},{321,65... | collective-permute-start | bytes 1277960 | tf_op jit(solution)/shard_map/ppermute | solution.py:156
  40.4 1.9 %collective-permute-start.1 = (bf16[832,256]{1,0:T(8,128)(2,1)S(1)}, bf16[832,256]{1,0:T(8,128)(2,1)S(1)}, u32[]{:S(2)}, u32[]{:S(2)}) collective-permute-start(bf16[832,256]{1,0:T(8,128)(2,1)S(1)} %get-tuple-element.13.own), channel_id=1, source_target_pairs={{0,64},{1,321},{64,0},{65,257},{256,320},{257,65},{320,256},{321,1... | collective-permute-start | bytes 1277960 | tf_op jit(solution)/shard_map/ppermute | solution.py:157
  42.3 3.7 %collective-permute-start.2 = (bf16[832,256]{1,0:T(8,128)(2,1)S(1)}, bf16[832,256]{1,0:T(8,128)(2,1)S(1)}, u32[]{:S(2)}, u32[]{:S(2)}) collective-permute-start(bf16[832,256]{1,0:T(8,128)(2,1)S(1)} %get-tuple-element.13.own), channel_id=1, source_target_pairs={{0,320},{1,65},{64,256},{65,1},{256,64},{257,321},{320,0},{321,257... | collective-permute-start | bytes 1277960 | tf_op jit(solution)/shard_map/ppermute | solution.py:158
  46.0 0.0 copy-start.5
  46.0 0.6 copy-done.5
  46.6 0.1 copy.12.gain
  46.8 0.5 copy-done.6
  47.3 0.1 copy.13.bias
  47.4 0.1 pad_add_fusion.ids
  47.5 3.5 %collective-permute-done.rx = bf16[832,256]{1,0:T(8,128)(2,1)S(1)} collective-permute-done((bf16[832,256]{1,0:T(8,128)(2,1)S(1)}, bf16[832,256]{1,0:T(8,128)(2,1)S(1)}, u32[]{:S(2)}, u32[]{:S(2)}) %collective-permute-start) | collective-permute-done | bytes 426016 | tf_op jit(solution)/shard_map/ppermute | solution.py:156
  51.0 10.8 %collective-permute-done.1.rk = bf16[832,256]{1,0:T(8,128)(2,1)S(1)} collective-permute-done((bf16[832,256]{1,0:T(8,128)(2,1)S(1)}, bf16[832,256]{1,0:T(8,128)(2,1)S(1)}, u32[]{:S(2)}, u32[]{:S(2)}) %collective-permute-start.1) | collective-permute-done | bytes 426016 | tf_op jit(solution)/shard_map/ppermute | solution.py:157
  61.8 8.1 %collective-permute-done.2.rs = bf16[832,256]{1,0:T(8,128)(2,1)S(1)} collective-permute-done((bf16[832,256]{1,0:T(8,128)(2,1)S(1)}, bf16[832,256]{1,0:T(8,128)(2,1)S(1)}, u32[]{:S(2)}, u32[]{:S(2)}) %collective-permute-start.2) | collective-permute-done | bytes 426016 | tf_op jit(solution)/shard_map/ppermute | solution.py:158
  70.0 0.0 all-to-all-done.1.wg
  70.0 0.9 copy-done.2
  70.9 2.2 %shard_map.83 = (bf16[4,208,256]{2,1,0:T(8,128)(2,1)S(1)}, bf16[4,208,256]{2,1,0:T(8,128)(2,1)}) custom-call(s32[2]{0:T(128)S(1)} %pad_add_fusion.ids, bf16[832,256]{1,0:T(8,128)(2,1)S(1)} %get-tuple-element.13.own, bf16[832,256]{1,0:T(8,128)(2,1)S(1)} %collective-permute-done.rx, bf16[832,256]{1,0:T(8,128)(2,1)S(1)} %collective-permute-done.1.rk, ...), custom_call_target="tpu_custom_call" | custom-call | tf_op jit(solution)/shard_map/pallas_call | solution.py:168
  73.0 2.0 %collective-permute-start.3 = (bf16[4,208,256]{2,1,0:T(8,128)(2,1)}, bf16[4,208,256]{2,1,0:T(8,128)(2,1)S(1)}, u32[]{:S(2)}, u32[]{:S(2)}) collective-permute-start(bf16[4,208,256]{2,1,0:T(8,128)(2,1)} %get-tuple-element.16), channel_id=1, source_target_pairs={{0,1},{1,0},{2,3},{3,2},{4,5},{5,4},{6,7},{7,6},{8,9},{9,8},{10,11... | collective-permute-start | bytes 1277960 | tf_op jit(solution)/shard_map/ppermute | solution.py:183
  75.0 0.0 copy-start.4
  75.0 0.7 copy-done.4
  75.7 0.1 convert_reduce_fusion
  75.8 1.1 collective-permute-done.3.got
  76.9 0.1 shard_map.84
  77.0 2.0 %collective-permute-start.4 = (bf16[208,256]{1,0:T(8,128)(2,1)S(1)}, bf16[208,256]{1,0:T(8,128)(2,1)S(1)}, u32[]{:S(2)}, u32[]{:S(2)}) collective-permute-start(bf16[208,256]{1,0:T(8,128)(2,1)S(1)} %get-tuple-element.17), channel_id=1, source_target_pairs={{0,0},{1,256},{2,2},{3,258},{4,64},{5,320},{6,66},{7,322},{64,65},... | collective-permute-start | bytes 319496 | tf_op jit(solution)/shard_map/ppermute | solution.py:188
  79.0 5.7 %collective-permute-start.5 = (bf16[208,256]{1,0:T(8,128)(2,1)S(1)}, bf16[208,256]{1,0:T(8,128)(2,1)S(1)}, u32[]{:S(2)}, u32[]{:S(2)}) collective-permute-start(bf16[208,256]{1,0:T(8,128)(2,1)S(1)} %get-tuple-element.18), channel_id=1, source_target_pairs={{0,2},{1,258},{2,0},{3,256},{4,66},{5,322},{6,64},{7,320},{64,67},... | collective-permute-start | bytes 319496 | tf_op jit(solution)/shard_map/ppermute | solution.py:188
  84.7 1.9 %collective-permute-start.6 = (bf16[208,256]{1,0:T(8,128)(2,1)S(1)}, bf16[208,256]{1,0:T(8,128)(2,1)S(1)}, u32[]{:S(2)}, u32[]{:S(2)}) collective-permute-start(bf16[208,256]{1,0:T(8,128)(2,1)S(1)} %get-tuple-element.19), channel_id=1, source_target_pairs={{0,64},{1,320},{2,66},{3,322},{4,0},{5,256},{6,2},{7,258},{64,1},{... | collective-permute-start | bytes 319496 | tf_op jit(solution)/shard_map/ppermute | solution.py:188
  86.6 0.0 copy-start.7
  86.6 9.0 %collective-permute-start.7 = (bf16[208,256]{1,0:T(8,128)(2,1)S(1)}, bf16[208,256]{1,0:T(8,128)(2,1)S(1)}, u32[]{:S(2)}, u32[]{:S(2)}) collective-permute-start(bf16[208,256]{1,0:T(8,128)(2,1)S(1)} %get-tuple-element.20), channel_id=1, source_target_pairs={{0,66},{1,322},{2,64},{3,320},{4,2},{5,258},{6,0},{7,256},{64,3},{... | collective-permute-start | bytes 319496 | tf_op jit(solution)/shard_map/ppermute | solution.py:188
  95.7 0.0 copy-done.7
  95.7 0.1 copy.14.bias
  95.9 0.0 collective-permute-done.4.z0
  95.9 0.0 collective-permute-done.5.z1
  95.9 0.0 collective-permute-done.6.z2
  95.9 1.4 %collective-permute-done.7.z3 = bf16[208,256]{1,0:T(8,128)(2,1)S(1)} collective-permute-done((bf16[208,256]{1,0:T(8,128)(2,1)S(1)}, bf16[208,256]{1,0:T(8,128)(2,1)S(1)}, u32[]{:S(2)}, u32[]{:S(2)}) %collective-permute-start.7) | collective-permute-done | bytes 106528 | tf_op jit(solution)/shard_map/ppermute | solution.py:188
  97.4 0.6 shard_map.85
  98.0 0.0 copy-start.1
  98.0 26.9 %all_to_all.15.got = bf16[64,24,128]{2,1,0:T(8,128)(2,1)S(1)} all-to-all(bf16[64,24,128]{2,1,0:T(8,128)(2,1)S(1)} %shard_map.85), channel_id=1, replica_groups=mesh['zl'=2,'xh'=2,'xl'=2,'y'=8,'zh'=4,'c'=2] {'zl','xh','xl','y'}, dimensions={0} | all-to-all | bytes 786432 | tf_op jit(solution)/shard_map/all_to_all | solution.py:209
  124.9 0.0 copy-done.1
  124.9 1.8 %shard_map.86 = bf16[208,384]{1,0:T(8,128)(2,1)} custom-call(bf16[64,24,128]{2,1,0:T(8,128)(2,1)S(1)} %all_to_all.15.got, bf16[208,384]{1,0:T(8,128)(2,1)S(1)} %copy-done.1), custom_call_target="tpu_custom_call" | custom-call | tf_op jit(solution)/shard_map/pallas_call | solution.py:210
  (12 shorter events, 0.1 us)
Async XLA Ops:
  0.0 1.0 copy-start
  2.2 13.0 %copy-start.3 = (bf16[4,208,26]{1,0,2:T(4,128)(2,1)S(1)}, bf16[4,208,26]{1,0,2:T(4,128)(2,1)}, u32[]{:S(2)}) copy-start(bf16[4,208,26]{1,0,2:T(4,128)(2,1)} %param.11) | copy-start | bytes 129796
  2.2 25.3 %all-to-all-start = ((f32[32,8,256]{2,1,0:T(8,128)}), f32[32,8,256]{2,1,0:T(8,128)S(1)}, u32[]{:S(2)}, u32[]{:S(2)}) async-start(f32[32,8,256]{2,1,0:T(8,128)} %broadcast_in_dim.38), calls=%async_computation | async-start | bytes 524288 | tf_op jit(solution)/shard_map/all_to_all | solution.py:159
  28.5 41.5 %all-to-all-start.1 = ((bf16[16,32,832]{2,1,0:T(8,128)(2,1)}), bf16[16,32,832]{2,1,0:T(8,128)(2,1)S(1)}, u32[]{:S(2)}, u32[]{:S(2)}) async-start(bf16[16,32,832]{2,1,0:T(8,128)(2,1)} %broadcast_in_dim.43), calls=%async_computation.1 | async-start | bytes 1835008 | tf_op jit(solution)/shard_map/all_to_all | solution.py:150
  37.6 13.5 %collective-permute-start = (bf16[832,256]{1,0:T(8,128)(2,1)S(1)}, bf16[832,256]{1,0:T(8,128)(2,1)S(1)}, u32[]{:S(2)}, u32[]{:S(2)}) collective-permute-start(bf16[832,256]{1,0:T(8,128)(2,1)S(1)} %get-tuple-element.13.own), channel_id=1, source_target_pairs={{0,256},{1,257},{64,320},{65,321},{256,0},{257,1},{320,64},{321,65... | collective-permute-start | bytes 1277960 | tf_op jit(solution)/shard_map/ppermute | solution.py:156
  40.4 21.4 %collective-permute-start.1 = (bf16[832,256]{1,0:T(8,128)(2,1)S(1)}, bf16[832,256]{1,0:T(8,128)(2,1)S(1)}, u32[]{:S(2)}, u32[]{:S(2)}) collective-permute-start(bf16[832,256]{1,0:T(8,128)(2,1)S(1)} %get-tuple-element.13.own), channel_id=1, source_target_pairs={{0,64},{1,321},{64,0},{65,257},{256,320},{257,65},{320,256},{321,1... | collective-permute-start | bytes 1277960 | tf_op jit(solution)/shard_map/ppermute | solution.py:157
  42.3 27.7 %collective-permute-start.2 = (bf16[832,256]{1,0:T(8,128)(2,1)S(1)}, bf16[832,256]{1,0:T(8,128)(2,1)S(1)}, u32[]{:S(2)}, u32[]{:S(2)}) collective-permute-start(bf16[832,256]{1,0:T(8,128)(2,1)S(1)} %get-tuple-element.13.own), channel_id=1, source_target_pairs={{0,320},{1,65},{64,256},{65,1},{256,64},{257,321},{320,0},{321,257... | collective-permute-start | bytes 1277960 | tf_op jit(solution)/shard_map/ppermute | solution.py:158
  46.0 0.7 copy-start.5
  46.6 0.7 copy-start.6
  70.0 0.9 copy-start.2
  73.0 3.9 %collective-permute-start.3 = (bf16[4,208,256]{2,1,0:T(8,128)(2,1)}, bf16[4,208,256]{2,1,0:T(8,128)(2,1)S(1)}, u32[]{:S(2)}, u32[]{:S(2)}) collective-permute-start(bf16[4,208,256]{2,1,0:T(8,128)(2,1)} %get-tuple-element.16), channel_id=1, source_target_pairs={{0,1},{1,0},{2,3},{3,2},{4,5},{5,4},{6,7},{7,6},{8,9},{9,8},{10,11... | collective-permute-start | bytes 1277960 | tf_op jit(solution)/shard_map/ppermute | solution.py:183
  75.0 0.7 copy-start.4
  77.0 18.9 %collective-permute-start.4 = (bf16[208,256]{1,0:T(8,128)(2,1)S(1)}, bf16[208,256]{1,0:T(8,128)(2,1)S(1)}, u32[]{:S(2)}, u32[]{:S(2)}) collective-permute-start(bf16[208,256]{1,0:T(8,128)(2,1)S(1)} %get-tuple-element.17), channel_id=1, source_target_pairs={{0,0},{1,256},{2,2},{3,258},{4,64},{5,320},{6,66},{7,322},{64,65},... | collective-permute-start | bytes 319496 | tf_op jit(solution)/shard_map/ppermute | solution.py:188
  79.0 16.9 %collective-permute-start.5 = (bf16[208,256]{1,0:T(8,128)(2,1)S(1)}, bf16[208,256]{1,0:T(8,128)(2,1)S(1)}, u32[]{:S(2)}, u32[]{:S(2)}) collective-permute-start(bf16[208,256]{1,0:T(8,128)(2,1)S(1)} %get-tuple-element.18), channel_id=1, source_target_pairs={{0,2},{1,258},{2,0},{3,256},{4,66},{5,322},{6,64},{7,320},{64,67},... | collective-permute-start | bytes 319496 | tf_op jit(solution)/shard_map/ppermute | solution.py:188
  84.7 11.2 %collective-permute-start.6 = (bf16[208,256]{1,0:T(8,128)(2,1)S(1)}, bf16[208,256]{1,0:T(8,128)(2,1)S(1)}, u32[]{:S(2)}, u32[]{:S(2)}) collective-permute-start(bf16[208,256]{1,0:T(8,128)(2,1)S(1)} %get-tuple-element.19), channel_id=1, source_target_pairs={{0,64},{1,320},{2,66},{3,322},{4,0},{5,256},{6,2},{7,258},{64,1},{... | collective-permute-start | bytes 319496 | tf_op jit(solution)/shard_map/ppermute | solution.py:188
  86.6 9.1 %copy-start.7 = (bf16[208]{0:T(256)(128)(2,1)S(1)}, bf16[208]{0:T(256)(128)(2,1)}, u32[]{:S(2)}) copy-start(bf16[208]{0:T(256)(128)(2,1)} %param.12) | copy-start | bytes 1252
  86.6 10.7 %collective-permute-start.7 = (bf16[208,256]{1,0:T(8,128)(2,1)S(1)}, bf16[208,256]{1,0:T(8,128)(2,1)S(1)}, u32[]{:S(2)}, u32[]{:S(2)}) collective-permute-start(bf16[208,256]{1,0:T(8,128)(2,1)S(1)} %get-tuple-element.20), channel_id=1, source_target_pairs={{0,66},{1,322},{2,64},{3,320},{4,2},{5,258},{6,0},{7,256},{64,3},{... | collective-permute-start | bytes 319496 | tf_op jit(solution)/shard_map/ppermute | solution.py:188
  98.0 26.9 %copy-start.1 = (bf16[208,384]{1,0:T(8,128)(2,1)S(1)}, bf16[208,384]{1,0:T(8,128)(2,1)}, u32[]{:S(2)}) copy-start(bf16[208,384]{1,0:T(8,128)(2,1)} %text.1) | copy-start | bytes 479236

commit v2 on v1

--- a/solution.py
+++ b/solution.py
@@ -24,7 +24,6 @@
 HALF = FEAT // 2
 LANES = 128
 SHARE = ("zl", "xl")
-GATHER = ("xh", "y")
 SEQ = ("zl", "xh", "xl", "y")
 TP = ("zh", "c")
 BF16 = jnp.bfloat16
@@ -66,7 +65,7 @@
 ):
     c, q = ids[0], ids[1]
     for g in range(2):
-        rows = jnp.concatenate([wg[g * 8 + y] for y in range(8)], axis=0)
+        rows = jnp.concatenate([wg[y, g ^ ids[2]] for y in range(8)], axis=0)
         weight[g] = jnp.dot(pack[...], rows, preferred_element_type=F32).astype(BF16)
     gain_col = jnp.broadcast_to(gain[...], (FEAT, ROWS))
     bias_col = jnp.broadcast_to(bias[...], (FEAT, ROWS))
@@ -143,13 +142,12 @@
 
 def shards(patches, ln_gain, ln_bias, merge_weight, merge_bias, targets, text_embed):
     sds = jax.ShapeDtypeStruct
-    zl, xl, zh, c = (lax.axis_index(a) for a in ("zl", "xl", "zh", "c"))
+    zl, xh, xl, zh, c = (lax.axis_index(a) for a in ("zl", "xh", "xl", "zh", "c"))
 
     chunk = jnp.transpose(merge_weight, (2, 0, 1)).reshape(CHUNK, GROUP * FEAT)
     chunk = jnp.pad(chunk, ((0, CHUNK_PAD - CHUNK), (0, 0)))
-    columns = lax.all_to_all(
-        jnp.broadcast_to(chunk[None], (16, CHUNK_PAD, GROUP * FEAT)), GATHER, 0, 0, tiled=True
-    )
+    other = lax.ppermute(chunk, "xh", [(0, 1), (1, 0)])
+    columns = lax.all_gather(jnp.stack([chunk, other]), "y")
 
     own, stats = _call(split_body, (sds((GROUP * FEAT, ROWS), BF16), sds((8, ROWS), F32)), 1)(patches)
     axes, sizes = ("zl", "xl", "c"), (2, 2, 2)
@@ -163,7 +161,7 @@
     packed = np.arange(FEAT)
     pack = np.zeros((FEAT, 8 * CHUNK_PAD), np.float32)
     pack[packed, packed // CHUNK * CHUNK_PAD + packed % CHUNK] = 1.0
-    ids = jnp.stack([c, 2 * zl + xl]).astype(jnp.int32)
+    ids = jnp.stack([c, 2 * zl + xl, xh]).astype(jnp.int32)
     piece = sds((4, FEAT, ROWS), BF16)
     keep, send = pl.pallas_call(
         project_body,

time: 127 us -> 123 us (0.969)
  waiting for transfers between devices: 37 us -> 9.72 us
  blocking collectives: 26.9 us -> 48.2 us
  starting transfers between devices: 51.1 us -> 53.6 us
    all_gather x0 -> x1, blocking collectives: none -> 23.4 us  [shards(): columns = lax.all_gather(jnp.stack([chunk, other]), 'y')]
    all_to_all x1, waiting for transfers between devices: 12.1 us -> 0.01 us  [shards(): lax.all_to_all(jnp.broadcast_to(stats[None], (32, 8, ROWS)), SHARE + TP,...]
    ppermute x1, waiting for transfers between devices: 10.8 us -> 0.01 us  [shards(): lax.ppermute(own, axes, _pairs(sizes, lambda z, x, k: (z ^ k, x ^ 1, k)))]
    all_to_all x1 -> x0, starting transfers between devices: 9.09 us -> none  [shards(): lax.all_to_all(jnp.broadcast_to(chunk[None], (16, CHUNK_PAD, GROUP * FEAT...]
    ppermute x1, waiting for transfers between devices: 8.15 us -> 0.01 us  [shards(): lax.ppermute(own, axes, _pairs(sizes, lambda z, x, k: (z ^ k ^ 1, x ^ 1,...]
    ppermute x0 -> x1, waiting for transfers between devices: none -> 4.67 us  [shards(): other = lax.ppermute(chunk, 'xh', [(0, 1), (1, 0)])]
    ppermute x0 -> x1, starting transfers between devices: none -> 4.62 us  [shards(): other = lax.ppermute(chunk, 'xh', [(0, 1), (1, 0)])]
    ppermute x1, starting transfers between devices: 1.96 us -> 5.78 us  [shards(): got = lax.ppermute(send, 'c', [(0, 1), (1, 0)])]
  transfers between devices with their start and end apart: 10 -> 10, of which waited for: 6 -> 3; matrix products, arithmetic and copies ran while one was open for 1% -> 1% of each run, Pallas kernels for 0% -> 0%
where the time goes in v2:
time: 123 us; the launch traced here: 122 us
  starting transfers between devices  53.6 us (44%)
  blocking collectives  48.2 us (39%)
  waiting for transfers between devices  9.72 us (8%)
  Pallas kernels  5.22 us (4%)
  local copies, waits for them, and re-layouts  4.93 us (4%)
    all_to_all x1, blocking collectives, shards(): rows = lax.all_to_all(sent, SEQ, 0, 0, tiled=True)  24.8 us
    all_gather x1, blocking collectives, shards(): columns = lax.all_gather(jnp.stack([chunk, other]), 'y')  23.4 us
    ppermute x4, starting transfers between devices, shards(): lax.ppermute(parts[k], axes, _pairs(sizes, lambda z, x, h, k2, k=k: (z ^...  21.6 us
    all_to_all x1, starting transfers between devices, shards(): lax.all_to_all(jnp.broadcast_to(stats[None], (32, 8, ROWS)), SHARE + TP,...  11.7 us
    ppermute x1, starting transfers between devices, shards(): got = lax.ppermute(send, 'c', [(0, 1), (1, 0)])  5.78 us
    ppermute x1, starting transfers between devices, shards(): rx = lax.ppermute(own, axes, _pairs(sizes, lambda z, x, k: (z ^ 1, x, k)))  4.83 us
    ppermute x1, waiting for transfers between devices, shards(): other = lax.ppermute(chunk, 'xh', [(0, 1), (1, 0)])  4.67 us
    ppermute x1, starting transfers between devices, shards(): other = lax.ppermute(chunk, 'xh', [(0, 1), (1, 0)])  4.62 us
  transfers between devices with their start and end apart: 10, of which 3 were waited for; matrix products, arithmetic and copies ran while one was open for 1% of the time, Pallas kernels for 0%

profile of v2, /device:TPU:1, one launch (start us, length us, event | category | flops | bytes accessed | tf_op | source)
XLA Modules:
  0.0 122.1 jit_solution(11692971707040628189)
XLA Ops:
  0.0 0.0 copy-start
  0.0 1.0 copy-done
  1.0 0.5 shard_map.82
  1.5 4.8 %collective-permute-start = (bf16[832,256]{1,0:T(8,128)(2,1)S(1)}, bf16[832,256]{1,0:T(8,128)(2,1)S(1)}, u32[]{:S(2)}, u32[]{:S(2)}) collective-permute-start(bf16[832,256]{1,0:T(8,128)(2,1)S(1)} %get-tuple-element.13.own), channel_id=1, source_target_pairs={{0,256},{1,257},{64,320},{65,321},{256,0},{257,1},{320,64},{321,65... | collective-permute-start | bytes 1277960 | tf_op jit(solution)/shard_map/ppermute | solution.py:154
  6.4 2.8 %collective-permute-start.1 = (bf16[832,256]{1,0:T(8,128)(2,1)S(1)}, bf16[832,256]{1,0:T(8,128)(2,1)S(1)}, u32[]{:S(2)}, u32[]{:S(2)}) collective-permute-start(bf16[832,256]{1,0:T(8,128)(2,1)S(1)} %get-tuple-element.13.own), channel_id=1, source_target_pairs={{0,64},{1,321},{64,0},{65,257},{256,320},{257,65},{320,256},{321,1... | collective-permute-start | bytes 1277960 | tf_op jit(solution)/shard_map/ppermute | solution.py:155
  9.2 2.2 %collective-permute-start.2 = (bf16[832,256]{1,0:T(8,128)(2,1)S(1)}, bf16[832,256]{1,0:T(8,128)(2,1)S(1)}, u32[]{:S(2)}, u32[]{:S(2)}) collective-permute-start(bf16[832,256]{1,0:T(8,128)(2,1)S(1)} %get-tuple-element.13.own), channel_id=1, source_target_pairs={{0,320},{1,65},{64,256},{65,1},{256,64},{257,321},{320,0},{321,257... | collective-permute-start | bytes 1277960 | tf_op jit(solution)/shard_map/ppermute | solution.py:156
  11.4 0.0 copy-done.3
  11.4 0.1 reshape.10
  11.6 4.6 %collective-permute-start.3 = (bf16[32,832]{1,0:T(8,128)(2,1)S(1)}, bf16[32,832]{1,0:T(8,128)(2,1)S(1)}, u32[]{:S(2)}, u32[]{:S(2)}) collective-permute-start(bf16[32,832]{1,0:T(8,128)(2,1)S(1)} %get-tuple-element.22), channel_id=1, source_target_pairs={{0,128},{128,0},{1,129},{129,1},{2,130},{130,2},{3,131},{131,3},{4... | collective-permute-start | bytes 159752 | tf_op jit(solution)/shard_map/ppermute | solution.py:149
  16.2 0.7 broadcast_in_dim.32
  16.9 11.7 %all-to-all-start = ((f32[32,8,256]{2,1,0:T(8,128)}), f32[32,8,256]{2,1,0:T(8,128)S(1)}, u32[]{:S(2)}, u32[]{:S(2)}) async-start(f32[32,8,256]{2,1,0:T(8,128)} %broadcast_in_dim.32), calls=%async_computation | async-start | bytes 524288 | tf_op jit(solution)/shard_map/all_to_all | solution.py:157
  28.6 0.0 copy-start.5
  28.6 0.1 pad_add_fusion.ids
  28.7 0.6 copy-done.5
  29.2 0.1 copy.15.gain
  29.4 0.5 copy-done.6
  29.9 0.1 copy.16.bias
  30.0 4.7 %collective-permute-done.3 = bf16[32,832]{1,0:T(8,128)(2,1)S(1)} collective-permute-done((bf16[32,832]{1,0:T(8,128)(2,1)S(1)}, bf16[32,832]{1,0:T(8,128)(2,1)S(1)}, u32[]{:S(2)}, u32[]{:S(2)}) %collective-permute-start.3) | collective-permute-done | bytes 53280 | tf_op jit(solution)/shard_map/ppermute | solution.py:149
  34.7 23.4 %all-gather = bf16[16,32,832]{2,1,0:T(8,128)(2,1)S(1)} all-gather(bf16[2,32,832]{2,1,0:T(8,128)(2,1)S(1)} %pad_maximum_fusion), channel_id=2, replica_groups=mesh['zl'=2,'xh'=2,'xl'=2,'y'=8,'zh'=4,'c'=2] {'y'}, dimensions={0}, use_global_device_ids=true | all-gather | bytes 958464 | tf_op jit(solution)/shard_map/all_gather | solution.py:150
  58.1 0.0 collective-permute-done.rx
  58.1 0.0 collective-permute-done.1.rk
  58.1 0.0 collective-permute-done.2.rs
  58.1 0.0 all-to-all-done
  58.1 0.0 copy-start.2
  58.1 0.9 copy-done.2
  59.0 2.2 %shard_map.83 = (bf16[4,208,256]{2,1,0:T(8,128)(2,1)S(1)}, bf16[4,208,256]{2,1,0:T(8,128)(2,1)}) custom-call(s32[3]{0:T(128)S(1)} %pad_add_fusion.ids, bf16[832,256]{1,0:T(8,128)(2,1)S(1)} %get-tuple-element.13.own, bf16[832,256]{1,0:T(8,128)(2,1)S(1)} %collective-permute-done.rx, bf16[832,256]{1,0:T(8,128)(2,1)S(1)} %collective-permute-done.1.rk, ...), custom_call_target="tpu_custom_call" | custom-call | tf_op jit(solution)/shard_map/pallas_call | solution.py:166
  61.2 5.8 %collective-permute-start.4 = (bf16[4,208,256]{2,1,0:T(8,128)(2,1)}, bf16[4,208,256]{2,1,0:T(8,128)(2,1)S(1)}, u32[]{:S(2)}, u32[]{:S(2)}) collective-permute-start(bf16[4,208,256]{2,1,0:T(8,128)(2,1)} %get-tuple-element.16), channel_id=1, source_target_pairs={{0,1},{1,0},{2,3},{3,2},{4,5},{5,4},{6,7},{7,6},{8,9},{9,8},{10,11... | collective-permute-start | bytes 1277960 | tf_op jit(solution)/shard_map/ppermute | solution.py:181
  67.0 0.0 copy-start.4
  67.0 0.7 copy-done.4
  67.7 0.1 convert_reduce_fusion
  67.8 0.8 collective-permute-done.4.got
  68.6 0.1 shard_map.84
  68.7 1.9 %collective-permute-start.5 = (bf16[208,256]{1,0:T(8,128)(2,1)S(1)}, bf16[208,256]{1,0:T(8,128)(2,1)S(1)}, u32[]{:S(2)}, u32[]{:S(2)}) collective-permute-start(bf16[208,256]{1,0:T(8,128)(2,1)S(1)} %get-tuple-element.17), channel_id=1, source_target_pairs={{0,0},{1,256},{2,2},{3,258},{4,64},{5,320},{6,66},{7,322},{64,65},... | collective-permute-start | bytes 319496 | tf_op jit(solution)/shard_map/ppermute | solution.py:186
  70.6 13.2 %collective-permute-start.6 = (bf16[208,256]{1,0:T(8,128)(2,1)S(1)}, bf16[208,256]{1,0:T(8,128)(2,1)S(1)}, u32[]{:S(2)}, u32[]{:S(2)}) collective-permute-start(bf16[208,256]{1,0:T(8,128)(2,1)S(1)} %get-tuple-element.18), channel_id=1, source_target_pairs={{0,2},{1,258},{2,0},{3,256},{4,66},{5,322},{6,64},{7,320},{64,67},... | collective-permute-start | bytes 319496 | tf_op jit(solution)/shard_map/ppermute | solution.py:186
  83.8 3.1 %collective-permute-start.7 = (bf16[208,256]{1,0:T(8,128)(2,1)S(1)}, bf16[208,256]{1,0:T(8,128)(2,1)S(1)}, u32[]{:S(2)}, u32[]{:S(2)}) collective-permute-start(bf16[208,256]{1,0:T(8,128)(2,1)S(1)} %get-tuple-element.19), channel_id=1, source_target_pairs={{0,64},{1,320},{2,66},{3,322},{4,0},{5,256},{6,2},{7,258},{64,1},{... | collective-permute-start | bytes 319496 | tf_op jit(solution)/shard_map/ppermute | solution.py:186
  86.9 0.0 copy-start.7
  86.9 3.4 %collective-permute-start.8 = (bf16[208,256]{1,0:T(8,128)(2,1)S(1)}, bf16[208,256]{1,0:T(8,128)(2,1)S(1)}, u32[]{:S(2)}, u32[]{:S(2)}) collective-permute-start(bf16[208,256]{1,0:T(8,128)(2,1)S(1)} %get-tuple-element.20), channel_id=1, source_target_pairs={{0,66},{1,322},{2,64},{3,320},{4,2},{5,258},{6,0},{7,256},{64,3},{... | collective-permute-start | bytes 319496 | tf_op jit(solution)/shard_map/ppermute | solution.py:186
  90.4 0.0 copy-done.7
  90.4 0.1 copy.17.bias
  90.6 0.0 collective-permute-done.5.z0
  90.6 0.0 collective-permute-done.6.z1
  90.6 0.0 collective-permute-done.7.z2
  90.6 4.3 %collective-permute-done.8.z3 = bf16[208,256]{1,0:T(8,128)(2,1)S(1)} collective-permute-done((bf16[208,256]{1,0:T(8,128)(2,1)S(1)}, bf16[208,256]{1,0:T(8,128)(2,1)S(1)}, u32[]{:S(2)}, u32[]{:S(2)}) %collective-permute-start.8) | collective-permute-done | bytes 106528 | tf_op jit(solution)/shard_map/ppermute | solution.py:186
  94.9 0.6 shard_map.85
  95.5 0.0 copy-start.1
  95.5 24.8 %all_to_all.10.got = bf16[64,24,128]{2,1,0:T(8,128)(2,1)S(1)} all-to-all(bf16[64,24,128]{2,1,0:T(8,128)(2,1)S(1)} %shard_map.85), channel_id=1, replica_groups=mesh['zl'=2,'xh'=2,'xl'=2,'y'=8,'zh'=4,'c'=2] {'zl','xh','xl','y'}, dimensions={0} | all-to-all | bytes 786432 | tf_op jit(solution)/shard_map/all_to_all | solution.py:207
  120.3 0.0 copy-done.1
  120.3 1.8 %shard_map.86 = bf16[208,384]{1,0:T(8,128)(2,1)} custom-call(bf16[64,24,128]{2,1,0:T(8,128)(2,1)S(1)} %all_to_all.10.got, bf16[208,384]{1,0:T(8,128)(2,1)S(1)} %copy-done.1), custom_call_target="tpu_custom_call" | custom-call | tf_op jit(solution)/shard_map/pallas_call | solution.py:208
  (13 shorter events, 0.1 us)
Async XLA Ops:
  0.0 1.0 copy-start
  1.0 10.4 %copy-start.3 = (bf16[4,208,26]{1,0,2:T(4,128)(2,1)S(1)}, bf16[4,208,26]{1,0,2:T(4,128)(2,1)}, u32[]{:S(2)}) copy-start(bf16[4,208,26]{1,0,2:T(4,128)(2,1)} %param.11) | copy-start | bytes 129796
  1.5 56.6 %collective-permute-start = (bf16[832,256]{1,0:T(8,128)(2,1)S(1)}, bf16[832,256]{1,0:T(8,128)(2,1)S(1)}, u32[]{:S(2)}, u32[]{:S(2)}) collective-permute-start(bf16[832,256]{1,0:T(8,128)(2,1)S(1)} %get-tuple-element.13.own), channel_id=1, source_target_pairs={{0,256},{1,257},{64,320},{65,321},{256,0},{257,1},{320,64},{321,65... | collective-permute-start | bytes 1277960 | tf_op jit(solution)/shard_map/ppermute | solution.py:154
  6.4 51.7 %collective-permute-start.1 = (bf16[832,256]{1,0:T(8,128)(2,1)S(1)}, bf16[832,256]{1,0:T(8,128)(2,1)S(1)}, u32[]{:S(2)}, u32[]{:S(2)}) collective-permute-start(bf16[832,256]{1,0:T(8,128)(2,1)S(1)} %get-tuple-element.13.own), channel_id=1, source_target_pairs={{0,64},{1,321},{64,0},{65,257},{256,320},{257,65},{320,256},{321,1... | collective-permute-start | bytes 1277960 | tf_op jit(solution)/shard_map/ppermute | solution.py:155
  9.2 48.9 %collective-permute-start.2 = (bf16[832,256]{1,0:T(8,128)(2,1)S(1)}, bf16[832,256]{1,0:T(8,128)(2,1)S(1)}, u32[]{:S(2)}, u32[]{:S(2)}) collective-permute-start(bf16[832,256]{1,0:T(8,128)(2,1)S(1)} %get-tuple-element.13.own), channel_id=1, source_target_pairs={{0,320},{1,65},{64,256},{65,1},{256,64},{257,321},{320,0},{321,257... | collective-permute-start | bytes 1277960 | tf_op jit(solution)/shard_map/ppermute | solution.py:156
  11.6 23.1 %collective-permute-start.3 = (bf16[32,832]{1,0:T(8,128)(2,1)S(1)}, bf16[32,832]{1,0:T(8,128)(2,1)S(1)}, u32[]{:S(2)}, u32[]{:S(2)}) collective-permute-start(bf16[32,832]{1,0:T(8,128)(2,1)S(1)} %get-tuple-element.22), channel_id=1, source_target_pairs={{0,128},{128,0},{1,129},{129,1},{2,130},{130,2},{3,131},{131,3},{4... | collective-permute-start | bytes 159752 | tf_op jit(solution)/shard_map/ppermute | solution.py:149
  16.9 41.2 %all-to-all-start = ((f32[32,8,256]{2,1,0:T(8,128)}), f32[32,8,256]{2,1,0:T(8,128)S(1)}, u32[]{:S(2)}, u32[]{:S(2)}) async-start(f32[32,8,256]{2,1,0:T(8,128)} %broadcast_in_dim.32), calls=%async_computation | async-start | bytes 524288 | tf_op jit(solution)/shard_map/all_to_all | solution.py:157
  28.6 0.7 copy-start.5
  29.2 0.7 copy-start.6
  58.1 0.9 copy-start.2
  61.2 7.4 %collective-permute-start.4 = (bf16[4,208,256]{2,1,0:T(8,128)(2,1)}, bf16[4,208,256]{2,1,0:T(8,128)(2,1)S(1)}, u32[]{:S(2)}, u32[]{:S(2)}) collective-permute-start(bf16[4,208,256]{2,1,0:T(8,128)(2,1)} %get-tuple-element.16), channel_id=1, source_target_pairs={{0,1},{1,0},{2,3},{3,2},{4,5},{5,4},{6,7},{7,6},{8,9},{9,8},{10,11... | collective-permute-start | bytes 1277960 | tf_op jit(solution)/shard_map/ppermute | solution.py:181
  67.0 0.7 copy-start.4
  68.7 21.9 %collective-permute-start.5 = (bf16[208,256]{1,0:T(8,128)(2,1)S(1)}, bf16[208,256]{1,0:T(8,128)(2,1)S(1)}, u32[]{:S(2)}, u32[]{:S(2)}) collective-permute-start(bf16[208,256]{1,0:T(8,128)(2,1)S(1)} %get-tuple-element.17), channel_id=1, source_target_pairs={{0,0},{1,256},{2,2},{3,258},{4,64},{5,320},{6,66},{7,322},{64,65},... | collective-permute-start | bytes 319496 | tf_op jit(solution)/shard_map/ppermute | solution.py:186
  70.6 20.0 %collective-permute-start.6 = (bf16[208,256]{1,0:T(8,128)(2,1)S(1)}, bf16[208,256]{1,0:T(8,128)(2,1)S(1)}, u32[]{:S(2)}, u32[]{:S(2)}) collective-permute-start(bf16[208,256]{1,0:T(8,128)(2,1)S(1)} %get-tuple-element.18), channel_id=1, source_target_pairs={{0,2},{1,258},{2,0},{3,256},{4,66},{5,322},{6,64},{7,320},{64,67},... | collective-permute-start | bytes 319496 | tf_op jit(solution)/shard_map/ppermute | solution.py:186
  83.8 6.8 %collective-permute-start.7 = (bf16[208,256]{1,0:T(8,128)(2,1)S(1)}, bf16[208,256]{1,0:T(8,128)(2,1)S(1)}, u32[]{:S(2)}, u32[]{:S(2)}) collective-permute-start(bf16[208,256]{1,0:T(8,128)(2,1)S(1)} %get-tuple-element.19), channel_id=1, source_target_pairs={{0,64},{1,320},{2,66},{3,322},{4,0},{5,256},{6,2},{7,258},{64,1},{... | collective-permute-start | bytes 319496 | tf_op jit(solution)/shard_map/ppermute | solution.py:186
  86.9 3.4 %copy-start.7 = (bf16[208]{0:T(256)(128)(2,1)S(1)}, bf16[208]{0:T(256)(128)(2,1)}, u32[]{:S(2)}) copy-start(bf16[208]{0:T(256)(128)(2,1)} %param.12) | copy-start | bytes 1252
  86.9 7.9 %collective-permute-start.8 = (bf16[208,256]{1,0:T(8,128)(2,1)S(1)}, bf16[208,256]{1,0:T(8,128)(2,1)S(1)}, u32[]{:S(2)}, u32[]{:S(2)}) collective-permute-start(bf16[208,256]{1,0:T(8,128)(2,1)S(1)} %get-tuple-element.20), channel_id=1, source_target_pairs={{0,66},{1,322},{2,64},{3,320},{4,2},{5,258},{6,0},{7,256},{64,3},{... | collective-permute-start | bytes 319496 | tf_op jit(solution)/shard_map/ppermute | solution.py:186
  95.5 24.8 %copy-start.1 = (bf16[208,384]{1,0:T(8,128)(2,1)S(1)}, bf16[208,384]{1,0:T(8,128)(2,1)}, u32[]{:S(2)}) copy-start(bf16[208,384]{1,0:T(8,128)(2,1)} %text.1) | copy-start | bytes 479236

commit v3 on v2

--- a/solution.py
+++ b/solution.py
@@ -23,7 +23,6 @@
 SLOTS = 24
 HALF = FEAT // 2
 LANES = 128
-SHARE = ("zl", "xl")
 SEQ = ("zl", "xh", "xl", "y")
 TP = ("zh", "c")
 BF16 = jnp.bfloat16
@@ -60,33 +59,33 @@
             st_ref[pl.ds(GROUP + k, 1), lanes] = jnp.sum(off * off, axis=0, keepdims=True)
 
 
-def project_body(
-    ids, own, rx, rk, rs, st, gain, bias, wg, pack, keep_ref, send_ref, normed, weight
-):
-    c, q = ids[0], ids[1]
-    for g in range(2):
-        rows = jnp.concatenate([wg[y, g ^ ids[2]] for y in range(8)], axis=0)
-        weight[g] = jnp.dot(pack[...], rows, preferred_element_type=F32).astype(BF16)
+def norm_body(x_ref, st, gain, bias, out_ref):
     gain_col = jnp.broadcast_to(gain[...], (FEAT, ROWS))
     bias_col = jnp.broadcast_to(bias[...], (FEAT, ROWS))
+    parts = st[...]
+    mean = jnp.sum(parts[:, :GROUP], axis=0) * (1.0 / N_TP)
+    off = parts[:, :GROUP] - mean[None]
+    var = (jnp.sum(parts[:, GROUP:], axis=0) + FEAT * jnp.sum(off * off, axis=0)) * (1.0 / D)
+    scale = lax.rsqrt(var + 1e-06)
+    for k in range(GROUP):
+        at = pl.ds(k * FEAT, FEAT)
+        centered = x_ref[at, :].astype(F32) - mean[k : k + 1]
+        out_ref[at, :] = (centered * scale[k : k + 1] * gain_col + bias_col).astype(BF16)
+
+
+def project_body(ids, own, rx, rk, rs, wg, pack, keep_ref, send_ref, weight):
+    c, xh = ids[0], ids[1]
+    for g in range(2):
+        rows = jnp.concatenate([wg[y, g ^ xh] for y in range(8)], axis=0)
+        weight[g] = jnp.dot(pack[...], rows, preferred_element_type=F32).astype(BF16)
     for job in range(4):
         kept, i = job // 2 == 1, job % 2
-        e = 2 * (c if kept else 1 - c) + i
-        parts = st[q ^ e]
-        mean = jnp.sum(parts[:, :GROUP], axis=0) * (1.0 / N_TP)
-        off = parts[:, :GROUP] - mean[None]
-        var = (jnp.sum(parts[:, GROUP:], axis=0) + FEAT * jnp.sum(off * off, axis=0)) * (1.0 / D)
-        scale = lax.rsqrt(var + 1e-06)
-        for k in range(GROUP):
-            at = pl.ds(k * FEAT, FEAT)
-            if i == 1:
-                x = (rk if kept else rs)[at, :]
-            else:
-                x = jnp.where((c == 1) == kept, rx[at, :], own[at, :])
-            centered = x.astype(F32) - mean[k : k + 1]
-            normed[at, :] = (centered * scale[k : k + 1] * gain_col + bias_col).astype(BF16)
+        if i == 1:
+            x = (rk if kept else rs)[...]
+        else:
+            x = jnp.where((c == 1) == kept, rx[...], own[...])
         for g in range(2):
-            out = jnp.dot(weight[g], normed[...], preferred_element_type=F32).astype(BF16)
+            out = jnp.dot(weight[g], x, preferred_element_type=F32).astype(BF16)
             (keep_ref if kept else send_ref)[2 * i + g] = out
 
 
@@ -142,7 +141,7 @@
 
 def shards(patches, ln_gain, ln_bias, merge_weight, merge_bias, targets, text_embed):
     sds = jax.ShapeDtypeStruct
-    zl, xh, xl, zh, c = (lax.axis_index(a) for a in ("zl", "xh", "xl", "zh", "c"))
+    xh, zh, c = (lax.axis_index(a) for a in ("xh", "zh", "c"))
 
     chunk = jnp.transpose(merge_weight, (2, 0, 1)).reshape(CHUNK, GROUP * FEAT)
     chunk = jnp.pad(chunk, ((0, CHUNK_PAD - CHUNK), (0, 0)))
@@ -150,33 +149,28 @@
     columns = lax.all_gather(jnp.stack([chunk, other]), "y")
 
     own, stats = _call(split_body, (sds((GROUP * FEAT, ROWS), BF16), sds((8, ROWS), F32)), 1)(patches)
+    all_stats = lax.all_to_all(jnp.broadcast_to(stats[None], (N_TP, 8, ROWS)), TP, 0, 0, tiled=True)
+    own = _call(norm_body, sds((GROUP * FEAT, ROWS), BF16), 4)(
+        own, all_stats, ln_gain.astype(F32)[:, None], ln_bias.astype(F32)[:, None]
+    )
     axes, sizes = ("zl", "xl", "c"), (2, 2, 2)
     rx = lax.ppermute(own, axes, _pairs(sizes, lambda z, x, k: (z ^ 1, x, k)))
     rk = lax.ppermute(own, axes, _pairs(sizes, lambda z, x, k: (z ^ k, x ^ 1, k)))
     rs = lax.ppermute(own, axes, _pairs(sizes, lambda z, x, k: (z ^ k ^ 1, x ^ 1, k)))
-    all_stats = lax.all_to_all(
-        jnp.broadcast_to(stats[None], (32, 8, ROWS)), SHARE + TP, 0, 0, tiled=True
-    ).reshape(4, N_TP, 8, ROWS)
 
     packed = np.arange(FEAT)
     pack = np.zeros((FEAT, 8 * CHUNK_PAD), np.float32)
     pack[packed, packed // CHUNK * CHUNK_PAD + packed % CHUNK] = 1.0
-    ids = jnp.stack([c, 2 * zl + xl, xh]).astype(jnp.int32)
+    ids = jnp.stack([c, xh]).astype(jnp.int32)
     piece = sds((4, FEAT, ROWS), BF16)
     keep, send = pl.pallas_call(
         project_body,
         out_shape=(piece, piece),
-        in_specs=[pl.BlockSpec(memory_space=pltpu.SMEM)] + _vmem(9),
+        in_specs=[pl.BlockSpec(memory_space=pltpu.SMEM)] + _vmem(6),
         out_specs=tuple(_vmem(2)),
-        scratch_shapes=[
-            pltpu.VMEM((GROUP * FEAT, ROWS), BF16),
-            pltpu.VMEM((2, FEAT, GROUP * FEAT), BF16),
-        ],
+        scratch_shapes=[pltpu.VMEM((2, FEAT, GROUP * FEAT), BF16)],
         compiler_params=pltpu.CompilerParams(vmem_limit_bytes=48 << 20),
-    )(
-        ids, own, rx, rk, rs, all_stats,
-        ln_gain.astype(F32)[:, None], ln_bias.astype(F32)[:, None], columns, jnp.asarray(pack, BF16),
-    )
+    )(ids, own, rx, rk, rs, columns, jnp.asarray(pack, BF16))
 
     got = lax.ppermute(send, "c", [(0, 1), (1, 0)])
     part = sds((FEAT, ROWS), BF16)

time: 123 us -> 115 us (0.935)
  waiting for transfers between devices: 9.72 us -> 4.93 us
    ppermute x1, waiting for transfers between devices: 4.67 us -> 0.01 us  [shards(): other = lax.ppermute(chunk, 'xh', [(0, 1), (1, 0)])]
    ppermute x1, starting transfers between devices: 5.78 us -> 8.91 us  [shards(): got = lax.ppermute(send, 'c', [(0, 1), (1, 0)])]
    ppermute x4, starting transfers between devices: 21.6 us -> 18.6 us  [shards(): lax.ppermute(parts[k], axes, _pairs(sizes, lambda z, x, h, k2, k=k: (z ^...]
    ppermute x1, starting transfers between devices: 4.83 us -> 2.74 us  [shards(): rx = lax.ppermute(own, axes, _pairs(sizes, lambda z, x, k: (z ^ 1, x, k)))]
    all_to_all x1, waiting for transfers between devices: 0.01 us -> 1.54 us  [shards(): lax.all_to_all(jnp.broadcast_to(stats[None], (N_TP, 8, ROWS)), TP, 0, 0,...]
    ppermute x4, waiting for transfers between devices: 4.28 us -> 2.83 us  [shards(): lax.ppermute(parts[k], axes, _pairs(sizes, lambda z, x, h, k2, k=k: (z ^...]
where the time goes in v3:
time: 115 us; the launch traced here: 114 us
  starting transfers between devices  52.5 us (46%)
  blocking collectives  47.3 us (41%)
  Pallas kernels  5.09 us (4%)
  waiting for transfers between devices  4.93 us (4%)
  local copies, waits for them, and re-layouts  3.97 us (3%)
    all_to_all x1, blocking collectives, shards(): rows = lax.all_to_all(sent, SEQ, 0, 0, tiled=True)  24.4 us
    all_gather x1, blocking collectives, shards(): columns = lax.all_gather(jnp.stack([chunk, other]), 'y')  22.9 us
    ppermute x4, starting transfers between devices, shards(): lax.ppermute(parts[k], axes, _pairs(sizes, lambda z, x, h, k2, k=k: (z ^...  18.6 us
    all_to_all x1, starting transfers between devices, shards(): lax.all_to_all(jnp.broadcast_to(stats[None], (N_TP, 8, ROWS)), TP, 0, 0,...  11.9 us
    ppermute x1, starting transfers between devices, shards(): got = lax.ppermute(send, 'c', [(0, 1), (1, 0)])  8.91 us
    ppermute x1, starting transfers between devices, shards(): other = lax.ppermute(chunk, 'xh', [(0, 1), (1, 0)])  4.65 us
    ppermute x1, starting transfers between devices, shards(): lax.ppermute(own, axes, _pairs(sizes, lambda z, x, k: (z ^ k, x ^ 1, k)))  3.46 us
    ppermute x4, waiting for transfers between devices, shards(): lax.ppermute(parts[k], axes, _pairs(sizes, lambda z, x, h, k2, k=k: (z ^...  2.83 us
  transfers between devices with their start and end apart: 10, of which 3 were waited for; matrix products, arithmetic and copies ran while one was open for 1% of the time, Pallas kernels for 0%

profile of v3, /device:TPU:1, one launch (start us, length us, event | category | flops | bytes accessed | tf_op | source)
XLA Modules:
  0.0 114.4 jit_solution(15989022083060918026)
XLA Ops:
  0.0 1.0 copy-done
  1.0 0.5 shard_map.82
  1.5 0.6 broadcast_in_dim.32
  2.2 11.9 %all-to-all-start = ((f32[8,8,256]{2,1,0:T(8,128)}), f32[8,8,256]{2,1,0:T(8,128)S(1)}, u32[]{:S(2)}, u32[]{:S(2)}) async-start(f32[8,8,256]{2,1,0:T(8,128)} %broadcast_in_dim.32), calls=%async_computation | async-start | bytes 131072 | tf_op jit(solution)/shard_map/all_to_all | solution.py:152
  14.1 0.0 copy-done.3
  14.1 0.1 reshape.6
  14.2 4.7 %collective-permute-start.3 = (bf16[32,832]{1,0:T(8,128)(2,1)S(1)}, bf16[32,832]{1,0:T(8,128)(2,1)S(1)}, u32[]{:S(2)}, u32[]{:S(2)}) collective-permute-start(bf16[32,832]{1,0:T(8,128)(2,1)S(1)} %get-tuple-element.22), channel_id=1, source_target_pairs={{0,128},{128,0},{1,129},{129,1},{2,130},{130,2},{3,131},{131,3},{4... | collective-permute-start | bytes 159752 | tf_op jit(solution)/shard_map/ppermute | solution.py:148
  18.9 0.0 copy-start.5
  18.9 0.1 pad_add_fusion.ids
  19.0 0.6 copy-done.5
  19.6 0.1 copy.15.gain
  19.7 0.5 copy-done.6
  20.2 0.1 copy.16.bias
  20.3 1.5 %all-to-all-done.st = f32[8,8,256]{2,1,0:T(8,128)S(1)} async-done(((f32[8,8,256]{2,1,0:T(8,128)}), f32[8,8,256]{2,1,0:T(8,128)S(1)}, u32[]{:S(2)}, u32[]{:S(2)}) %all-to-all-start) | async-done | bytes 65568 | tf_op jit(solution)/shard_map/all_to_all | solution.py:152
  21.9 0.2 shard_map.83.own
  22.1 2.7 %collective-permute-start = (bf16[832,256]{1,0:T(8,128)(2,1)S(1)}, bf16[832,256]{1,0:T(8,128)(2,1)S(1)}, u32[]{:S(2)}, u32[]{:S(2)}) collective-permute-start(bf16[832,256]{1,0:T(8,128)(2,1)S(1)} %shard_map.83.own), channel_id=1, source_target_pairs={{0,256},{1,257},{64,320},{65,321},{256,0},{257,1},{320,64},{321,65... | collective-permute-start | bytes 1277960 | tf_op jit(solution)/shard_map/ppermute | solution.py:157
  24.8 3.5 %collective-permute-start.1 = (bf16[832,256]{1,0:T(8,128)(2,1)S(1)}, bf16[832,256]{1,0:T(8,128)(2,1)S(1)}, u32[]{:S(2)}, u32[]{:S(2)}) collective-permute-start(bf16[832,256]{1,0:T(8,128)(2,1)S(1)} %shard_map.83.own), channel_id=1, source_target_pairs={{0,64},{1,321},{64,0},{65,257},{256,320},{257,65},{320,256},{321,1... | collective-permute-start | bytes 1277960 | tf_op jit(solution)/shard_map/ppermute | solution.py:158
  28.3 2.2 %collective-permute-start.2 = (bf16[832,256]{1,0:T(8,128)(2,1)S(1)}, bf16[832,256]{1,0:T(8,128)(2,1)S(1)}, u32[]{:S(2)}, u32[]{:S(2)}) collective-permute-start(bf16[832,256]{1,0:T(8,128)(2,1)S(1)} %shard_map.83.own), channel_id=1, source_target_pairs={{0,320},{1,65},{64,256},{65,1},{256,64},{257,321},{320,0},{321,257... | collective-permute-start | bytes 1277960 | tf_op jit(solution)/shard_map/ppermute | solution.py:159
  30.5 0.0 collective-permute-done.3
  30.5 0.0 copy-start.2
  30.5 22.9 %all-gather = bf16[16,32,832]{2,1,0:T(8,128)(2,1)S(1)} all-gather(bf16[2,32,832]{2,1,0:T(8,128)(2,1)S(1)} %pad_maximum_fusion), channel_id=2, replica_groups=mesh['zl'=2,'xh'=2,'xl'=2,'y'=8,'zh'=4,'c'=2] {'y'}, dimensions={0}, use_global_device_ids=true | all-gather | bytes 958464 | tf_op jit(solution)/shard_map/all_gather | solution.py:149
  53.5 0.0 collective-permute-done.rx
  53.5 0.0 collective-permute-done.1.rk
  53.5 0.0 collective-permute-done.2.rs
  53.5 0.0 copy-done.2
  53.5 1.9 %shard_map.84 = (bf16[4,208,256]{2,1,0:T(8,128)(2,1)S(1)}, bf16[4,208,256]{2,1,0:T(8,128)(2,1)S(1)}) custom-call(s32[2]{0:T(128)S(1)} %pad_add_fusion.ids, bf16[832,256]{1,0:T(8,128)(2,1)S(1)} %shard_map.83.own, bf16[832,256]{1,0:T(8,128)(2,1)S(1)} %collective-permute-done.rx, bf16[832,256]{1,0:T(8,128)(2,1)S(1)} %collective-permute-done.1.rk, ...), custom_call_target="tpu_custom_call" | custom-call | tf_op jit(solution)/shard_map/pallas_call | solution.py:166
  55.4 8.9 %collective-permute-start.4 = (bf16[4,208,256]{2,1,0:T(8,128)(2,1)S(1)}, bf16[4,208,256]{2,1,0:T(8,128)(2,1)S(1)}, u32[]{:S(2)}, u32[]{:S(2)}) collective-permute-start(bf16[4,208,256]{2,1,0:T(8,128)(2,1)S(1)} %get-tuple-element.16), channel_id=1, source_target_pairs={{0,1},{1,0},{2,3},{3,2},{4,5},{5,4},{6,7},{7,6},{8,9},{9,8},{10,11... | collective-permute-start | bytes 1277960 | tf_op jit(solution)/shard_map/ppermute | solution.py:175
  64.3 0.0 copy-start.4
  64.3 0.7 copy-done.4
  65.0 0.1 convert_reduce_fusion
  65.1 0.5 collective-permute-done.4.got
  65.7 0.1 shard_map.85
  65.8 3.0 %collective-permute-start.5 = (bf16[208,256]{1,0:T(8,128)(2,1)S(1)}, bf16[208,256]{1,0:T(8,128)(2,1)S(1)}, u32[]{:S(2)}, u32[]{:S(2)}) collective-permute-start(bf16[208,256]{1,0:T(8,128)(2,1)S(1)} %get-tuple-element.17), channel_id=1, source_target_pairs={{0,0},{1,256},{2,2},{3,258},{4,64},{5,320},{6,66},{7,322},{64,65},... | collective-permute-start | bytes 319496 | tf_op jit(solution)/shard_map/ppermute | solution.py:180
  68.8 6.2 %collective-permute-start.6 = (bf16[208,256]{1,0:T(8,128)(2,1)S(1)}, bf16[208,256]{1,0:T(8,128)(2,1)S(1)}, u32[]{:S(2)}, u32[]{:S(2)}) collective-permute-start(bf16[208,256]{1,0:T(8,128)(2,1)S(1)} %get-tuple-element.18), channel_id=1, source_target_pairs={{0,2},{1,258},{2,0},{3,256},{4,66},{5,322},{6,64},{7,320},{64,67},... | collective-permute-start | bytes 319496 | tf_op jit(solution)/shard_map/ppermute | solution.py:180
  75.0 1.9 %collective-permute-start.7 = (bf16[208,256]{1,0:T(8,128)(2,1)S(1)}, bf16[208,256]{1,0:T(8,128)(2,1)S(1)}, u32[]{:S(2)}, u32[]{:S(2)}) collective-permute-start(bf16[208,256]{1,0:T(8,128)(2,1)S(1)} %get-tuple-element.19), channel_id=1, source_target_pairs={{0,64},{1,320},{2,66},{3,322},{4,0},{5,256},{6,2},{7,258},{64,1},{... | collective-permute-start | bytes 319496 | tf_op jit(solution)/shard_map/ppermute | solution.py:180
  76.9 0.0 copy-start.7
  76.9 7.5 %collective-permute-start.8 = (bf16[208,256]{1,0:T(8,128)(2,1)S(1)}, bf16[208,256]{1,0:T(8,128)(2,1)S(1)}, u32[]{:S(2)}, u32[]{:S(2)}) collective-permute-start(bf16[208,256]{1,0:T(8,128)(2,1)S(1)} %get-tuple-element.20), channel_id=1, source_target_pairs={{0,66},{1,322},{2,64},{3,320},{4,2},{5,258},{6,0},{7,256},{64,3},{... | collective-permute-start | bytes 319496 | tf_op jit(solution)/shard_map/ppermute | solution.py:180
  84.5 0.0 copy-done.7
  84.5 0.1 copy.17.bias
  84.7 0.0 collective-permute-done.5.z0
  84.7 0.0 collective-permute-done.6.z1
  84.7 0.0 collective-permute-done.7.z2
  84.7 2.8 %collective-permute-done.8.z3 = bf16[208,256]{1,0:T(8,128)(2,1)S(1)} collective-permute-done((bf16[208,256]{1,0:T(8,128)(2,1)S(1)}, bf16[208,256]{1,0:T(8,128)(2,1)S(1)}, u32[]{:S(2)}, u32[]{:S(2)}) %collective-permute-start.8) | collective-permute-done | bytes 106528 | tf_op jit(solution)/shard_map/ppermute | solution.py:180
  87.5 0.6 shard_map.86
  88.2 0.0 copy-start.1
  88.2 24.4 %all_to_all.10.got = bf16[64,24,128]{2,1,0:T(8,128)(2,1)S(1)} all-to-all(bf16[64,24,128]{2,1,0:T(8,128)(2,1)S(1)} %shard_map.86), channel_id=1, replica_groups=mesh['zl'=2,'xh'=2,'xl'=2,'y'=8,'zh'=4,'c'=2] {'zl','xh','xl','y'}, dimensions={0} | all-to-all | bytes 786432 | tf_op jit(solution)/shard_map/all_to_all | solution.py:201
  112.6 0.0 copy-done.1
  112.6 1.8 %shard_map.87 = bf16[208,384]{1,0:T(8,128)(2,1)} custom-call(bf16[64,24,128]{2,1,0:T(8,128)(2,1)S(1)} %all_to_all.10.got, bf16[208,384]{1,0:T(8,128)(2,1)S(1)} %copy-done.1), custom_call_target="tpu_custom_call" | custom-call | tf_op jit(solution)/shard_map/pallas_call | solution.py:202
  (14 shorter events, 0.1 us)
Async XLA Ops:
  0.0 1.0 copy-start
  2.1 11.9 %copy-start.3 = (bf16[4,208,26]{1,0,2:T(4,128)(2,1)S(1)}, bf16[4,208,26]{1,0,2:T(4,128)(2,1)}, u32[]{:S(2)}) copy-start(bf16[4,208,26]{1,0,2:T(4,128)(2,1)} %param.11) | copy-start | bytes 129796
  2.2 19.7 %all-to-all-start = ((f32[8,8,256]{2,1,0:T(8,128)}), f32[8,8,256]{2,1,0:T(8,128)S(1)}, u32[]{:S(2)}, u32[]{:S(2)}) async-start(f32[8,8,256]{2,1,0:T(8,128)} %broadcast_in_dim.32), calls=%async_computation | async-start | bytes 131072 | tf_op jit(solution)/shard_map/all_to_all | solution.py:152
  14.2 16.3 %collective-permute-start.3 = (bf16[32,832]{1,0:T(8,128)(2,1)S(1)}, bf16[32,832]{1,0:T(8,128)(2,1)S(1)}, u32[]{:S(2)}, u32[]{:S(2)}) collective-permute-start(bf16[32,832]{1,0:T(8,128)(2,1)S(1)} %get-tuple-element.22), channel_id=1, source_target_pairs={{0,128},{128,0},{1,129},{129,1},{2,130},{130,2},{3,131},{131,3},{4... | collective-permute-start | bytes 159752 | tf_op jit(solution)/shard_map/ppermute | solution.py:148
  18.9 0.7 copy-start.5
  19.6 0.7 copy-start.6
  22.1 31.4 %collective-permute-start = (bf16[832,256]{1,0:T(8,128)(2,1)S(1)}, bf16[832,256]{1,0:T(8,128)(2,1)S(1)}, u32[]{:S(2)}, u32[]{:S(2)}) collective-permute-start(bf16[832,256]{1,0:T(8,128)(2,1)S(1)} %shard_map.83.own), channel_id=1, source_target_pairs={{0,256},{1,257},{64,320},{65,321},{256,0},{257,1},{320,64},{321,65... | collective-permute-start | bytes 1277960 | tf_op jit(solution)/shard_map/ppermute | solution.py:157
  24.8 28.7 %collective-permute-start.1 = (bf16[832,256]{1,0:T(8,128)(2,1)S(1)}, bf16[832,256]{1,0:T(8,128)(2,1)S(1)}, u32[]{:S(2)}, u32[]{:S(2)}) collective-permute-start(bf16[832,256]{1,0:T(8,128)(2,1)S(1)} %shard_map.83.own), channel_id=1, source_target_pairs={{0,64},{1,321},{64,0},{65,257},{256,320},{257,65},{320,256},{321,1... | collective-permute-start | bytes 1277960 | tf_op jit(solution)/shard_map/ppermute | solution.py:158
  28.3 25.2 %collective-permute-start.2 = (bf16[832,256]{1,0:T(8,128)(2,1)S(1)}, bf16[832,256]{1,0:T(8,128)(2,1)S(1)}, u32[]{:S(2)}, u32[]{:S(2)}) collective-permute-start(bf16[832,256]{1,0:T(8,128)(2,1)S(1)} %shard_map.83.own), channel_id=1, source_target_pairs={{0,320},{1,65},{64,256},{65,1},{256,64},{257,321},{320,0},{321,257... | collective-permute-start | bytes 1277960 | tf_op jit(solution)/shard_map/ppermute | solution.py:159
  30.5 23.0 %copy-start.2 = (bf16[208,256]{1,0:T(8,128)(2,1)S(1)}, bf16[208,256]{1,0:T(8,128)(2,1)}, u32[]{:S(2)}) copy-start(bf16[208,256]{1,0:T(8,128)(2,1)} %constant.65.clone.pack) | copy-start | bytes 319492
  55.4 10.3 %collective-permute-start.4 = (bf16[4,208,256]{2,1,0:T(8,128)(2,1)S(1)}, bf16[4,208,256]{2,1,0:T(8,128)(2,1)S(1)}, u32[]{:S(2)}, u32[]{:S(2)}) collective-permute-start(bf16[4,208,256]{2,1,0:T(8,128)(2,1)S(1)} %get-tuple-element.16), channel_id=1, source_target_pairs={{0,1},{1,0},{2,3},{3,2},{4,5},{5,4},{6,7},{7,6},{8,9},{9,8},{10,11... | collective-permute-start | bytes 1277960 | tf_op jit(solution)/shard_map/ppermute | solution.py:175
  64.3 0.7 copy-start.4
  65.8 18.9 %collective-permute-start.5 = (bf16[208,256]{1,0:T(8,128)(2,1)S(1)}, bf16[208,256]{1,0:T(8,128)(2,1)S(1)}, u32[]{:S(2)}, u32[]{:S(2)}) collective-permute-start(bf16[208,256]{1,0:T(8,128)(2,1)S(1)} %get-tuple-element.17), channel_id=1, source_target_pairs={{0,0},{1,256},{2,2},{3,258},{4,64},{5,320},{6,66},{7,322},{64,65},... | collective-permute-start | bytes 319496 | tf_op jit(solution)/shard_map/ppermute | solution.py:180
  68.8 15.9 %collective-permute-start.6 = (bf16[208,256]{1,0:T(8,128)(2,1)S(1)}, bf16[208,256]{1,0:T(8,128)(2,1)S(1)}, u32[]{:S(2)}, u32[]{:S(2)}) collective-permute-start(bf16[208,256]{1,0:T(8,128)(2,1)S(1)} %get-tuple-element.18), channel_id=1, source_target_pairs={{0,2},{1,258},{2,0},{3,256},{4,66},{5,322},{6,64},{7,320},{64,67},... | collective-permute-start | bytes 319496 | tf_op jit(solution)/shard_map/ppermute | solution.py:180
  75.0 9.7 %collective-permute-start.7 = (bf16[208,256]{1,0:T(8,128)(2,1)S(1)}, bf16[208,256]{1,0:T(8,128)(2,1)S(1)}, u32[]{:S(2)}, u32[]{:S(2)}) collective-permute-start(bf16[208,256]{1,0:T(8,128)(2,1)S(1)} %get-tuple-element.19), channel_id=1, source_target_pairs={{0,64},{1,320},{2,66},{3,322},{4,0},{5,256},{6,2},{7,258},{64,1},{... | collective-permute-start | bytes 319496 | tf_op jit(solution)/shard_map/ppermute | solution.py:180
  76.9 7.6 %copy-start.7 = (bf16[208]{0:T(256)(128)(2,1)S(1)}, bf16[208]{0:T(256)(128)(2,1)}, u32[]{:S(2)}) copy-start(bf16[208]{0:T(256)(128)(2,1)} %param.12) | copy-start | bytes 1252
  76.9 10.6 %collective-permute-start.8 = (bf16[208,256]{1,0:T(8,128)(2,1)S(1)}, bf16[208,256]{1,0:T(8,128)(2,1)S(1)}, u32[]{:S(2)}, u32[]{:S(2)}) collective-permute-start(bf16[208,256]{1,0:T(8,128)(2,1)S(1)} %get-tuple-element.20), channel_id=1, source_target_pairs={{0,66},{1,322},{2,64},{3,320},{4,2},{5,258},{6,0},{7,256},{64,3},{... | collective-permute-start | bytes 319496 | tf_op jit(solution)/shard_map/ppermute | solution.py:180
  88.2 24.4 %copy-start.1 = (bf16[208,384]{1,0:T(8,128)(2,1)S(1)}, bf16[208,384]{1,0:T(8,128)(2,1)}, u32[]{:S(2)}) copy-start(bf16[208,384]{1,0:T(8,128)(2,1)} %text.1) | copy-start | bytes 479236

commit v4 on v3

--- a/solution.py
+++ b/solution.py
@@ -23,7 +23,7 @@
 SLOTS = 24
 HALF = FEAT // 2
 LANES = 128
-SEQ = ("zl", "xh", "xl", "y")
+SEQ = ("zl", "xh", "xl", "yh", "yl")
 TP = ("zh", "c")
 BF16 = jnp.bfloat16
 F32 = jnp.float32
@@ -33,17 +33,18 @@
     return [pl.BlockSpec(memory_space=pltpu.VMEM)] * n
 
 
-def _call(body, outs, n_in, n_smem=0):
+def _call(body, outs, n_in, n_smem=0, scratch=()):
     return pl.pallas_call(
         body,
         out_shape=outs,
         in_specs=[pl.BlockSpec(memory_space=pltpu.SMEM)] * n_smem + _vmem(n_in),
         out_specs=jax.tree.map(lambda _: pl.BlockSpec(memory_space=pltpu.VMEM), outs),
+        scratch_shapes=scratch,
         compiler_params=pltpu.CompilerParams(vmem_limit_bytes=48 << 20),
     )
 
 
-def split_body(x_ref, xd_ref, st_ref):
+def split_body(x_ref, xd_ref, st_ref, part):
     row = lax.broadcasted_iota(jnp.int32, (512, 512), 0)
     col = lax.broadcasted_iota(jnp.int32, (512, 512), 1)
     pick = jnp.where(row == 4 * (col & 127) + (col >> 7), 1.0, 0.0).astype(BF16)
@@ -55,11 +56,13 @@
             xd_ref[pl.ds(k * FEAT, FEAT), lanes] = block.astype(BF16)
             mean = jnp.sum(block, axis=0, keepdims=True) * (1.0 / FEAT)
             off = block - mean
-            st_ref[pl.ds(k, 1), lanes] = mean
-            st_ref[pl.ds(GROUP + k, 1), lanes] = jnp.sum(off * off, axis=0, keepdims=True)
-
-
-def norm_body(x_ref, st, gain, bias, out_ref):
+            part[pl.ds(k, 1), lanes] = mean
+            part[pl.ds(GROUP + k, 1), lanes] = jnp.sum(off * off, axis=0, keepdims=True)
+    for t in range(N_TP):
+        st_ref[t] = part[...]
+
+
+def norm_body(x_ref, st, gain, bias, _, out_ref):
     gain_col = jnp.broadcast_to(gain[...], (FEAT, ROWS))
     bias_col = jnp.broadcast_to(bias[...], (FEAT, ROWS))
     parts = st[...]
@@ -73,11 +76,21 @@
         out_ref[at, :] = (centered * scale[k : k + 1] * gain_col + bias_col).astype(BF16)
 
 
-def project_body(ids, own, rx, rk, rs, wg, pack, keep_ref, send_ref, weight):
-    c, xh = ids[0], ids[1]
+def pack_body(ids, mine, theirs, pack, out_ref):
+    parts = []
     for g in range(2):
-        rows = jnp.concatenate([wg[y, g ^ xh] for y in range(8)], axis=0)
-        weight[g] = jnp.dot(pack[...], rows, preferred_element_type=F32).astype(BF16)
+        for y in range(2):
+            i = g ^ ids[0]
+            parts.append(jnp.where(ids[1] == y, mine[i], theirs[i]))
+    rows = jnp.concatenate(parts, axis=0)
+    out_ref[...] = jnp.dot(pack[...], rows, preferred_element_type=F32).astype(BF16)
+
+
+def project_body(ids, own, rx, rk, rs, wg, order, keep_ref, send_ref, weight):
+    c = ids[0]
+    for g in range(2):
+        rows = [jnp.dot(order[g, y], wg[y], preferred_element_type=F32) for y in range(4)]
+        weight[g] = ((rows[0] + rows[1]) + (rows[2] + rows[3])).astype(BF16)
     for job in range(4):
         kept, i = job // 2 == 1, job % 2
         if i == 1:
@@ -115,17 +128,16 @@
 
 
 def final_body(got, text, out_ref):
-    rows = got[...].reshape(N_SEQ * SLOTS, LANES)
-    tags = rows.astype(F32)
-    at = tags[:, HALF : HALF + 1] * 16.0 + tags[:, HALF + 1 : HALF + 2] - 16.0
-    side = tags[:, HALF + 3 : HALF + 4]
-    want = lax.broadcasted_iota(jnp.int32, (N_SEQ * SLOTS, POS), 1).astype(F32)
+    rows = got[...].reshape(N_SEQ * SLOTS, LANES).astype(F32).T
+    at = rows[HALF : HALF + 1] * 16.0 + rows[HALF + 1 : HALF + 2] - 16.0
+    side = rows[HALF + 3 : HALF + 4]
+    want = lax.broadcasted_iota(jnp.int32, (POS, N_SEQ * SLOTS), 0).astype(F32)
+    pick = jnp.where(want == at, 1.0, 0.0).astype(BF16)
     halves = []
     for h in range(2):
-        mine = jnp.where(side == float(h), at, -1.0)
-        pick = jnp.where(want == mine, 1.0, 0.0).astype(BF16)
+        mine = jnp.where(side == float(h), rows, 0.0).astype(BF16)
         halves.append(
-            lax.dot_general(rows, pick, (((0,), (0,)), ((), ())), preferred_element_type=F32)
+            lax.dot_general(mine, pick, (((1,), (1,)), ((), ())), preferred_element_type=F32)
         )
     hit = halves[0][HALF + 2 : HALF + 3] > 0.5
     full = jnp.concatenate([halves[0][:HALF], halves[1][:HALF]], axis=0)
@@ -141,27 +153,40 @@
 
 def shards(patches, ln_gain, ln_bias, merge_weight, merge_bias, targets, text_embed):
     sds = jax.ShapeDtypeStruct
-    xh, zh, c = (lax.axis_index(a) for a in ("xh", "zh", "c"))
+    xh, yl, zh, c = (lax.axis_index(a) for a in ("xh", "yl", "zh", "c"))
 
     chunk = jnp.transpose(merge_weight, (2, 0, 1)).reshape(CHUNK, GROUP * FEAT)
     chunk = jnp.pad(chunk, ((0, CHUNK_PAD - CHUNK), (0, 0)))
-    other = lax.ppermute(chunk, "xh", [(0, 1), (1, 0)])
-    columns = lax.all_gather(jnp.stack([chunk, other]), "y")
-
-    own, stats = _call(split_body, (sds((GROUP * FEAT, ROWS), BF16), sds((8, ROWS), F32)), 1)(patches)
-    all_stats = lax.all_to_all(jnp.broadcast_to(stats[None], (N_TP, 8, ROWS)), TP, 0, 0, tiled=True)
-    own = _call(norm_body, sds((GROUP * FEAT, ROWS), BF16), 4)(
-        own, all_stats, ln_gain.astype(F32)[:, None], ln_bias.astype(F32)[:, None]
+    pair = jnp.stack([chunk, lax.ppermute(chunk, "xh", [(0, 1), (1, 0)])])
+    pair_y = lax.ppermute(pair, "yl", [(0, 1), (1, 0)])
+    packed = np.arange(4 * CHUNK)
+    pack = np.zeros((4 * CHUNK, 4 * CHUNK_PAD), np.float32)
+    pack[packed, packed // CHUNK * CHUNK_PAD + packed % CHUNK] = 1.0
+    quad = _call(pack_body, sds((4 * CHUNK, GROUP * FEAT), BF16), 3, 1)(
+        jnp.stack([xh, yl]).astype(jnp.int32), pair, pair_y, jnp.asarray(pack, BF16)
+    )
+    columns = lax.all_gather(quad, "yh")
+
+    own, stats = _call(
+        split_body,
+        (sds((GROUP * FEAT, ROWS), BF16), sds((N_TP, 8, ROWS), F32)),
+        1,
+        scratch=[pltpu.VMEM((8, ROWS), F32)],
+    )(patches)
+    all_stats = lax.all_to_all(stats, TP, 0, 0, tiled=True)
+    own = _call(norm_body, sds((GROUP * FEAT, ROWS), BF16), 5)(
+        own, all_stats, ln_gain.astype(F32)[:, None], ln_bias.astype(F32)[:, None], pair_y
     )
     axes, sizes = ("zl", "xl", "c"), (2, 2, 2)
     rx = lax.ppermute(own, axes, _pairs(sizes, lambda z, x, k: (z ^ 1, x, k)))
     rk = lax.ppermute(own, axes, _pairs(sizes, lambda z, x, k: (z ^ k, x ^ 1, k)))
     rs = lax.ppermute(own, axes, _pairs(sizes, lambda z, x, k: (z ^ k ^ 1, x ^ 1, k)))
 
-    packed = np.arange(FEAT)
-    pack = np.zeros((FEAT, 8 * CHUNK_PAD), np.float32)
-    pack[packed, packed // CHUNK * CHUNK_PAD + packed % CHUNK] = 1.0
-    ids = jnp.stack([c, xh]).astype(jnp.int32)
+    order = np.zeros((2, 4, FEAT, 4 * CHUNK), np.float32)
+    for g in range(2):
+        for r in range(FEAT):
+            order[g, r // (2 * CHUNK), r, g * 2 * CHUNK + r % (2 * CHUNK)] = 1.0
+    ids = c[None].astype(jnp.int32)
     piece = sds((4, FEAT, ROWS), BF16)
     keep, send = pl.pallas_call(
         project_body,
@@ -170,7 +195,7 @@
         out_specs=tuple(_vmem(2)),
         scratch_shapes=[pltpu.VMEM((2, FEAT, GROUP * FEAT), BF16)],
         compiler_params=pltpu.CompilerParams(vmem_limit_bytes=48 << 20),
-    )(ids, own, rx, rk, rs, columns, jnp.asarray(pack, BF16))
+    )(ids, own, rx, rk, rs, columns, jnp.asarray(order, BF16))
 
     got = lax.ppermute(send, "c", [(0, 1), (1, 0)])
     part = sds((FEAT, ROWS), BF16)
@@ -203,7 +228,7 @@
 
 
 def solution(mesh):
-    wide = Mesh(mesh.devices.reshape(2, 2, 2, 8, 4, 2), ("zl", "xh", "xl", "y", "zh", "c"))
+    wide = Mesh(mesh.devices.reshape(2, 2, 2, 4, 2, 4, 2), ("zl", "xh", "xl", "yh", "yl", "zh", "c"))
     in_specs = (
         P(TP, SEQ),
         P(TP),

time: 115 us -> 113 us (0.983)
  blocking collectives: 47.3 us -> 40 us
  waiting for transfers between devices: 4.93 us -> 7.83 us
  starting transfers between devices: 52.5 us -> 54.6 us
  Pallas kernels: 5.09 us -> 6.35 us
    all_gather x1, blocking collectives: 22.9 us -> 17.5 us  [shards(): columns = lax.all_gather(quad, 'yh')]
    ppermute x1 -> x2, starting transfers between devices: 4.65 us -> 8.69 us  [the longest x1 5.48 us: shards(): pair = jnp.stack([chunk, lax.ppermute(chunk, 'xh', [(0, 1), (1, 0)])])]
    all_to_all x1, waiting for transfers between devices: 1.54 us -> 3.74 us  [shards(): all_stats = lax.all_to_all(stats, TP, 0, 0, tiled=True)]
    all_to_all x1, blocking collectives: 24.4 us -> 22.5 us  [shards(): rows = lax.all_to_all(sent, SEQ, 0, 0, tiled=True)]
    pallas_call x2 -> x3, Pallas kernels: 0.69 us -> 2.08 us  [the longest x1 1.14 us: shards(): _call(split_body, (sds((GROUP * FEAT, ROWS), BF16), sds((N_TP, 8, ROWS),...]
    ppermute x1, starting transfers between devices: 8.91 us -> 7.66 us  [shards(): got = lax.ppermute(send, 'c', [(0, 1), (1, 0)])]
  transfers between devices with their start and end apart: 10 -> 11, of which waited for: 3 -> 4; matrix products, arithmetic and copies ran while one was open for 1% -> 1% of each run, Pallas kernels for 0% -> 2%
where the time goes in v4:
time: 113 us
  starting transfers between devices  54.6 us (48%)
  blocking collectives  40 us (35%)
  waiting for transfers between devices  7.83 us (7%)
  Pallas kernels  6.35 us (6%)
  local copies, waits for them, and re-layouts  3.56 us (3%)
    all_to_all x1, blocking collectives, shards(): rows = lax.all_to_all(sent, SEQ, 0, 0, tiled=True)  22.5 us
    ppermute x4, starting transfers between devices, shards(): lax.ppermute(parts[k], axes, _pairs(sizes, lambda z, x, h, k2, k=k: (z ^...  18.6 us
    all_gather x1, blocking collectives, shards(): columns = lax.all_gather(quad, 'yh')  17.5 us
    all_to_all x1, starting transfers between devices, shards(): all_stats = lax.all_to_all(stats, TP, 0, 0, tiled=True)  11.3 us
    ppermute x1, starting transfers between devices, shards(): got = lax.ppermute(send, 'c', [(0, 1), (1, 0)])  7.66 us
    ppermute x1, starting transfers between devices, shards(): pair = jnp.stack([chunk, lax.ppermute(chunk, 'xh', [(0, 1), (1, 0)])])  5.48 us
    all_to_all x1, waiting for transfers between devices, shards(): all_stats = lax.all_to_all(stats, TP, 0, 0, tiled=True)  3.74 us
    ppermute x4, waiting for transfers between devices, shards(): lax.ppermute(parts[k], axes, _pairs(sizes, lambda z, x, h, k2, k=k: (z ^...  3.41 us
  transfers between devices with their start and end apart: 11, of which 4 were waited for; matrix products, arithmetic and copies ran while one was open for 1% of the time, Pallas kernels for 2%

profile of v4, /device:TPU:1, one launch (start us, length us, event | category | flops | bytes accessed | tf_op | source)
XLA Modules:
  0.0 112.8 jit_solution(10806495380351649018)
XLA Ops:
  0.0 0.9 reshape.5
  0.9 5.5 %collective-permute-start = (bf16[32,832]{1,0:T(8,128)(2,1)S(1)}, bf16[32,832]{1,0:T(8,128)(2,1)S(1)}, u32[]{:S(2)}, u32[]{:S(2)}) collective-permute-start(bf16[32,832]{1,0:T(8,128)(2,1)S(1)} %get-tuple-element.22), channel_id=1, source_target_pairs={{0,128},{128,0},{1,129},{129,1},{2,130},{130,2},{3,131},{131,3},{4... | collective-permute-start | bytes 159752 | tf_op jit(solution)/shard_map/ppermute | solution.py:160
  6.4 0.0 copy-start.1
  6.4 1.0 copy-done.1
  7.4 1.1 %shard_map.91 = (bf16[832,256]{1,0:T(8,128)(2,1)S(1)}, f32[8,8,256]{2,1,0:T(8,128)}) custom-call(bf16[208,1024]{1,0:T(8,128)(2,1)S(1)} %copy-done.1), custom_call_target="tpu_custom_call" | custom-call | tf_op jit(solution)/shard_map/pallas_call | solution.py:170
  8.6 11.3 %all-to-all-start = ((f32[8,8,256]{2,1,0:T(8,128)}), f32[8,8,256]{2,1,0:T(8,128)S(1)}, u32[]{:S(2)}, u32[]{:S(2)}) async-start(f32[8,8,256]{2,1,0:T(8,128)} %get-tuple-element.14), calls=%async_computation | async-start | bytes 131072 | tf_op jit(solution)/shard_map/all_to_all | solution.py:176
  19.8 0.0 collective-permute-done
  19.9 3.2 %collective-permute-start.1 = (bf16[2,32,832]{2,1,0:T(8,128)(2,1)S(1)}, bf16[2,32,832]{2,1,0:T(8,128)(2,1)S(1)}, u32[]{:S(2)}, u32[]{:S(2)}) collective-permute-start(bf16[2,32,832]{2,1,0:T(8,128)(2,1)S(1)} %pad_maximum_fusion.mine), channel_id=1, source_target_pairs={{0,8},{8,0},{1,9},{9,1},{2,10},{10,2},{3,11},{11,3},{4,12},{12,4},... | collective-permute-start | bytes 319496 | tf_op jit(solution)/shard_map/ppermute | solution.py:161
  23.1 0.0 copy-start.6
  23.1 0.1 copy.13.gain
  23.3 0.5 copy-done.6
  23.8 0.1 copy.14.bias
  23.9 3.7 %all-to-all-done.st = f32[8,8,256]{2,1,0:T(8,128)S(1)} async-done(((f32[8,8,256]{2,1,0:T(8,128)}), f32[8,8,256]{2,1,0:T(8,128)S(1)}, u32[]{:S(2)}, u32[]{:S(2)}) %all-to-all-start) | async-done | bytes 65568 | tf_op jit(solution)/shard_map/all_to_all | solution.py:176
  27.6 0.0 collective-permute-done.1._.theirs
  27.7 0.2 shard_map.92.own
  27.9 2.7 %collective-permute-start.2 = (bf16[832,256]{1,0:T(8,128)(2,1)S(1)}, bf16[832,256]{1,0:T(8,128)(2,1)S(1)}, u32[]{:S(2)}, u32[]{:S(2)}) collective-permute-start(bf16[832,256]{1,0:T(8,128)(2,1)S(1)} %shard_map.92.own), channel_id=1, source_target_pairs={{0,256},{1,257},{64,320},{65,321},{256,0},{257,1},{320,64},{321,65... | collective-permute-start | bytes 1277960 | tf_op jit(solution)/shard_map/ppermute | solution.py:181
  30.6 2.6 %collective-permute-start.3 = (bf16[832,256]{1,0:T(8,128)(2,1)S(1)}, bf16[832,256]{1,0:T(8,128)(2,1)S(1)}, u32[]{:S(2)}, u32[]{:S(2)}) collective-permute-start(bf16[832,256]{1,0:T(8,128)(2,1)S(1)} %shard_map.92.own), channel_id=1, source_target_pairs={{0,64},{1,321},{64,0},{65,257},{256,320},{257,65},{320,256},{321,1... | collective-permute-start | bytes 1277960 | tf_op jit(solution)/shard_map/ppermute | solution.py:182
  33.2 3.1 %collective-permute-start.4 = (bf16[832,256]{1,0:T(8,128)(2,1)S(1)}, bf16[832,256]{1,0:T(8,128)(2,1)S(1)}, u32[]{:S(2)}, u32[]{:S(2)}) collective-permute-start(bf16[832,256]{1,0:T(8,128)(2,1)S(1)} %shard_map.92.own), channel_id=1, source_target_pairs={{0,320},{1,65},{64,256},{65,1},{256,64},{257,321},{320,0},{321,257... | collective-permute-start | bytes 1277960 | tf_op jit(solution)/shard_map/ppermute | solution.py:183
  36.3 0.1 pad_add_fusion.ids
  36.3 0.0 copy-done.3
  36.3 0.7 shard_map.93
  37.1 0.0 copy-start
  37.1 17.5 %all-gather = bf16[416,832]{1,0:T(8,128)(2,1)S(1)} all-gather(bf16[104,832]{1,0:T(8,128)(2,1)S(1)} %shard_map.93), channel_id=2, replica_groups=mesh['zl'=2,'xh'=2,'xl'=2,'yh'=4,'yl'=2,'zh'=4,'c'=2] {'yh'}, dimensions={0}, use_global_device_ids=true | all-gather | bytes 865280 | tf_op jit(solution)/shard_map/all_gather | solution.py:168
  54.6 0.0 collective-permute-done.2.rx
  54.6 0.0 collective-permute-done.3.rk
  54.6 0.1 collective-permute-done.4.rs
  54.7 0.0 copy-done
  54.7 1.9 %shard_map.94 = (bf16[4,208,256]{2,1,0:T(8,128)(2,1)S(1)}, bf16[4,208,256]{2,1,0:T(8,128)(2,1)S(1)}) custom-call(s32[1]{0:T(128)} %bitcast.1.ids, bf16[832,256]{1,0:T(8,128)(2,1)S(1)} %shard_map.92.own, bf16[832,256]{1,0:T(8,128)(2,1)S(1)} %collective-permute-done.2.rx, bf16[832,256]{1,0:T(8,128)(2,1)S(1)} %collective-permute-done.3.rk, ...), custom_call_target="tpu_custom_call" | custom-call | tf_op jit(solution)/shard_map/pallas_call | solution.py:191
  56.6 7.7 %collective-permute-start.5 = (bf16[4,208,256]{2,1,0:T(8,128)(2,1)S(1)}, bf16[4,208,256]{2,1,0:T(8,128)(2,1)S(1)}, u32[]{:S(2)}, u32[]{:S(2)}) collective-permute-start(bf16[4,208,256]{2,1,0:T(8,128)(2,1)S(1)} %get-tuple-element.16), channel_id=1, source_target_pairs={{0,1},{1,0},{2,3},{3,2},{4,5},{5,4},{6,7},{7,6},{8,9},{9,8},{10,11... | collective-permute-start | bytes 1277960 | tf_op jit(solution)/shard_map/ppermute | solution.py:200
  64.3 0.0 copy-start.4
  64.3 0.7 copy-done.4
  65.0 0.1 convert_reduce_fusion
  65.1 0.5 collective-permute-done.5.got
  65.7 0.1 shard_map.95
  65.8 2.9 %collective-permute-start.6 = (bf16[208,256]{1,0:T(8,128)(2,1)S(1)}, bf16[208,256]{1,0:T(8,128)(2,1)S(1)}, u32[]{:S(2)}, u32[]{:S(2)}) collective-permute-start(bf16[208,256]{1,0:T(8,128)(2,1)S(1)} %get-tuple-element.17), channel_id=1, source_target_pairs={{0,0},{1,256},{2,2},{3,258},{4,64},{5,320},{6,66},{7,322},{64,65},... | collective-permute-start | bytes 319496 | tf_op jit(solution)/shard_map/ppermute | solution.py:205
  68.7 6.5 %collective-permute-start.7 = (bf16[208,256]{1,0:T(8,128)(2,1)S(1)}, bf16[208,256]{1,0:T(8,128)(2,1)S(1)}, u32[]{:S(2)}, u32[]{:S(2)}) collective-permute-start(bf16[208,256]{1,0:T(8,128)(2,1)S(1)} %get-tuple-element.18), channel_id=1, source_target_pairs={{0,2},{1,258},{2,0},{3,256},{4,66},{5,322},{6,64},{7,320},{64,67},... | collective-permute-start | bytes 319496 | tf_op jit(solution)/shard_map/ppermute | solution.py:205
  75.3 1.9 %collective-permute-start.8 = (bf16[208,256]{1,0:T(8,128)(2,1)S(1)}, bf16[208,256]{1,0:T(8,128)(2,1)S(1)}, u32[]{:S(2)}, u32[]{:S(2)}) collective-permute-start(bf16[208,256]{1,0:T(8,128)(2,1)S(1)} %get-tuple-element.19), channel_id=1, source_target_pairs={{0,64},{1,320},{2,66},{3,322},{4,0},{5,256},{6,2},{7,258},{64,1},{... | collective-permute-start | bytes 319496 | tf_op jit(solution)/shard_map/ppermute | solution.py:205
  77.2 0.0 copy-start.7
  77.2 7.2 %collective-permute-start.9 = (bf16[208,256]{1,0:T(8,128)(2,1)S(1)}, bf16[208,256]{1,0:T(8,128)(2,1)S(1)}, u32[]{:S(2)}, u32[]{:S(2)}) collective-permute-start(bf16[208,256]{1,0:T(8,128)(2,1)S(1)} %get-tuple-element.20), channel_id=1, source_target_pairs={{0,66},{1,322},{2,64},{3,320},{4,2},{5,258},{6,0},{7,256},{64,3},{... | collective-permute-start | bytes 319496 | tf_op jit(solution)/shard_map/ppermute | solution.py:205
  84.5 0.1 copy.15.bias
  84.6 0.0 collective-permute-done.6.z0
  84.7 0.0 collective-permute-done.7.z1
  84.7 0.0 collective-permute-done.8.z2
  84.7 3.4 %collective-permute-done.9.z3 = bf16[208,256]{1,0:T(8,128)(2,1)S(1)} collective-permute-done((bf16[208,256]{1,0:T(8,128)(2,1)S(1)}, bf16[208,256]{1,0:T(8,128)(2,1)S(1)}, u32[]{:S(2)}, u32[]{:S(2)}) %collective-permute-start.9) | collective-permute-done | bytes 106528 | tf_op jit(solution)/shard_map/ppermute | solution.py:205
  88.1 0.6 shard_map.96
  88.7 0.0 copy-start.2
  88.7 22.5 %all_to_all.10.got = bf16[64,24,128]{2,1,0:T(8,128)(2,1)S(1)} all-to-all(bf16[64,24,128]{2,1,0:T(8,128)(2,1)S(1)} %shard_map.96), channel_id=1, replica_groups=mesh['zl'=2,'xh'=2,'xl'=2,'yh'=4,'yl'=2,'zh'=4,'c'=2] {'zl','xh','xl','y..., dimensions={0} | all-to-all | bytes 786432 | tf_op jit(solution)/shard_map/all_to_all | solution.py:226
  111.2 1.6 %shard_map.97 = bf16[208,384]{1,0:T(8,128)(2,1)} custom-call(bf16[64,24,128]{2,1,0:T(8,128)(2,1)S(1)} %all_to_all.10.got, bf16[208,384]{1,0:T(8,128)(2,1)S(1)} %copy-done.2), custom_call_target="tpu_custom_call" | custom-call | tf_op jit(solution)/shard_map/pallas_call | solution.py:227
  (16 shorter events, 0.1 us)
Async XLA Ops:
  0.9 18.9 %collective-permute-start = (bf16[32,832]{1,0:T(8,128)(2,1)S(1)}, bf16[32,832]{1,0:T(8,128)(2,1)S(1)}, u32[]{:S(2)}, u32[]{:S(2)}) collective-permute-start(bf16[32,832]{1,0:T(8,128)(2,1)S(1)} %get-tuple-element.22), channel_id=1, source_target_pairs={{0,128},{128,0},{1,129},{129,1},{2,130},{130,2},{3,131},{131,3},{4... | collective-permute-start | bytes 159752 | tf_op jit(solution)/shard_map/ppermute | solution.py:160
  6.4 1.0 copy-start.1
  8.6 19.1 %all-to-all-start = ((f32[8,8,256]{2,1,0:T(8,128)}), f32[8,8,256]{2,1,0:T(8,128)S(1)}, u32[]{:S(2)}, u32[]{:S(2)}) async-start(f32[8,8,256]{2,1,0:T(8,128)} %get-tuple-element.14), calls=%async_computation | async-start | bytes 131072 | tf_op jit(solution)/shard_map/all_to_all | solution.py:176
  19.8 3.2 %copy-start.5 = (bf16[208]{0:T(256)(128)(2,1)S(1)}, bf16[208]{0:T(256)(128)(2,1)}, u32[]{:S(2)}) copy-start(bf16[208]{0:T(256)(128)(2,1)} %param.10) | copy-start | bytes 1252
  19.9 7.8 %collective-permute-start.1 = (bf16[2,32,832]{2,1,0:T(8,128)(2,1)S(1)}, bf16[2,32,832]{2,1,0:T(8,128)(2,1)S(1)}, u32[]{:S(2)}, u32[]{:S(2)}) collective-permute-start(bf16[2,32,832]{2,1,0:T(8,128)(2,1)S(1)} %pad_maximum_fusion.mine), channel_id=1, source_target_pairs={{0,8},{8,0},{1,9},{9,1},{2,10},{10,2},{3,11},{11,3},{4,12},{12,4},... | collective-permute-start | bytes 319496 | tf_op jit(solution)/shard_map/ppermute | solution.py:161
  23.1 0.7 copy-start.6
  27.6 8.7 %copy-start.3 = (bf16[104,128]{1,0:T(8,128)(2,1)S(1)}, bf16[104,128]{1,0:T(8,128)(2,1)}, u32[]{:S(2)}) copy-start(bf16[104,128]{1,0:T(8,128)(2,1)} %constant.70.clone.pack) | copy-start | bytes 79876
  27.9 26.7 %collective-permute-start.2 = (bf16[832,256]{1,0:T(8,128)(2,1)S(1)}, bf16[832,256]{1,0:T(8,128)(2,1)S(1)}, u32[]{:S(2)}, u32[]{:S(2)}) collective-permute-start(bf16[832,256]{1,0:T(8,128)(2,1)S(1)} %shard_map.92.own), channel_id=1, source_target_pairs={{0,256},{1,257},{64,320},{65,321},{256,0},{257,1},{320,64},{321,65... | collective-permute-start | bytes 1277960 | tf_op jit(solution)/shard_map/ppermute | solution.py:181
  30.6 24.0 %collective-permute-start.3 = (bf16[832,256]{1,0:T(8,128)(2,1)S(1)}, bf16[832,256]{1,0:T(8,128)(2,1)S(1)}, u32[]{:S(2)}, u32[]{:S(2)}) collective-permute-start(bf16[832,256]{1,0:T(8,128)(2,1)S(1)} %shard_map.92.own), channel_id=1, source_target_pairs={{0,64},{1,321},{64,0},{65,257},{256,320},{257,65},{320,256},{321,1... | collective-permute-start | bytes 1277960 | tf_op jit(solution)/shard_map/ppermute | solution.py:182
  33.2 21.5 %collective-permute-start.4 = (bf16[832,256]{1,0:T(8,128)(2,1)S(1)}, bf16[832,256]{1,0:T(8,128)(2,1)S(1)}, u32[]{:S(2)}, u32[]{:S(2)}) collective-permute-start(bf16[832,256]{1,0:T(8,128)(2,1)S(1)} %shard_map.92.own), channel_id=1, source_target_pairs={{0,320},{1,65},{64,256},{65,1},{256,64},{257,321},{320,0},{321,257... | collective-permute-start | bytes 1277960 | tf_op jit(solution)/shard_map/ppermute | solution.py:183
  37.1 17.6 %copy-start = (bf16[2,4,208,104]{3,2,1,0:T(8,128)(2,1)S(1)}, bf16[2,4,208,104]{3,2,1,0:T(8,128)(2,1)}, u32[]{:S(2)}) copy-start(bf16[2,4,208,104]{3,2,1,0:T(8,128)(2,1)} %constant.71.clone.order) | copy-start | bytes 1038340
  56.6 9.0 %collective-permute-start.5 = (bf16[4,208,256]{2,1,0:T(8,128)(2,1)S(1)}, bf16[4,208,256]{2,1,0:T(8,128)(2,1)S(1)}, u32[]{:S(2)}, u32[]{:S(2)}) collective-permute-start(bf16[4,208,256]{2,1,0:T(8,128)(2,1)S(1)} %get-tuple-element.16), channel_id=1, source_target_pairs={{0,1},{1,0},{2,3},{3,2},{4,5},{5,4},{6,7},{7,6},{8,9},{9,8},{10,11... | collective-permute-start | bytes 1277960 | tf_op jit(solution)/shard_map/ppermute | solution.py:200
  64.3 0.7 copy-start.4
  65.8 18.9 %collective-permute-start.6 = (bf16[208,256]{1,0:T(8,128)(2,1)S(1)}, bf16[208,256]{1,0:T(8,128)(2,1)S(1)}, u32[]{:S(2)}, u32[]{:S(2)}) collective-permute-start(bf16[208,256]{1,0:T(8,128)(2,1)S(1)} %get-tuple-element.17), channel_id=1, source_target_pairs={{0,0},{1,256},{2,2},{3,258},{4,64},{5,320},{6,66},{7,322},{64,65},... | collective-permute-start | bytes 319496 | tf_op jit(solution)/shard_map/ppermute | solution.py:205
  68.7 16.0 %collective-permute-start.7 = (bf16[208,256]{1,0:T(8,128)(2,1)S(1)}, bf16[208,256]{1,0:T(8,128)(2,1)S(1)}, u32[]{:S(2)}, u32[]{:S(2)}) collective-permute-start(bf16[208,256]{1,0:T(8,128)(2,1)S(1)} %get-tuple-element.18), channel_id=1, source_target_pairs={{0,2},{1,258},{2,0},{3,256},{4,66},{5,322},{6,64},{7,320},{64,67},... | collective-permute-start | bytes 319496 | tf_op jit(solution)/shard_map/ppermute | solution.py:205
  75.3 9.4 %collective-permute-start.8 = (bf16[208,256]{1,0:T(8,128)(2,1)S(1)}, bf16[208,256]{1,0:T(8,128)(2,1)S(1)}, u32[]{:S(2)}, u32[]{:S(2)}) collective-permute-start(bf16[208,256]{1,0:T(8,128)(2,1)S(1)} %get-tuple-element.19), channel_id=1, source_target_pairs={{0,64},{1,320},{2,66},{3,322},{4,0},{5,256},{6,2},{7,258},{64,1},{... | collective-permute-start | bytes 319496 | tf_op jit(solution)/shard_map/ppermute | solution.py:205
  77.2 7.3 %copy-start.7 = (bf16[208]{0:T(256)(128)(2,1)S(1)}, bf16[208]{0:T(256)(128)(2,1)}, u32[]{:S(2)}) copy-start(bf16[208]{0:T(256)(128)(2,1)} %param.13) | copy-start | bytes 1252
  77.2 10.9 %collective-permute-start.9 = (bf16[208,256]{1,0:T(8,128)(2,1)S(1)}, bf16[208,256]{1,0:T(8,128)(2,1)S(1)}, u32[]{:S(2)}, u32[]{:S(2)}) collective-permute-start(bf16[208,256]{1,0:T(8,128)(2,1)S(1)} %get-tuple-element.20), channel_id=1, source_target_pairs={{0,66},{1,322},{2,64},{3,320},{4,2},{5,258},{6,0},{7,256},{64,3},{... | collective-permute-start | bytes 319496 | tf_op jit(solution)/shard_map/ppermute | solution.py:205
  88.7 22.5 %copy-start.2 = (bf16[208,384]{1,0:T(8,128)(2,1)S(1)}, bf16[208,384]{1,0:T(8,128)(2,1)}, u32[]{:S(2)}) copy-start(bf16[208,384]{1,0:T(8,128)(2,1)} %text.1) | copy-start | bytes 479236

commit v5 on v4

--- a/solution.py
+++ b/solution.py
@@ -25,6 +25,7 @@
 LANES = 128
 SEQ = ("zl", "xh", "xl", "yh", "yl")
 TP = ("zh", "c")
+SHARE = ("zl", "xl")
 BF16 = jnp.bfloat16
 F32 = jnp.float32
 
@@ -73,7 +74,9 @@
     for k in range(GROUP):
         at = pl.ds(k * FEAT, FEAT)
         centered = x_ref[at, :].astype(F32) - mean[k : k + 1]
-        out_ref[at, :] = (centered * scale[k : k + 1] * gain_col + bias_col).astype(BF16)
+        block = (centered * scale[k : k + 1] * gain_col + bias_col).astype(BF16)
+        for t in range(4):
+            out_ref[t, at, :] = block
 
 
 def pack_body(ids, mine, theirs, pack, out_ref):
@@ -86,17 +89,14 @@
     out_ref[...] = jnp.dot(pack[...], rows, preferred_element_type=F32).astype(BF16)
 
 
-def project_body(ids, own, rx, rk, rs, wg, order, keep_ref, send_ref, weight):
-    c = ids[0]
+def project_body(ids, x_ref, wg, order, keep_ref, send_ref, weight):
+    c, q = ids[0], ids[1]
     for g in range(2):
         rows = [jnp.dot(order[g, y], wg[y], preferred_element_type=F32) for y in range(4)]
         weight[g] = ((rows[0] + rows[1]) + (rows[2] + rows[3])).astype(BF16)
     for job in range(4):
         kept, i = job // 2 == 1, job % 2
-        if i == 1:
-            x = (rk if kept else rs)[...]
-        else:
-            x = jnp.where((c == 1) == kept, rx[...], own[...])
+        x = x_ref[q ^ (2 * (c if kept else 1 - c) + i)]
         for g in range(2):
             out = jnp.dot(weight[g], x, preferred_element_type=F32).astype(BF16)
             (keep_ref if kept else send_ref)[2 * i + g] = out
@@ -133,14 +133,12 @@
     side = rows[HALF + 3 : HALF + 4]
     want = lax.broadcasted_iota(jnp.int32, (POS, N_SEQ * SLOTS), 0).astype(F32)
     pick = jnp.where(want == at, 1.0, 0.0).astype(BF16)
-    halves = []
-    for h in range(2):
-        mine = jnp.where(side == float(h), rows, 0.0).astype(BF16)
-        halves.append(
-            lax.dot_general(mine, pick, (((1,), (1,)), ((), ())), preferred_element_type=F32)
-        )
-    hit = halves[0][HALF + 2 : HALF + 3] > 0.5
-    full = jnp.concatenate([halves[0][:HALF], halves[1][:HALF]], axis=0)
+    mine = [jnp.where(side == float(h), rows, 0.0).astype(BF16) for h in range(2)]
+    both = lax.dot_general(
+        jnp.concatenate(mine, axis=0), pick, (((1,), (1,)), ((), ())), preferred_element_type=F32
+    )
+    hit = both[HALF + 2 : HALF + 3] > 0.5
+    full = jnp.concatenate([both[:HALF], both[LANES : LANES + HALF]], axis=0)
     out_ref[...] = jnp.where(hit, full, text[...].astype(F32)).astype(BF16)
 
 
@@ -153,7 +151,7 @@
 
 def shards(patches, ln_gain, ln_bias, merge_weight, merge_bias, targets, text_embed):
     sds = jax.ShapeDtypeStruct
-    xh, yl, zh, c = (lax.axis_index(a) for a in ("xh", "yl", "zh", "c"))
+    zl, xh, xl, yl, zh, c = (lax.axis_index(a) for a in ("zl", "xh", "xl", "yl", "zh", "c"))
 
     chunk = jnp.transpose(merge_weight, (2, 0, 1)).reshape(CHUNK, GROUP * FEAT)
     chunk = jnp.pad(chunk, ((0, CHUNK_PAD - CHUNK), (0, 0)))
@@ -174,28 +172,25 @@
         scratch=[pltpu.VMEM((8, ROWS), F32)],
     )(patches)
     all_stats = lax.all_to_all(stats, TP, 0, 0, tiled=True)
-    own = _call(norm_body, sds((GROUP * FEAT, ROWS), BF16), 5)(
+    copies = _call(norm_body, sds((4, GROUP * FEAT, ROWS), BF16), 5)(
         own, all_stats, ln_gain.astype(F32)[:, None], ln_bias.astype(F32)[:, None], pair_y
     )
-    axes, sizes = ("zl", "xl", "c"), (2, 2, 2)
-    rx = lax.ppermute(own, axes, _pairs(sizes, lambda z, x, k: (z ^ 1, x, k)))
-    rk = lax.ppermute(own, axes, _pairs(sizes, lambda z, x, k: (z ^ k, x ^ 1, k)))
-    rs = lax.ppermute(own, axes, _pairs(sizes, lambda z, x, k: (z ^ k ^ 1, x ^ 1, k)))
+    shared = lax.all_to_all(copies, SHARE, 0, 0, tiled=True)
 
     order = np.zeros((2, 4, FEAT, 4 * CHUNK), np.float32)
     for g in range(2):
         for r in range(FEAT):
             order[g, r // (2 * CHUNK), r, g * 2 * CHUNK + r % (2 * CHUNK)] = 1.0
-    ids = c[None].astype(jnp.int32)
+    ids = jnp.stack([c, 2 * zl + xl]).astype(jnp.int32)
     piece = sds((4, FEAT, ROWS), BF16)
     keep, send = pl.pallas_call(
         project_body,
         out_shape=(piece, piece),
-        in_specs=[pl.BlockSpec(memory_space=pltpu.SMEM)] + _vmem(6),
+        in_specs=[pl.BlockSpec(memory_space=pltpu.SMEM)] + _vmem(3),
         out_specs=tuple(_vmem(2)),
         scratch_shapes=[pltpu.VMEM((2, FEAT, GROUP * FEAT), BF16)],
         compiler_params=pltpu.CompilerParams(vmem_limit_bytes=48 << 20),
-    )(ids, own, rx, rk, rs, columns, jnp.asarray(order, BF16))
+    )(ids, shared, columns, jnp.asarray(order, BF16))
 
     got = lax.ppermute(send, "c", [(0, 1), (1, 0)])
     part = sds((FEAT, ROWS), BF16)
@@ -207,7 +202,7 @@
             axes,
             _pairs(sizes, lambda z, x, h, k2, k=k: (z ^ k2, x ^ ((h ^ k) >> 1), 2 * z + ((h ^ k) & 1), x)),
         )
-        for k in range(4)
+        for k in (2, 3, 1, 0)
     ]
 
     target_dev = targets // POS

time: 113 us -> 110 us (0.973)
  the two profiles are of different devices: /device:TPU:1 before, /device:TPU:8 now
where the time goes in v5:
time: 110 us; the launch traced here: 109 us
  blocking collectives  52.6 us (48%)
  starting transfers between devices  33.9 us (31%)
  waiting for transfers between devices  10.2 us (9%)
  Pallas kernels  8.5 us (8%)
  local copies, waits for them, and re-layouts  2.36 us (2%)
  other arithmetic  1.64 us (1%)
    all_to_all x1, blocking collectives, shards(): rows = lax.all_to_all(sent, SEQ, 0, 0, tiled=True)  31.3 us
    all_gather x1, blocking collectives, shards(): columns = lax.all_gather(quad, 'yh')  21.3 us
    ppermute x4, starting transfers between devices, shards(): lax.ppermute(parts[k], axes, _pairs(sizes, lambda z, x, h, k2, k=k: (z ^...  10.5 us
    all_to_all x1, starting transfers between devices, shards(): all_stats = lax.all_to_all(stats, TP, 0, 0, tiled=True)  10.3 us
    ppermute x1, starting transfers between devices, shards(): pair = jnp.stack([chunk, lax.ppermute(chunk, 'xh', [(0, 1), (1, 0)])])  4.93 us
    all_to_all x1, waiting for transfers between devices, shards(): all_stats = lax.all_to_all(stats, TP, 0, 0, tiled=True)  4.59 us
    ppermute x4, waiting for transfers between devices, shards(): lax.ppermute(parts[k], axes, _pairs(sizes, lambda z, x, h, k2, k=k: (z ^...  3.82 us
    all_to_all x1, starting transfers between devices, shards(): shared = lax.all_to_all(copies, SHARE, 0, 0, tiled=True)  3.7 us
  transfers between devices with their start and end apart: 9, of which 5 were waited for; matrix products, arithmetic and copies ran while one was open for 2% of the time, Pallas kernels for 2%

profile of v5, /device:TPU:8, one launch (start us, length us, event | category | flops | bytes accessed | tf_op | source)
XLA Modules:
  0.0 109.4 jit_solution(4603930486495567387)
XLA Ops:
  0.0 0.9 reshape.5
  0.9 4.9 %collective-permute-start = (bf16[32,832]{1,0:T(8,128)(2,1)S(1)}, bf16[32,832]{1,0:T(8,128)(2,1)S(1)}, u32[]{:S(2)}, u32[]{:S(2)}) collective-permute-start(bf16[32,832]{1,0:T(8,128)(2,1)S(1)} %get-tuple-element.22), channel_id=1, source_target_pairs={{0,128},{128,0},{1,129},{129,1},{2,130},{130,2},{3,131},{131,3},{4... | collective-permute-start | bytes 159752 | tf_op jit(solution)/shard_map/ppermute | solution.py:158
  5.9 0.0 copy-start.1
  5.9 1.0 copy-done.1
  6.9 1.1 %shard_map.91 = (bf16[832,256]{1,0:T(8,128)(2,1)S(1)}, f32[8,8,256]{2,1,0:T(8,128)}) custom-call(bf16[208,1024]{1,0:T(8,128)(2,1)S(1)} %copy-done.1), custom_call_target="tpu_custom_call" | custom-call | tf_op jit(solution)/shard_map/pallas_call | solution.py:168
  8.0 10.3 %all-to-all-start = ((f32[8,8,256]{2,1,0:T(8,128)}), f32[8,8,256]{2,1,0:T(8,128)S(1)}, u32[]{:S(2)}, u32[]{:S(2)}) async-start(f32[8,8,256]{2,1,0:T(8,128)} %get-tuple-element.14), calls=%async_computation | async-start | bytes 131072 | tf_op jit(solution)/shard_map/all_to_all | solution.py:174
  18.3 0.0 collective-permute-done
  18.4 2.4 %collective-permute-start.1 = (bf16[2,32,832]{2,1,0:T(8,128)(2,1)S(1)}, bf16[2,32,832]{2,1,0:T(8,128)(2,1)S(1)}, u32[]{:S(2)}, u32[]{:S(2)}) collective-permute-start(bf16[2,32,832]{2,1,0:T(8,128)(2,1)S(1)} %pad_maximum_fusion.mine), channel_id=1, source_target_pairs={{0,8},{8,0},{1,9},{9,1},{2,10},{10,2},{3,11},{11,3},{4,12},{12,4},... | collective-permute-start | bytes 319496 | tf_op jit(solution)/shard_map/ppermute | solution.py:159
  20.7 0.7 broadcast_in_dim.33
  21.4 0.1 copy.13.gain
  21.5 0.7 broadcast_in_dim.34
  22.2 0.1 copy.14.bias
  22.3 4.6 %all-to-all-done.st = f32[8,8,256]{2,1,0:T(8,128)S(1)} async-done(((f32[8,8,256]{2,1,0:T(8,128)}), f32[8,8,256]{2,1,0:T(8,128)S(1)}, u32[]{:S(2)}, u32[]{:S(2)}) %all-to-all-start) | async-done | bytes 65568 | tf_op jit(solution)/shard_map/all_to_all | solution.py:174
  26.9 0.0 collective-permute-done.1._.theirs
  26.9 1.5 %shard_map.92 = bf16[4,832,256]{2,1,0:T(8,128)(2,1)} custom-call(bf16[832,256]{1,0:T(8,128)(2,1)S(1)} %get-tuple-element.13.x_ref, f32[8,8,256]{2,1,0:T(8,128)S(1)} %all-to-all-done.st, f32[208,1]{1,0:T(8,128)S(1)} %copy.13.gain, f32[208,1]{1,0:T(8,128)S(1)} %copy.14.bias, bf16[2,32,832]{2,1,0:T(8,128)(2,1)S(1)} %collective-permute-done.1._.theirs), custom_call_target="tpu_custom_call" | custom-call | tf_op jit(solution)/shard_map/pallas_call | solution.py:175
  28.4 0.0 copy-start.3
  28.4 0.0 copy-start
  28.4 3.7 %all-to-all-start.1 = ((bf16[4,832,256]{2,1,0:T(8,128)(2,1)}), bf16[4,832,256]{2,1,0:T(8,128)(2,1)S(1)}, u32[]{:S(2)}, u32[]{:S(2)}) async-start(bf16[4,832,256]{2,1,0:T(8,128)(2,1)} %shard_map.92), calls=%async_computation.1 | async-start | bytes 3407872 | tf_op jit(solution)/shard_map/all_to_all | solution.py:178
  32.1 0.1 pad_add_fusion.ids
  32.2 0.1 pad_add_fusion.1.ids
  32.3 0.0 copy-done.3
  32.3 0.7 shard_map.93
  33.1 0.0 copy-start.4
  33.1 21.3 %all-gather = bf16[416,832]{1,0:T(8,128)(2,1)S(1)} all-gather(bf16[104,832]{1,0:T(8,128)(2,1)S(1)} %shard_map.93), channel_id=2, replica_groups=mesh['zl'=2,'xh'=2,'xl'=2,'yh'=4,'yl'=2,'zh'=4,'c'=2] {'yh'}, dimensions={0}, use_global_device_ids=true | all-gather | bytes 865280 | tf_op jit(solution)/shard_map/all_gather | solution.py:166
  54.4 0.0 all-to-all-done.1.x_ref
  54.4 0.0 copy-done
  54.4 0.0 copy-start.5
  54.4 3.0 %shard_map.94 = (bf16[4,208,256]{2,1,0:T(8,128)(2,1)S(1)}, bf16[4,208,256]{2,1,0:T(8,128)(2,1)}) custom-call(s32[2]{0:T(128)S(1)} %pad_add_fusion.ids, bf16[4,832,256]{2,1,0:T(8,128)(2,1)S(1)} %all-to-all-done.1.x_ref, bf16[4,104,832]{2,1,0:T(8,128)(2,1)S(1)} %bitcast.16, bf16[2,4,208,104]{3,2,1,0:T(8,128)(2,1)S(1)} %copy-done), custom_call_target="tpu_custom_call" | custom-call | tf_op jit(solution)/shard_map/pallas_call | solution.py:186
  57.4 0.0 copy-start.2
  57.4 2.0 %collective-permute-start.2 = (bf16[4,208,256]{2,1,0:T(8,128)(2,1)}, bf16[4,208,256]{2,1,0:T(8,128)(2,1)S(1)}, u32[]{:S(2)}, u32[]{:S(2)}) collective-permute-start(bf16[4,208,256]{2,1,0:T(8,128)(2,1)} %get-tuple-element.16), channel_id=1, source_target_pairs={{0,1},{1,0},{2,3},{3,2},{4,5},{5,4},{6,7},{7,6},{8,9},{9,8},{10,11... | collective-permute-start | bytes 1277960 | tf_op jit(solution)/shard_map/ppermute | solution.py:195
  59.5 0.0 copy-done.4
  59.5 0.1 convert_reduce_fusion
  59.6 1.8 %collective-permute-done.2.got = bf16[4,208,256]{2,1,0:T(8,128)(2,1)S(1)} collective-permute-done((bf16[4,208,256]{2,1,0:T(8,128)(2,1)}, bf16[4,208,256]{2,1,0:T(8,128)(2,1)S(1)}, u32[]{:S(2)}, u32[]{:S(2)}) %collective-permute-start.2) | collective-permute-done | bytes 426016 | tf_op jit(solution)/shard_map/ppermute | solution.py:195
  61.4 0.1 shard_map.95
  61.5 2.8 %collective-permute-start.3 = (bf16[208,256]{1,0:T(8,128)(2,1)S(1)}, bf16[208,256]{1,0:T(8,128)(2,1)S(1)}, u32[]{:S(2)}, u32[]{:S(2)}) collective-permute-start(bf16[208,256]{1,0:T(8,128)(2,1)S(1)} %get-tuple-element.17), channel_id=1, source_target_pairs={{0,64},{1,320},{2,66},{3,322},{4,0},{5,256},{6,2},{7,258},{64,1},{... | collective-permute-start | bytes 319496 | tf_op jit(solution)/shard_map/ppermute | solution.py:200
  64.3 2.4 %collective-permute-start.4 = (bf16[208,256]{1,0:T(8,128)(2,1)S(1)}, bf16[208,256]{1,0:T(8,128)(2,1)S(1)}, u32[]{:S(2)}, u32[]{:S(2)}) collective-permute-start(bf16[208,256]{1,0:T(8,128)(2,1)S(1)} %get-tuple-element.18), channel_id=1, source_target_pairs={{0,66},{1,322},{2,64},{3,320},{4,2},{5,258},{6,0},{7,256},{64,3},{... | collective-permute-start | bytes 319496 | tf_op jit(solution)/shard_map/ppermute | solution.py:200
  66.7 4.6 %collective-permute-start.5 = (bf16[208,256]{1,0:T(8,128)(2,1)S(1)}, bf16[208,256]{1,0:T(8,128)(2,1)S(1)}, u32[]{:S(2)}, u32[]{:S(2)}) collective-permute-start(bf16[208,256]{1,0:T(8,128)(2,1)S(1)} %get-tuple-element.19), channel_id=1, source_target_pairs={{0,2},{1,258},{2,0},{3,256},{4,66},{5,322},{6,64},{7,320},{64,67},... | collective-permute-start | bytes 319496 | tf_op jit(solution)/shard_map/ppermute | solution.py:200
  71.4 0.7 collective-permute-start.6
  72.1 0.0 copy-done.5
  72.1 0.1 copy.15.bias
  72.3 1.1 collective-permute-done.3.z0
  73.3 0.1 collective-permute-done.4.z1
  73.5 2.6 %collective-permute-done.5.z2 = bf16[208,256]{1,0:T(8,128)(2,1)S(1)} collective-permute-done((bf16[208,256]{1,0:T(8,128)(2,1)S(1)}, bf16[208,256]{1,0:T(8,128)(2,1)S(1)}, u32[]{:S(2)}, u32[]{:S(2)}) %collective-permute-start.5) | collective-permute-done | bytes 106528 | tf_op jit(solution)/shard_map/ppermute | solution.py:200
  76.1 0.0 collective-permute-done.6.z3
  76.1 0.6 shard_map.96
  76.7 31.3 %all_to_all.15.got = bf16[64,24,128]{2,1,0:T(8,128)(2,1)S(1)} all-to-all(bf16[64,24,128]{2,1,0:T(8,128)(2,1)S(1)} %shard_map.96), channel_id=1, replica_groups=mesh['zl'=2,'xh'=2,'xl'=2,'yh'=4,'yl'=2,'zh'=4,'c'=2] {'zl','xh','xl','y..., dimensions={0} | all-to-all | bytes 786432 | tf_op jit(solution)/shard_map/all_to_all | solution.py:221
  108.0 0.0 copy-done.2
  108.0 1.4 %shard_map.97 = bf16[208,384]{1,0:T(8,128)(2,1)} custom-call(bf16[64,24,128]{2,1,0:T(8,128)(2,1)S(1)} %all_to_all.15.got, bf16[208,384]{1,0:T(8,128)(2,1)S(1)} %copy-done.2), custom_call_target="tpu_custom_call" | custom-call | tf_op jit(solution)/shard_map/pallas_call | solution.py:222
  (9 shorter events, 0.1 us)
Async XLA Ops:
  0.9 17.4 %collective-permute-start = (bf16[32,832]{1,0:T(8,128)(2,1)S(1)}, bf16[32,832]{1,0:T(8,128)(2,1)S(1)}, u32[]{:S(2)}, u32[]{:S(2)}) collective-permute-start(bf16[32,832]{1,0:T(8,128)(2,1)S(1)} %get-tuple-element.22), channel_id=1, source_target_pairs={{0,128},{128,0},{1,129},{129,1},{2,130},{130,2},{3,131},{131,3},{4... | collective-permute-start | bytes 159752 | tf_op jit(solution)/shard_map/ppermute | solution.py:158
  5.9 1.0 copy-start.1
  8.0 18.9 %all-to-all-start = ((f32[8,8,256]{2,1,0:T(8,128)}), f32[8,8,256]{2,1,0:T(8,128)S(1)}, u32[]{:S(2)}, u32[]{:S(2)}) async-start(f32[8,8,256]{2,1,0:T(8,128)} %get-tuple-element.14), calls=%async_computation | async-start | bytes 131072 | tf_op jit(solution)/shard_map/all_to_all | solution.py:174
  18.4 8.5 %collective-permute-start.1 = (bf16[2,32,832]{2,1,0:T(8,128)(2,1)S(1)}, bf16[2,32,832]{2,1,0:T(8,128)(2,1)S(1)}, u32[]{:S(2)}, u32[]{:S(2)}) collective-permute-start(bf16[2,32,832]{2,1,0:T(8,128)(2,1)S(1)} %pad_maximum_fusion.mine), channel_id=1, source_target_pairs={{0,8},{8,0},{1,9},{9,1},{2,10},{10,2},{3,11},{11,3},{4,12},{12,4},... | collective-permute-start | bytes 319496 | tf_op jit(solution)/shard_map/ppermute | solution.py:159
  28.4 3.9 %copy-start.3 = (bf16[104,128]{1,0:T(8,128)(2,1)S(1)}, bf16[104,128]{1,0:T(8,128)(2,1)}, u32[]{:S(2)}) copy-start(bf16[104,128]{1,0:T(8,128)(2,1)} %constant.80.clone.pack) | copy-start | bytes 79876
  28.4 26.0 %copy-start = (bf16[2,4,208,104]{3,2,1,0:T(8,128)(2,1)S(1)}, bf16[2,4,208,104]{3,2,1,0:T(8,128)(2,1)}, u32[]{:S(2)}) copy-start(bf16[2,4,208,104]{3,2,1,0:T(8,128)(2,1)} %constant.81.clone.order) | copy-start | bytes 1038340
  28.4 26.0 %all-to-all-start.1 = ((bf16[4,832,256]{2,1,0:T(8,128)(2,1)}), bf16[4,832,256]{2,1,0:T(8,128)(2,1)S(1)}, u32[]{:S(2)}, u32[]{:S(2)}) async-start(bf16[4,832,256]{2,1,0:T(8,128)(2,1)} %shard_map.92), calls=%async_computation.1 | async-start | bytes 3407872 | tf_op jit(solution)/shard_map/all_to_all | solution.py:178
  33.1 26.4 %copy-start.4 = (s32[256]{0:T(256)S(1)}, s32[256]{0:T(256)}, u32[]{:S(2)}) copy-start(s32[256]{0:T(256)} %param.14) | copy-start | bytes 3076
  54.4 17.7 %copy-start.5 = (bf16[208]{0:T(256)(128)(2,1)S(1)}, bf16[208]{0:T(256)(128)(2,1)}, u32[]{:S(2)}) copy-start(bf16[208]{0:T(256)(128)(2,1)} %param.13) | copy-start | bytes 1252
  57.4 50.6 %copy-start.2 = (bf16[208,384]{1,0:T(8,128)(2,1)S(1)}, bf16[208,384]{1,0:T(8,128)(2,1)}, u32[]{:S(2)}) copy-start(bf16[208,384]{1,0:T(8,128)(2,1)} %text.1) | copy-start | bytes 479236
  57.4 4.0 %collective-permute-start.2 = (bf16[4,208,256]{2,1,0:T(8,128)(2,1)}, bf16[4,208,256]{2,1,0:T(8,128)(2,1)S(1)}, u32[]{:S(2)}, u32[]{:S(2)}) collective-permute-start(bf16[4,208,256]{2,1,0:T(8,128)(2,1)} %get-tuple-element.16), channel_id=1, source_target_pairs={{0,1},{1,0},{2,3},{3,2},{4,5},{5,4},{6,7},{7,6},{8,9},{9,8},{10,11... | collective-permute-start | bytes 1277960 | tf_op jit(solution)/shard_map/ppermute | solution.py:195
  61.5 11.8 %collective-permute-start.3 = (bf16[208,256]{1,0:T(8,128)(2,1)S(1)}, bf16[208,256]{1,0:T(8,128)(2,1)S(1)}, u32[]{:S(2)}, u32[]{:S(2)}) collective-permute-start(bf16[208,256]{1,0:T(8,128)(2,1)S(1)} %get-tuple-element.17), channel_id=1, source_target_pairs={{0,64},{1,320},{2,66},{3,322},{4,0},{5,256},{6,2},{7,258},{64,1},{... | collective-permute-start | bytes 319496 | tf_op jit(solution)/shard_map/ppermute | solution.py:200
  64.3 9.2 %collective-permute-start.4 = (bf16[208,256]{1,0:T(8,128)(2,1)S(1)}, bf16[208,256]{1,0:T(8,128)(2,1)S(1)}, u32[]{:S(2)}, u32[]{:S(2)}) collective-permute-start(bf16[208,256]{1,0:T(8,128)(2,1)S(1)} %get-tuple-element.18), channel_id=1, source_target_pairs={{0,66},{1,322},{2,64},{3,320},{4,2},{5,258},{6,0},{7,256},{64,3},{... | collective-permute-start | bytes 319496 | tf_op jit(solution)/shard_map/ppermute | solution.py:200
  66.7 9.4 %collective-permute-start.5 = (bf16[208,256]{1,0:T(8,128)(2,1)S(1)}, bf16[208,256]{1,0:T(8,128)(2,1)S(1)}, u32[]{:S(2)}, u32[]{:S(2)}) collective-permute-start(bf16[208,256]{1,0:T(8,128)(2,1)S(1)} %get-tuple-element.19), channel_id=1, source_target_pairs={{0,2},{1,258},{2,0},{3,256},{4,66},{5,322},{6,64},{7,320},{64,67},... | collective-permute-start | bytes 319496 | tf_op jit(solution)/shard_map/ppermute | solution.py:200
  71.4 4.7 %collective-permute-start.6 = (bf16[208,256]{1,0:T(8,128)(2,1)S(1)}, bf16[208,256]{1,0:T(8,128)(2,1)S(1)}, u32[]{:S(2)}, u32[]{:S(2)}) collective-permute-start(bf16[208,256]{1,0:T(8,128)(2,1)S(1)} %get-tuple-element.20), channel_id=1, source_target_pairs={{0,0},{1,256},{2,2},{3,258},{4,64},{5,320},{6,66},{7,322},{64,65},... | collective-permute-start | bytes 319496 | tf_op jit(solution)/shard_map/ppermute | solution.py:200

commit v6 on v5

--- a/solution.py
+++ b/solution.py
@@ -63,7 +63,7 @@
         st_ref[t] = part[...]
 
 
-def norm_body(x_ref, st, gain, bias, _, out_ref):
+def norm_body(x_ref, st, gain, bias, _, out_ref, held, sem):
     gain_col = jnp.broadcast_to(gain[...], (FEAT, ROWS))
     bias_col = jnp.broadcast_to(bias[...], (FEAT, ROWS))
     parts = st[...]
@@ -71,12 +71,17 @@
     off = parts[:, :GROUP] - mean[None]
     var = (jnp.sum(parts[:, GROUP:], axis=0) + FEAT * jnp.sum(off * off, axis=0)) * (1.0 / D)
     scale = lax.rsqrt(var + 1e-06)
+    copies = []
     for k in range(GROUP):
         at = pl.ds(k * FEAT, FEAT)
         centered = x_ref[at, :].astype(F32) - mean[k : k + 1]
-        block = (centered * scale[k : k + 1] * gain_col + bias_col).astype(BF16)
+        held[at, :] = (centered * scale[k : k + 1] * gain_col + bias_col).astype(BF16)
         for t in range(4):
-            out_ref[t, at, :] = block
+            copy = pltpu.make_async_copy(held.at[at, :], out_ref.at[t, at, :], sem.at[k, t])
+            copy.start()
+            copies.append(copy)
+    for copy in copies:
+        copy.wait()
 
 
 def pack_body(ids, mine, theirs, pack, out_ref):
@@ -172,9 +177,17 @@
         scratch=[pltpu.VMEM((8, ROWS), F32)],
     )(patches)
     all_stats = lax.all_to_all(stats, TP, 0, 0, tiled=True)
-    copies = _call(norm_body, sds((4, GROUP * FEAT, ROWS), BF16), 5)(
-        own, all_stats, ln_gain.astype(F32)[:, None], ln_bias.astype(F32)[:, None], pair_y
-    )
+    copies = pl.pallas_call(
+        norm_body,
+        out_shape=sds((4, GROUP * FEAT, ROWS), BF16),
+        in_specs=_vmem(5),
+        out_specs=pl.BlockSpec(memory_space=pltpu.HBM),
+        scratch_shapes=[
+            pltpu.VMEM((GROUP * FEAT, ROWS), BF16),
+            pltpu.SemaphoreType.DMA((GROUP, 4)),
+        ],
+        compiler_params=pltpu.CompilerParams(vmem_limit_bytes=48 << 20),
+    )(own, all_stats, ln_gain.astype(F32)[:, None], ln_bias.astype(F32)[:, None], pair_y)
     shared = lax.all_to_all(copies, SHARE, 0, 0, tiled=True)
 
     order = np.zeros((2, 4, FEAT, 4 * CHUNK), np.float32)

time: 110 us -> 110 us (level)
  no operation moved by 1% of the time
where the time goes in v6:
time: 110 us; the launch traced here: 109 us
  blocking collectives  52.6 us (48%)
  starting transfers between devices  33.9 us (31%)
  waiting for transfers between devices  10.2 us (9%)
  Pallas kernels  8.53 us (8%)
  local copies, waits for them, and re-layouts  2.36 us (2%)
  other arithmetic  1.64 us (1%)
    all_to_all x1, blocking collectives, shards(): rows = lax.all_to_all(sent, SEQ, 0, 0, tiled=True)  31.3 us
    all_gather x1, blocking collectives, shards(): columns = lax.all_gather(quad, 'yh')  21.3 us
    ppermute x4, starting transfers between devices, shards(): lax.ppermute(parts[k], axes, _pairs(sizes, lambda z, x, h, k2, k=k: (z ^...  10.5 us
    all_to_all x1, starting transfers between devices, shards(): all_stats = lax.all_to_all(stats, TP, 0, 0, tiled=True)  10.3 us
    ppermute x1, starting transfers between devices, shards(): pair = jnp.stack([chunk, lax.ppermute(chunk, 'xh', [(0, 1), (1, 0)])])  4.93 us
    all_to_all x1, waiting for transfers between devices, shards(): all_stats = lax.all_to_all(stats, TP, 0, 0, tiled=True)  4.59 us
    ppermute x4, waiting for transfers between devices, shards(): lax.ppermute(parts[k], axes, _pairs(sizes, lambda z, x, h, k2, k=k: (z ^...  3.78 us
    all_to_all x1, starting transfers between devices, shards(): shared = lax.all_to_all(copies, SHARE, 0, 0, tiled=True)  3.72 us
  transfers between devices with their start and end apart: 9, of which 5 were waited for; matrix products, arithmetic and copies ran while one was open for 2% of the time, Pallas kernels for 2%

profile of v6, /device:TPU:8, one launch (start us, length us, event | category | flops | bytes accessed | tf_op | source)
XLA Modules:
  0.0 109.4 jit_solution(13728653700040215878)
XLA Ops:
  0.0 0.9 reshape.5
  0.9 4.9 %collective-permute-start = (bf16[32,832]{1,0:T(8,128)(2,1)S(1)}, bf16[32,832]{1,0:T(8,128)(2,1)S(1)}, u32[]{:S(2)}, u32[]{:S(2)}) collective-permute-start(bf16[32,832]{1,0:T(8,128)(2,1)S(1)} %get-tuple-element.22), channel_id=1, source_target_pairs={{0,128},{128,0},{1,129},{129,1},{2,130},{130,2},{3,131},{131,3},{4... | collective-permute-start | bytes 159752 | tf_op jit(solution)/shard_map/ppermute | solution.py:163
  5.9 0.0 copy-start.1
  5.9 1.0 copy-done.1
  6.9 1.1 %shard_map.91 = (bf16[832,256]{1,0:T(8,128)(2,1)S(1)}, f32[8,8,256]{2,1,0:T(8,128)}) custom-call(bf16[208,1024]{1,0:T(8,128)(2,1)S(1)} %copy-done.1), custom_call_target="tpu_custom_call" | custom-call | tf_op jit(solution)/shard_map/pallas_call | solution.py:173
  8.0 10.3 %all-to-all-start = ((f32[8,8,256]{2,1,0:T(8,128)}), f32[8,8,256]{2,1,0:T(8,128)S(1)}, u32[]{:S(2)}, u32[]{:S(2)}) async-start(f32[8,8,256]{2,1,0:T(8,128)} %get-tuple-element.14), calls=%async_computation | async-start | bytes 131072 | tf_op jit(solution)/shard_map/all_to_all | solution.py:179
  18.3 0.0 collective-permute-done
  18.4 2.4 %collective-permute-start.1 = (bf16[2,32,832]{2,1,0:T(8,128)(2,1)S(1)}, bf16[2,32,832]{2,1,0:T(8,128)(2,1)S(1)}, u32[]{:S(2)}, u32[]{:S(2)}) collective-permute-start(bf16[2,32,832]{2,1,0:T(8,128)(2,1)S(1)} %pad_maximum_fusion.mine), channel_id=1, source_target_pairs={{0,8},{8,0},{1,9},{9,1},{2,10},{10,2},{3,11},{11,3},{4,12},{12,4},... | collective-permute-start | bytes 319496 | tf_op jit(solution)/shard_map/ppermute | solution.py:164
  20.7 0.7 broadcast_in_dim.33
  21.4 0.1 copy.13.gain
  21.5 0.7 broadcast_in_dim.34
  22.2 0.1 copy.14.bias
  22.3 4.6 %all-to-all-done.st = f32[8,8,256]{2,1,0:T(8,128)S(1)} async-done(((f32[8,8,256]{2,1,0:T(8,128)}), f32[8,8,256]{2,1,0:T(8,128)S(1)}, u32[]{:S(2)}, u32[]{:S(2)}) %all-to-all-start) | async-done | bytes 65568 | tf_op jit(solution)/shard_map/all_to_all | solution.py:179
  26.9 0.0 collective-permute-done.1._.theirs
  26.9 1.5 %shard_map.92 = bf16[4,832,256]{2,1,0:T(8,128)(2,1)} custom-call(bf16[832,256]{1,0:T(8,128)(2,1)S(1)} %get-tuple-element.13.x_ref, f32[8,8,256]{2,1,0:T(8,128)S(1)} %all-to-all-done.st, f32[208,1]{1,0:T(8,128)S(1)} %copy.13.gain, f32[208,1]{1,0:T(8,128)S(1)} %copy.14.bias, bf16[2,32,832]{2,1,0:T(8,128)(2,1)S(1)} %collective-permute-done.1._.theirs), custom_call_target="tpu_custom_call" | custom-call | tf_op jit(solution)/shard_map/pallas_call | solution.py:180
  28.5 0.0 copy-start.3
  28.5 0.0 copy-start
  28.5 3.7 %all-to-all-start.1 = ((bf16[4,832,256]{2,1,0:T(8,128)(2,1)}), bf16[4,832,256]{2,1,0:T(8,128)(2,1)S(1)}, u32[]{:S(2)}, u32[]{:S(2)}) async-start(bf16[4,832,256]{2,1,0:T(8,128)(2,1)} %shard_map.92), calls=%async_computation.1 | async-start | bytes 3407872 | tf_op jit(solution)/shard_map/all_to_all | solution.py:191
  32.2 0.1 pad_add_fusion.ids
  32.3 0.1 pad_add_fusion.1.ids
  32.4 0.0 copy-done.3
  32.4 0.8 shard_map.93
  33.1 0.0 copy-start.4
  33.2 21.3 %all-gather = bf16[416,832]{1,0:T(8,128)(2,1)S(1)} all-gather(bf16[104,832]{1,0:T(8,128)(2,1)S(1)} %shard_map.93), channel_id=2, replica_groups=mesh['zl'=2,'xh'=2,'xl'=2,'yh'=4,'yl'=2,'zh'=4,'c'=2] {'yh'}, dimensions={0}, use_global_device_ids=true | all-gather | bytes 865280 | tf_op jit(solution)/shard_map/all_gather | solution.py:171
  54.5 0.0 all-to-all-done.1.x_ref
  54.5 0.0 copy-done
  54.5 0.0 copy-start.5
  54.5 3.0 %shard_map.94 = (bf16[4,208,256]{2,1,0:T(8,128)(2,1)S(1)}, bf16[4,208,256]{2,1,0:T(8,128)(2,1)}) custom-call(s32[2]{0:T(128)S(1)} %pad_add_fusion.ids, bf16[4,832,256]{2,1,0:T(8,128)(2,1)S(1)} %all-to-all-done.1.x_ref, bf16[4,104,832]{2,1,0:T(8,128)(2,1)S(1)} %bitcast.16, bf16[2,4,208,104]{3,2,1,0:T(8,128)(2,1)S(1)} %copy-done), custom_call_target="tpu_custom_call" | custom-call | tf_op jit(solution)/shard_map/pallas_call | solution.py:199
  57.5 0.0 copy-start.2
  57.5 2.0 %collective-permute-start.2 = (bf16[4,208,256]{2,1,0:T(8,128)(2,1)}, bf16[4,208,256]{2,1,0:T(8,128)(2,1)S(1)}, u32[]{:S(2)}, u32[]{:S(2)}) collective-permute-start(bf16[4,208,256]{2,1,0:T(8,128)(2,1)} %get-tuple-element.16), channel_id=1, source_target_pairs={{0,1},{1,0},{2,3},{3,2},{4,5},{5,4},{6,7},{7,6},{8,9},{9,8},{10,11... | collective-permute-start | bytes 1277960 | tf_op jit(solution)/shard_map/ppermute | solution.py:208
  59.5 0.0 copy-done.4
  59.6 0.1 convert_reduce_fusion
  59.7 1.8 %collective-permute-done.2.got = bf16[4,208,256]{2,1,0:T(8,128)(2,1)S(1)} collective-permute-done((bf16[4,208,256]{2,1,0:T(8,128)(2,1)}, bf16[4,208,256]{2,1,0:T(8,128)(2,1)S(1)}, u32[]{:S(2)}, u32[]{:S(2)}) %collective-permute-start.2) | collective-permute-done | bytes 426016 | tf_op jit(solution)/shard_map/ppermute | solution.py:208
  61.5 0.1 shard_map.95
  61.6 2.8 %collective-permute-start.3 = (bf16[208,256]{1,0:T(8,128)(2,1)S(1)}, bf16[208,256]{1,0:T(8,128)(2,1)S(1)}, u32[]{:S(2)}, u32[]{:S(2)}) collective-permute-start(bf16[208,256]{1,0:T(8,128)(2,1)S(1)} %get-tuple-element.17), channel_id=1, source_target_pairs={{0,64},{1,320},{2,66},{3,322},{4,0},{5,256},{6,2},{7,258},{64,1},{... | collective-permute-start | bytes 319496 | tf_op jit(solution)/shard_map/ppermute | solution.py:213
  64.4 2.4 %collective-permute-start.4 = (bf16[208,256]{1,0:T(8,128)(2,1)S(1)}, bf16[208,256]{1,0:T(8,128)(2,1)S(1)}, u32[]{:S(2)}, u32[]{:S(2)}) collective-permute-start(bf16[208,256]{1,0:T(8,128)(2,1)S(1)} %get-tuple-element.18), channel_id=1, source_target_pairs={{0,66},{1,322},{2,64},{3,320},{4,2},{5,258},{6,0},{7,256},{64,3},{... | collective-permute-start | bytes 319496 | tf_op jit(solution)/shard_map/ppermute | solution.py:213
  66.8 4.6 %collective-permute-start.5 = (bf16[208,256]{1,0:T(8,128)(2,1)S(1)}, bf16[208,256]{1,0:T(8,128)(2,1)S(1)}, u32[]{:S(2)}, u32[]{:S(2)}) collective-permute-start(bf16[208,256]{1,0:T(8,128)(2,1)S(1)} %get-tuple-element.19), channel_id=1, source_target_pairs={{0,2},{1,258},{2,0},{3,256},{4,66},{5,322},{6,64},{7,320},{64,67},... | collective-permute-start | bytes 319496 | tf_op jit(solution)/shard_map/ppermute | solution.py:213
  71.5 0.7 collective-permute-start.6
  72.1 0.0 copy-done.5
  72.2 0.1 copy.15.bias
  72.3 1.1 collective-permute-done.3.z0
  73.4 0.1 collective-permute-done.4.z1
  73.5 2.6 %collective-permute-done.5.z2 = bf16[208,256]{1,0:T(8,128)(2,1)S(1)} collective-permute-done((bf16[208,256]{1,0:T(8,128)(2,1)S(1)}, bf16[208,256]{1,0:T(8,128)(2,1)S(1)}, u32[]{:S(2)}, u32[]{:S(2)}) %collective-permute-start.5) | collective-permute-done | bytes 106528 | tf_op jit(solution)/shard_map/ppermute | solution.py:213
  76.1 0.0 collective-permute-done.6.z3
  76.1 0.6 shard_map.96
  76.8 31.3 %all_to_all.15.got = bf16[64,24,128]{2,1,0:T(8,128)(2,1)S(1)} all-to-all(bf16[64,24,128]{2,1,0:T(8,128)(2,1)S(1)} %shard_map.96), channel_id=1, replica_groups=mesh['zl'=2,'xh'=2,'xl'=2,'yh'=4,'yl'=2,'zh'=4,'c'=2] {'zl','xh','xl','y..., dimensions={0} | all-to-all | bytes 786432 | tf_op jit(solution)/shard_map/all_to_all | solution.py:234
  108.0 0.0 copy-done.2
  108.0 1.4 %shard_map.97 = bf16[208,384]{1,0:T(8,128)(2,1)} custom-call(bf16[64,24,128]{2,1,0:T(8,128)(2,1)S(1)} %all_to_all.15.got, bf16[208,384]{1,0:T(8,128)(2,1)S(1)} %copy-done.2), custom_call_target="tpu_custom_call" | custom-call | tf_op jit(solution)/shard_map/pallas_call | solution.py:235
  (9 shorter events, 0.1 us)
Async XLA Ops:
  0.9 17.4 %collective-permute-start = (bf16[32,832]{1,0:T(8,128)(2,1)S(1)}, bf16[32,832]{1,0:T(8,128)(2,1)S(1)}, u32[]{:S(2)}, u32[]{:S(2)}) collective-permute-start(bf16[32,832]{1,0:T(8,128)(2,1)S(1)} %get-tuple-element.22), channel_id=1, source_target_pairs={{0,128},{128,0},{1,129},{129,1},{2,130},{130,2},{3,131},{131,3},{4... | collective-permute-start | bytes 159752 | tf_op jit(solution)/shard_map/ppermute | solution.py:163
  5.9 1.0 copy-start.1
  8.0 18.9 %all-to-all-start = ((f32[8,8,256]{2,1,0:T(8,128)}), f32[8,8,256]{2,1,0:T(8,128)S(1)}, u32[]{:S(2)}, u32[]{:S(2)}) async-start(f32[8,8,256]{2,1,0:T(8,128)} %get-tuple-element.14), calls=%async_computation | async-start | bytes 131072 | tf_op jit(solution)/shard_map/all_to_all | solution.py:179
  18.4 8.5 %collective-permute-start.1 = (bf16[2,32,832]{2,1,0:T(8,128)(2,1)S(1)}, bf16[2,32,832]{2,1,0:T(8,128)(2,1)S(1)}, u32[]{:S(2)}, u32[]{:S(2)}) collective-permute-start(bf16[2,32,832]{2,1,0:T(8,128)(2,1)S(1)} %pad_maximum_fusion.mine), channel_id=1, source_target_pairs={{0,8},{8,0},{1,9},{9,1},{2,10},{10,2},{3,11},{11,3},{4,12},{12,4},... | collective-permute-start | bytes 319496 | tf_op jit(solution)/shard_map/ppermute | solution.py:164
  28.5 3.9 %copy-start.3 = (bf16[104,128]{1,0:T(8,128)(2,1)S(1)}, bf16[104,128]{1,0:T(8,128)(2,1)}, u32[]{:S(2)}) copy-start(bf16[104,128]{1,0:T(8,128)(2,1)} %constant.80.clone.pack) | copy-start | bytes 79876
  28.5 26.0 %copy-start = (bf16[2,4,208,104]{3,2,1,0:T(8,128)(2,1)S(1)}, bf16[2,4,208,104]{3,2,1,0:T(8,128)(2,1)}, u32[]{:S(2)}) copy-start(bf16[2,4,208,104]{3,2,1,0:T(8,128)(2,1)} %constant.81.clone.order) | copy-start | bytes 1038340
  28.5 26.0 %all-to-all-start.1 = ((bf16[4,832,256]{2,1,0:T(8,128)(2,1)}), bf16[4,832,256]{2,1,0:T(8,128)(2,1)S(1)}, u32[]{:S(2)}, u32[]{:S(2)}) async-start(bf16[4,832,256]{2,1,0:T(8,128)(2,1)} %shard_map.92), calls=%async_computation.1 | async-start | bytes 3407872 | tf_op jit(solution)/shard_map/all_to_all | solution.py:191
  33.1 26.4 %copy-start.4 = (s32[256]{0:T(256)S(1)}, s32[256]{0:T(256)}, u32[]{:S(2)}) copy-start(s32[256]{0:T(256)} %param.14) | copy-start | bytes 3076
  54.5 17.7 %copy-start.5 = (bf16[208]{0:T(256)(128)(2,1)S(1)}, bf16[208]{0:T(256)(128)(2,1)}, u32[]{:S(2)}) copy-start(bf16[208]{0:T(256)(128)(2,1)} %param.13) | copy-start | bytes 1252
  57.5 50.6 %copy-start.2 = (bf16[208,384]{1,0:T(8,128)(2,1)S(1)}, bf16[208,384]{1,0:T(8,128)(2,1)}, u32[]{:S(2)}) copy-start(bf16[208,384]{1,0:T(8,128)(2,1)} %text.1) | copy-start | bytes 479236
  57.5 4.0 %collective-permute-start.2 = (bf16[4,208,256]{2,1,0:T(8,128)(2,1)}, bf16[4,208,256]{2,1,0:T(8,128)(2,1)S(1)}, u32[]{:S(2)}, u32[]{:S(2)}) collective-permute-start(bf16[4,208,256]{2,1,0:T(8,128)(2,1)} %get-tuple-element.16), channel_id=1, source_target_pairs={{0,1},{1,0},{2,3},{3,2},{4,5},{5,4},{6,7},{7,6},{8,9},{9,8},{10,11... | collective-permute-start | bytes 1277960 | tf_op jit(solution)/shard_map/ppermute | solution.py:208
  61.6 11.8 %collective-permute-start.3 = (bf16[208,256]{1,0:T(8,128)(2,1)S(1)}, bf16[208,256]{1,0:T(8,128)(2,1)S(1)}, u32[]{:S(2)}, u32[]{:S(2)}) collective-permute-start(bf16[208,256]{1,0:T(8,128)(2,1)S(1)} %get-tuple-element.17), channel_id=1, source_target_pairs={{0,64},{1,320},{2,66},{3,322},{4,0},{5,256},{6,2},{7,258},{64,1},{... | collective-permute-start | bytes 319496 | tf_op jit(solution)/shard_map/ppermute | solution.py:213
  64.4 9.2 %collective-permute-start.4 = (bf16[208,256]{1,0:T(8,128)(2,1)S(1)}, bf16[208,256]{1,0:T(8,128)(2,1)S(1)}, u32[]{:S(2)}, u32[]{:S(2)}) collective-permute-start(bf16[208,256]{1,0:T(8,128)(2,1)S(1)} %get-tuple-element.18), channel_id=1, source_target_pairs={{0,66},{1,322},{2,64},{3,320},{4,2},{5,258},{6,0},{7,256},{64,3},{... | collective-permute-start | bytes 319496 | tf_op jit(solution)/shard_map/ppermute | solution.py:213
  66.8 9.3 %collective-permute-start.5 = (bf16[208,256]{1,0:T(8,128)(2,1)S(1)}, bf16[208,256]{1,0:T(8,128)(2,1)S(1)}, u32[]{:S(2)}, u32[]{:S(2)}) collective-permute-start(bf16[208,256]{1,0:T(8,128)(2,1)S(1)} %get-tuple-element.19), channel_id=1, source_target_pairs={{0,2},{1,258},{2,0},{3,256},{4,66},{5,322},{6,64},{7,320},{64,67},... | collective-permute-start | bytes 319496 | tf_op jit(solution)/shard_map/ppermute | solution.py:213
  71.5 4.7 %collective-permute-start.6 = (bf16[208,256]{1,0:T(8,128)(2,1)S(1)}, bf16[208,256]{1,0:T(8,128)(2,1)S(1)}, u32[]{:S(2)}, u32[]{:S(2)}) collective-permute-start(bf16[208,256]{1,0:T(8,128)(2,1)S(1)} %get-tuple-element.20), channel_id=1, source_target_pairs={{0,0},{1,256},{2,2},{3,258},{4,64},{5,320},{6,66},{7,322},{64,65},... | collective-permute-start | bytes 319496 | tf_op jit(solution)/shard_map/ppermute | solution.py:213

commit v7 on v6

--- a/solution.py
+++ b/solution.py
@@ -94,7 +94,7 @@
     out_ref[...] = jnp.dot(pack[...], rows, preferred_element_type=F32).astype(BF16)
 
 
-def project_body(ids, x_ref, wg, order, keep_ref, send_ref, weight):
+def project_body(ids, x_ref, wg, order, send_ref, keep_ref, weight):
     c, q = ids[0], ids[1]
     for g in range(2):
         rows = [jnp.dot(order[g, y], wg[y], preferred_element_type=F32) for y in range(4)]
@@ -196,7 +196,7 @@
             order[g, r // (2 * CHUNK), r, g * 2 * CHUNK + r % (2 * CHUNK)] = 1.0
     ids = jnp.stack([c, 2 * zl + xl]).astype(jnp.int32)
     piece = sds((4, FEAT, ROWS), BF16)
-    keep, send = pl.pallas_call(
+    send, keep = pl.pallas_call(
         project_body,
         out_shape=(piece, piece),
         in_specs=[pl.BlockSpec(memory_space=pltpu.SMEM)] + _vmem(3),

time: 110 us -> 110 us (level)
  no operation moved by 1% of the time
where the time goes in v7:
time: 110 us; the launch traced here: 109 us
  blocking collectives  52.6 us (48%)
  starting transfers between devices  33.9 us (31%)
  waiting for transfers between devices  10.2 us (9%)
  Pallas kernels  8.53 us (8%)
  local copies, waits for them, and re-layouts  2.36 us (2%)
  other arithmetic  1.64 us (1%)
    all_to_all x1, blocking collectives, shards(): rows = lax.all_to_all(sent, SEQ, 0, 0, tiled=True)  31.3 us
    all_gather x1, blocking collectives, shards(): columns = lax.all_gather(quad, 'yh')  21.3 us
    ppermute x4, starting transfers between devices, shards(): lax.ppermute(parts[k], axes, _pairs(sizes, lambda z, x, h, k2, k=k: (z ^...  10.5 us
    all_to_all x1, starting transfers between devices, shards(): all_stats = lax.all_to_all(stats, TP, 0, 0, tiled=True)  10.3 us
    ppermute x1, starting transfers between devices, shards(): pair = jnp.stack([chunk, lax.ppermute(chunk, 'xh', [(0, 1), (1, 0)])])  4.93 us
    all_to_all x1, waiting for transfers between devices, shards(): all_stats = lax.all_to_all(stats, TP, 0, 0, tiled=True)  4.59 us
    ppermute x4, waiting for transfers between devices, shards(): lax.ppermute(parts[k], axes, _pairs(sizes, lambda z, x, h, k2, k=k: (z ^...  3.78 us
    all_to_all x1, starting transfers between devices, shards(): shared = lax.all_to_all(copies, SHARE, 0, 0, tiled=True)  3.72 us
  transfers between devices with their start and end apart: 9, of which 5 were waited for; matrix products, arithmetic and copies ran while one was open for 2% of the time, Pallas kernels for 2%

profile of v7, /device:TPU:8, one launch (start us, length us, event | category | flops | bytes accessed | tf_op | source)
XLA Modules:
  0.0 109.4 jit_solution(3457273803567408398)
XLA Ops:
  0.0 0.9 reshape.5
  0.9 4.9 %collective-permute-start = (bf16[32,832]{1,0:T(8,128)(2,1)S(1)}, bf16[32,832]{1,0:T(8,128)(2,1)S(1)}, u32[]{:S(2)}, u32[]{:S(2)}) collective-permute-start(bf16[32,832]{1,0:T(8,128)(2,1)S(1)} %get-tuple-element.22), channel_id=1, source_target_pairs={{0,128},{128,0},{1,129},{129,1},{2,130},{130,2},{3,131},{131,3},{4... | collective-permute-start | bytes 159752 | tf_op jit(solution)/shard_map/ppermute | solution.py:163
  5.9 0.0 copy-start.1
  5.9 1.0 copy-done.1
  6.9 1.1 %shard_map.91 = (bf16[832,256]{1,0:T(8,128)(2,1)S(1)}, f32[8,8,256]{2,1,0:T(8,128)}) custom-call(bf16[208,1024]{1,0:T(8,128)(2,1)S(1)} %copy-done.1), custom_call_target="tpu_custom_call" | custom-call | tf_op jit(solution)/shard_map/pallas_call | solution.py:173
  8.0 10.3 %all-to-all-start = ((f32[8,8,256]{2,1,0:T(8,128)}), f32[8,8,256]{2,1,0:T(8,128)S(1)}, u32[]{:S(2)}, u32[]{:S(2)}) async-start(f32[8,8,256]{2,1,0:T(8,128)} %get-tuple-element.14), calls=%async_computation | async-start | bytes 131072 | tf_op jit(solution)/shard_map/all_to_all | solution.py:179
  18.3 0.0 collective-permute-done
  18.4 2.4 %collective-permute-start.1 = (bf16[2,32,832]{2,1,0:T(8,128)(2,1)S(1)}, bf16[2,32,832]{2,1,0:T(8,128)(2,1)S(1)}, u32[]{:S(2)}, u32[]{:S(2)}) collective-permute-start(bf16[2,32,832]{2,1,0:T(8,128)(2,1)S(1)} %pad_maximum_fusion.mine), channel_id=1, source_target_pairs={{0,8},{8,0},{1,9},{9,1},{2,10},{10,2},{3,11},{11,3},{4,12},{12,4},... | collective-permute-start | bytes 319496 | tf_op jit(solution)/shard_map/ppermute | solution.py:164
  20.7 0.7 broadcast_in_dim.33
  21.4 0.1 copy.13.gain
  21.5 0.7 broadcast_in_dim.34
  22.2 0.1 copy.14.bias
  22.3 4.6 %all-to-all-done.st = f32[8,8,256]{2,1,0:T(8,128)S(1)} async-done(((f32[8,8,256]{2,1,0:T(8,128)}), f32[8,8,256]{2,1,0:T(8,128)S(1)}, u32[]{:S(2)}, u32[]{:S(2)}) %all-to-all-start) | async-done | bytes 65568 | tf_op jit(solution)/shard_map/all_to_all | solution.py:179
  26.9 0.0 collective-permute-done.1._.theirs
  26.9 1.5 %shard_map.92 = bf16[4,832,256]{2,1,0:T(8,128)(2,1)} custom-call(bf16[832,256]{1,0:T(8,128)(2,1)S(1)} %get-tuple-element.13.x_ref, f32[8,8,256]{2,1,0:T(8,128)S(1)} %all-to-all-done.st, f32[208,1]{1,0:T(8,128)S(1)} %copy.13.gain, f32[208,1]{1,0:T(8,128)S(1)} %copy.14.bias, bf16[2,32,832]{2,1,0:T(8,128)(2,1)S(1)} %collective-permute-done.1._.theirs), custom_call_target="tpu_custom_call" | custom-call | tf_op jit(solution)/shard_map/pallas_call | solution.py:180
  28.5 0.0 copy-start.3
  28.5 0.0 copy-start
  28.5 3.7 %all-to-all-start.1 = ((bf16[4,832,256]{2,1,0:T(8,128)(2,1)}), bf16[4,832,256]{2,1,0:T(8,128)(2,1)S(1)}, u32[]{:S(2)}, u32[]{:S(2)}) async-start(bf16[4,832,256]{2,1,0:T(8,128)(2,1)} %shard_map.92), calls=%async_computation.1 | async-start | bytes 3407872 | tf_op jit(solution)/shard_map/all_to_all | solution.py:191
  32.2 0.1 pad_add_fusion.ids
  32.3 0.1 pad_add_fusion.1.ids
  32.4 0.0 copy-done.3
  32.4 0.8 shard_map.93
  33.1 0.0 copy-start.4
  33.2 21.3 %all-gather = bf16[416,832]{1,0:T(8,128)(2,1)S(1)} all-gather(bf16[104,832]{1,0:T(8,128)(2,1)S(1)} %shard_map.93), channel_id=2, replica_groups=mesh['zl'=2,'xh'=2,'xl'=2,'yh'=4,'yl'=2,'zh'=4,'c'=2] {'yh'}, dimensions={0}, use_global_device_ids=true | all-gather | bytes 865280 | tf_op jit(solution)/shard_map/all_gather | solution.py:171
  54.5 0.0 all-to-all-done.1.x_ref
  54.5 0.0 copy-done
  54.5 0.0 copy-start.5
  54.5 3.0 %shard_map.94 = (bf16[4,208,256]{2,1,0:T(8,128)(2,1)}, bf16[4,208,256]{2,1,0:T(8,128)(2,1)S(1)}) custom-call(s32[2]{0:T(128)S(1)} %pad_add_fusion.ids, bf16[4,832,256]{2,1,0:T(8,128)(2,1)S(1)} %all-to-all-done.1.x_ref, bf16[4,104,832]{2,1,0:T(8,128)(2,1)S(1)} %bitcast.16, bf16[2,4,208,104]{3,2,1,0:T(8,128)(2,1)S(1)} %copy-done), custom_call_target="tpu_custom_call" | custom-call | tf_op jit(solution)/shard_map/pallas_call | solution.py:199
  57.5 0.0 copy-start.2
  57.5 2.0 %collective-permute-start.2 = (bf16[4,208,256]{2,1,0:T(8,128)(2,1)}, bf16[4,208,256]{2,1,0:T(8,128)(2,1)S(1)}, u32[]{:S(2)}, u32[]{:S(2)}) collective-permute-start(bf16[4,208,256]{2,1,0:T(8,128)(2,1)} %get-tuple-element.16), channel_id=1, source_target_pairs={{0,1},{1,0},{2,3},{3,2},{4,5},{5,4},{6,7},{7,6},{8,9},{9,8},{10,11... | collective-permute-start | bytes 1277960 | tf_op jit(solution)/shard_map/ppermute | solution.py:208
  59.5 0.0 copy-done.4
  59.6 0.1 convert_reduce_fusion
  59.7 1.8 %collective-permute-done.2.got = bf16[4,208,256]{2,1,0:T(8,128)(2,1)S(1)} collective-permute-done((bf16[4,208,256]{2,1,0:T(8,128)(2,1)}, bf16[4,208,256]{2,1,0:T(8,128)(2,1)S(1)}, u32[]{:S(2)}, u32[]{:S(2)}) %collective-permute-start.2) | collective-permute-done | bytes 426016 | tf_op jit(solution)/shard_map/ppermute | solution.py:208
  61.5 0.1 shard_map.95
  61.6 2.8 %collective-permute-start.3 = (bf16[208,256]{1,0:T(8,128)(2,1)S(1)}, bf16[208,256]{1,0:T(8,128)(2,1)S(1)}, u32[]{:S(2)}, u32[]{:S(2)}) collective-permute-start(bf16[208,256]{1,0:T(8,128)(2,1)S(1)} %get-tuple-element.17), channel_id=1, source_target_pairs={{0,64},{1,320},{2,66},{3,322},{4,0},{5,256},{6,2},{7,258},{64,1},{... | collective-permute-start | bytes 319496 | tf_op jit(solution)/shard_map/ppermute | solution.py:213
  64.4 2.4 %collective-permute-start.4 = (bf16[208,256]{1,0:T(8,128)(2,1)S(1)}, bf16[208,256]{1,0:T(8,128)(2,1)S(1)}, u32[]{:S(2)}, u32[]{:S(2)}) collective-permute-start(bf16[208,256]{1,0:T(8,128)(2,1)S(1)} %get-tuple-element.18), channel_id=1, source_target_pairs={{0,66},{1,322},{2,64},{3,320},{4,2},{5,258},{6,0},{7,256},{64,3},{... | collective-permute-start | bytes 319496 | tf_op jit(solution)/shard_map/ppermute | solution.py:213
  66.8 4.6 %collective-permute-start.5 = (bf16[208,256]{1,0:T(8,128)(2,1)S(1)}, bf16[208,256]{1,0:T(8,128)(2,1)S(1)}, u32[]{:S(2)}, u32[]{:S(2)}) collective-permute-start(bf16[208,256]{1,0:T(8,128)(2,1)S(1)} %get-tuple-element.19), channel_id=1, source_target_pairs={{0,2},{1,258},{2,0},{3,256},{4,66},{5,322},{6,64},{7,320},{64,67},... | collective-permute-start | bytes 319496 | tf_op jit(solution)/shard_map/ppermute | solution.py:213
  71.5 0.7 collective-permute-start.6
  72.1 0.0 copy-done.5
  72.2 0.1 copy.15.bias
  72.3 1.1 collective-permute-done.3.z0
  73.4 0.1 collective-permute-done.4.z1
  73.5 2.6 %collective-permute-done.5.z2 = bf16[208,256]{1,0:T(8,128)(2,1)S(1)} collective-permute-done((bf16[208,256]{1,0:T(8,128)(2,1)S(1)}, bf16[208,256]{1,0:T(8,128)(2,1)S(1)}, u32[]{:S(2)}, u32[]{:S(2)}) %collective-permute-start.5) | collective-permute-done | bytes 106528 | tf_op jit(solution)/shard_map/ppermute | solution.py:213
  76.1 0.0 collective-permute-done.6.z3
  76.1 0.6 shard_map.96
  76.8 31.3 %all_to_all.15.got = bf16[64,24,128]{2,1,0:T(8,128)(2,1)S(1)} all-to-all(bf16[64,24,128]{2,1,0:T(8,128)(2,1)S(1)} %shard_map.96), channel_id=1, replica_groups=mesh['zl'=2,'xh'=2,'xl'=2,'yh'=4,'yl'=2,'zh'=4,'c'=2] {'zl','xh','xl','y..., dimensions={0} | all-to-all | bytes 786432 | tf_op jit(solution)/shard_map/all_to_all | solution.py:234
  108.0 0.0 copy-done.2
  108.0 1.4 %shard_map.97 = bf16[208,384]{1,0:T(8,128)(2,1)} custom-call(bf16[64,24,128]{2,1,0:T(8,128)(2,1)S(1)} %all_to_all.15.got, bf16[208,384]{1,0:T(8,128)(2,1)S(1)} %copy-done.2), custom_call_target="tpu_custom_call" | custom-call | tf_op jit(solution)/shard_map/pallas_call | solution.py:235
  (9 shorter events, 0.1 us)
Async XLA Ops:
  0.9 17.4 %collective-permute-start = (bf16[32,832]{1,0:T(8,128)(2,1)S(1)}, bf16[32,832]{1,0:T(8,128)(2,1)S(1)}, u32[]{:S(2)}, u32[]{:S(2)}) collective-permute-start(bf16[32,832]{1,0:T(8,128)(2,1)S(1)} %get-tuple-element.22), channel_id=1, source_target_pairs={{0,128},{128,0},{1,129},{129,1},{2,130},{130,2},{3,131},{131,3},{4... | collective-permute-start | bytes 159752 | tf_op jit(solution)/shard_map/ppermute | solution.py:163
  5.9 1.0 copy-start.1
  8.0 18.9 %all-to-all-start = ((f32[8,8,256]{2,1,0:T(8,128)}), f32[8,8,256]{2,1,0:T(8,128)S(1)}, u32[]{:S(2)}, u32[]{:S(2)}) async-start(f32[8,8,256]{2,1,0:T(8,128)} %get-tuple-element.14), calls=%async_computation | async-start | bytes 131072 | tf_op jit(solution)/shard_map/all_to_all | solution.py:179
  18.4 8.5 %collective-permute-start.1 = (bf16[2,32,832]{2,1,0:T(8,128)(2,1)S(1)}, bf16[2,32,832]{2,1,0:T(8,128)(2,1)S(1)}, u32[]{:S(2)}, u32[]{:S(2)}) collective-permute-start(bf16[2,32,832]{2,1,0:T(8,128)(2,1)S(1)} %pad_maximum_fusion.mine), channel_id=1, source_target_pairs={{0,8},{8,0},{1,9},{9,1},{2,10},{10,2},{3,11},{11,3},{4,12},{12,4},... | collective-permute-start | bytes 319496 | tf_op jit(solution)/shard_map/ppermute | solution.py:164
  28.5 3.9 %copy-start.3 = (bf16[104,128]{1,0:T(8,128)(2,1)S(1)}, bf16[104,128]{1,0:T(8,128)(2,1)}, u32[]{:S(2)}) copy-start(bf16[104,128]{1,0:T(8,128)(2,1)} %constant.80.clone.pack) | copy-start | bytes 79876
  28.5 26.0 %copy-start = (bf16[2,4,208,104]{3,2,1,0:T(8,128)(2,1)S(1)}, bf16[2,4,208,104]{3,2,1,0:T(8,128)(2,1)}, u32[]{:S(2)}) copy-start(bf16[2,4,208,104]{3,2,1,0:T(8,128)(2,1)} %constant.81.clone.order) | copy-start | bytes 1038340
  28.5 26.0 %all-to-all-start.1 = ((bf16[4,832,256]{2,1,0:T(8,128)(2,1)}), bf16[4,832,256]{2,1,0:T(8,128)(2,1)S(1)}, u32[]{:S(2)}, u32[]{:S(2)}) async-start(bf16[4,832,256]{2,1,0:T(8,128)(2,1)} %shard_map.92), calls=%async_computation.1 | async-start | bytes 3407872 | tf_op jit(solution)/shard_map/all_to_all | solution.py:191
  33.1 26.4 %copy-start.4 = (s32[256]{0:T(256)S(1)}, s32[256]{0:T(256)}, u32[]{:S(2)}) copy-start(s32[256]{0:T(256)} %param.14) | copy-start | bytes 3076
  54.5 17.7 %copy-start.5 = (bf16[208]{0:T(256)(128)(2,1)S(1)}, bf16[208]{0:T(256)(128)(2,1)}, u32[]{:S(2)}) copy-start(bf16[208]{0:T(256)(128)(2,1)} %param.13) | copy-start | bytes 1252
  57.5 50.6 %copy-start.2 = (bf16[208,384]{1,0:T(8,128)(2,1)S(1)}, bf16[208,384]{1,0:T(8,128)(2,1)}, u32[]{:S(2)}) copy-start(bf16[208,384]{1,0:T(8,128)(2,1)} %text.1) | copy-start | bytes 479236
  57.5 4.0 %collective-permute-start.2 = (bf16[4,208,256]{2,1,0:T(8,128)(2,1)}, bf16[4,208,256]{2,1,0:T(8,128)(2,1)S(1)}, u32[]{:S(2)}, u32[]{:S(2)}) collective-permute-start(bf16[4,208,256]{2,1,0:T(8,128)(2,1)} %get-tuple-element.16), channel_id=1, source_target_pairs={{0,1},{1,0},{2,3},{3,2},{4,5},{5,4},{6,7},{7,6},{8,9},{9,8},{10,11... | collective-permute-start | bytes 1277960 | tf_op jit(solution)/shard_map/ppermute | solution.py:208
  61.6 11.8 %collective-permute-start.3 = (bf16[208,256]{1,0:T(8,128)(2,1)S(1)}, bf16[208,256]{1,0:T(8,128)(2,1)S(1)}, u32[]{:S(2)}, u32[]{:S(2)}) collective-permute-start(bf16[208,256]{1,0:T(8,128)(2,1)S(1)} %get-tuple-element.17), channel_id=1, source_target_pairs={{0,64},{1,320},{2,66},{3,322},{4,0},{5,256},{6,2},{7,258},{64,1},{... | collective-permute-start | bytes 319496 | tf_op jit(solution)/shard_map/ppermute | solution.py:213
  64.4 9.2 %collective-permute-start.4 = (bf16[208,256]{1,0:T(8,128)(2,1)S(1)}, bf16[208,256]{1,0:T(8,128)(2,1)S(1)}, u32[]{:S(2)}, u32[]{:S(2)}) collective-permute-start(bf16[208,256]{1,0:T(8,128)(2,1)S(1)} %get-tuple-element.18), channel_id=1, source_target_pairs={{0,66},{1,322},{2,64},{3,320},{4,2},{5,258},{6,0},{7,256},{64,3},{... | collective-permute-start | bytes 319496 | tf_op jit(solution)/shard_map/ppermute | solution.py:213
  66.8 9.3 %collective-permute-start.5 = (bf16[208,256]{1,0:T(8,128)(2,1)S(1)}, bf16[208,256]{1,0:T(8,128)(2,1)S(1)}, u32[]{:S(2)}, u32[]{:S(2)}) collective-permute-start(bf16[208,256]{1,0:T(8,128)(2,1)S(1)} %get-tuple-element.19), channel_id=1, source_target_pairs={{0,2},{1,258},{2,0},{3,256},{4,66},{5,322},{6,64},{7,320},{64,67},... | collective-permute-start | bytes 319496 | tf_op jit(solution)/shard_map/ppermute | solution.py:213
  71.5 4.7 %collective-permute-start.6 = (bf16[208,256]{1,0:T(8,128)(2,1)S(1)}, bf16[208,256]{1,0:T(8,128)(2,1)S(1)}, u32[]{:S(2)}, u32[]{:S(2)}) collective-permute-start(bf16[208,256]{1,0:T(8,128)(2,1)S(1)} %get-tuple-element.20), channel_id=1, source_target_pairs={{0,0},{1,256},{2,2},{3,258},{4,64},{5,320},{6,66},{7,322},{64,65},... | collective-permute-start | bytes 319496 | tf_op jit(solution)/shard_map/ppermute | solution.py:213
